TPU v7x, 32 devices: a whole 2x2x4 slice. The times are simulated.
32 devices in a mesh: fsdp: 4 (over y, x), seq: 8 (over z, core).
Axes of the slice: x: 2, y: 2, z: 4, core: 2. Of those that a mesh axis runs over, the one named last changes fastest.
Arguments:
- residual_in: bfloat16 [4, 1024, 2048], P('fsdp', 'seq'), may hold values from -6 to 6
- attn_gain: bfloat16 [2048], replicated, may hold values from 0.5 to 1.5
- mlp_gain: bfloat16 [2048], replicated, may hold values from 0.5 to 1.5
- w_qkv: bfloat16 [2048, 3, 2048], P('fsdp'), may hold values from -0.125 to 0.125
- w_out: bfloat16 [2048, 2048], P('fsdp'), may hold values from -1 to 1
- w_gate_up: bfloat16 [8192, 2, 2048], P('fsdp'), may hold values from -0.125 to 0.125
- w_down: bfloat16 [2048, 8192], P('fsdp'), may hold values from -0.0625 to 0.0625
- cotangent: bfloat16 [4, 1024, 2048], P('fsdp', 'seq'), may hold values from -6 to 6
Outputs:
- layer_out: bfloat16 [4, 1024, 2048], P('fsdp', 'seq')
- grad_input: float32 [4, 1024, 2048], P('fsdp', 'seq')
- grad_attn_gain: float32 [2048], P(('fsdp', 'seq'))
- grad_mlp_gain: float32 [2048], P(('fsdp', 'seq'))
- grad_qkv: float32 [2048, 3, 2048], P(('seq', 'fsdp'))
- grad_out_proj: float32 [2048, 2048], P(None, ('seq', 'fsdp'))
- grad_gate_up: float32 [8192, 2, 2048], P(('seq', 'fsdp'))
- grad_down: float32 [2048, 8192], P(None, ('seq', 'fsdp'))
All inputs are finite; a program needn't handle non-finite values.
Results may differ from a plain program's by a relative error of at most 0.018.
Values may be sent and summed in bfloat16 or wider, within the bound.
No kernel may reach another device: no remote copies, remote signals or barrier semaphores. Data moves between devices by JAX's collectives and lax.ppermute only.
A program may use at most 384 MiB of HBM per device.

v0:
```python
import math

import jax
import jax.numpy as jnp
from jax import lax
from jax.sharding import PartitionSpec as P

HD = 64


NORM_EPS = 1e-05
ROPE_BASE = 130000.0


def rotate(matrix):
    shaped = matrix.reshape(matrix.shape[:-1] + (matrix.shape[-1] // HD, 2, HD // 2))
    turned = jnp.stack([-shaped[..., 1, :], shaped[..., 0, :]], axis=-2)
    return turned.reshape(matrix.shape)


def rotate_back(matrix):
    shaped = matrix.reshape(matrix.shape[:-1] + (matrix.shape[-1] // HD, 2, HD // 2))
    turned = jnp.stack([shaped[..., 1, :], -shaped[..., 0, :]], axis=-2)
    return turned.reshape(matrix.shape)


def rope_tables(positions, columns):
    freq_index = (jnp.arange(columns, dtype=jnp.int32) % (HD // 2)).astype(jnp.float32)
    inverse = ROPE_BASE ** (-2.0 * freq_index / HD)
    angles = positions.astype(jnp.float32)[:, None] * inverse[None, :]
    return (jnp.cos(angles), jnp.sin(angles))


def rms_scale(matrix):
    return lax.rsqrt(jnp.mean(matrix * matrix, axis=-1, keepdims=True) + NORM_EPS)


def rms_back(grad_normed, matrix, scale_rows, gain):
    weighted = grad_normed * gain
    inner_mean = jnp.mean(weighted * matrix, axis=-1, keepdims=True)
    grad_matrix = scale_rows * weighted - matrix * scale_rows**3 * inner_mean
    grad_gain = jnp.sum(grad_normed * matrix * scale_rows, axis=0)
    return (grad_matrix, grad_gain)


def attend_forward(queries, key_rows, values):
    seq_count, length, width_here = queries.shape
    heads_here = width_here // HD
    q_block = min(512, length)
    k_block = min(256, length)
    inv_root = 1.0 / math.sqrt(HD)
    shaped_q = queries.reshape(seq_count, length, heads_here, HD)
    shaped_k = key_rows.reshape(seq_count, length, heads_here, HD)
    shaped_v = values.reshape(seq_count, length, heads_here, HD)

    def query_step(q_index, carried):
        attended, totals = carried
        offset = q_index * q_block
        q_rows = lax.dynamic_slice_in_dim(shaped_q, offset, q_block, 1)
        query_pos = offset + jnp.arange(q_block, dtype=jnp.int32)

        def key_step(k_index, running):
            unnorm, denominator = running
            k_start = k_index * k_block
            k_rows = lax.dynamic_slice_in_dim(shaped_k, k_start, k_block, 1)
            v_rows = lax.dynamic_slice_in_dim(shaped_v, k_start, k_block, 1)
            scores = (
                jnp.einsum("bqhd,bkhd->bhqk", q_rows, k_rows, preferred_element_type=jnp.float32)
                * inv_root
            )
            causal = (k_start + jnp.arange(k_block, dtype=jnp.int32))[None, :] <= query_pos[:, None]
            exp_scores = jnp.where(causal, jnp.exp(scores), 0.0)
            denominator = denominator + jnp.sum(exp_scores, axis=-1)
            unnorm = unnorm + jnp.einsum(
                "bhqk,bkhd->bqhd",
                exp_scores.astype(jnp.bfloat16),
                v_rows,
                preferred_element_type=jnp.float32,
            )
            return (unnorm, denominator)

        start_state = (
            jnp.zeros((seq_count, q_block, heads_here, HD), jnp.float32),
            jnp.zeros((seq_count, heads_here, q_block), jnp.float32),
        )
        unnorm, denominator = lax.fori_loop(0, (offset + q_block) // k_block, key_step, start_state)
        block_out = unnorm / jnp.transpose(denominator, (0, 2, 1))[..., None]
        attended = lax.dynamic_update_slice_in_dim(attended, block_out, offset, 1)
        totals = lax.dynamic_update_slice_in_dim(totals, denominator, offset, 2)
        return (attended, totals)

    initial = (
        jnp.zeros((seq_count, length, heads_here, HD), jnp.float32),
        jnp.zeros((seq_count, heads_here, length), jnp.float32),
    )
    attended, totals = lax.fori_loop(0, length // q_block, query_step, initial)
    return (attended.reshape(seq_count, length, width_here), totals)


def attend_backward(queries, key_rows, values, attended, totals, grad_attended):
    seq_count, length, width_here = queries.shape
    heads_here = width_here // HD
    q_block = min(512, length)
    k_block = min(256, length)
    inv_root = 1.0 / math.sqrt(HD)
    shaped_q = queries.reshape(seq_count, length, heads_here, HD)
    shaped_k = key_rows.reshape(seq_count, length, heads_here, HD)
    shaped_v = values.reshape(seq_count, length, heads_here, HD)
    shaped_grad = grad_attended.reshape(seq_count, length, heads_here, HD).astype(jnp.float32)
    shaped_att = attended.reshape(seq_count, length, heads_here, HD)
    totals_rows = jnp.transpose(totals, (0, 2, 1))
    grad_total = -jnp.sum(shaped_grad * shaped_att, axis=-1) / totals_rows
    grad_unnorm = (shaped_grad / totals_rows[..., None]).astype(jnp.bfloat16)

    def query_step(q_index, carried):
        grad_q, grad_k, grad_v = carried
        offset = q_index * q_block
        q_rows = lax.dynamic_slice_in_dim(shaped_q, offset, q_block, 1)
        g_rows = lax.dynamic_slice_in_dim(grad_unnorm, offset, q_block, 1)
        total_rows = jnp.transpose(
            lax.dynamic_slice_in_dim(grad_total, offset, q_block, 1), (0, 2, 1)
        )
        query_pos = offset + jnp.arange(q_block, dtype=jnp.int32)

        def key_step(k_index, running):
            dq_acc, dk_all, dv_all = running
            k_start = k_index * k_block
            k_rows = lax.dynamic_slice_in_dim(shaped_k, k_start, k_block, 1)
            v_rows = lax.dynamic_slice_in_dim(shaped_v, k_start, k_block, 1)
            scores = (
                jnp.einsum("bqhd,bkhd->bhqk", q_rows, k_rows, preferred_element_type=jnp.float32)
                * inv_root
            )
            causal = (k_start + jnp.arange(k_block, dtype=jnp.int32))[None, :] <= query_pos[:, None]
            exp_scores = jnp.where(causal, jnp.exp(scores), 0.0)
            grad_prob = jnp.einsum(
                "bqhd,bkhd->bhqk", g_rows, v_rows, preferred_element_type=jnp.float32
            )
            grad_scores = (exp_scores * (grad_prob + total_rows[..., None])).astype(jnp.bfloat16)
            dq_acc = (
                dq_acc
                + jnp.einsum(
                    "bhqk,bkhd->bqhd", grad_scores, k_rows, preferred_element_type=jnp.float32
                )
                * inv_root
            )
            dk_part = (
                jnp.einsum(
                    "bhqk,bqhd->bkhd", grad_scores, q_rows, preferred_element_type=jnp.float32
                )
                * inv_root
            )
            dv_part = jnp.einsum(
                "bhqk,bqhd->bkhd",
                exp_scores.astype(jnp.bfloat16),
                g_rows,
                preferred_element_type=jnp.float32,
            )
            dk_slice = lax.dynamic_slice_in_dim(dk_all, k_start, k_block, 1) + dk_part
            dv_slice = lax.dynamic_slice_in_dim(dv_all, k_start, k_block, 1) + dv_part
            dk_all = lax.dynamic_update_slice_in_dim(dk_all, dk_slice, k_start, 1)
            dv_all = lax.dynamic_update_slice_in_dim(dv_all, dv_slice, k_start, 1)
            return (dq_acc, dk_all, dv_all)

        start_state = (jnp.zeros((seq_count, q_block, heads_here, HD), jnp.float32), grad_k, grad_v)
        dq_block, grad_k, grad_v = lax.fori_loop(
            0, (offset + q_block) // k_block, key_step, start_state
        )
        grad_q = lax.dynamic_update_slice_in_dim(grad_q, dq_block, offset, 1)
        return (grad_q, grad_k, grad_v)

    empty = jnp.zeros((seq_count, length, heads_here, HD), jnp.float32)
    grad_q, grad_k, grad_v = lax.fori_loop(0, length // q_block, query_step, (empty, empty, empty))
    cosine, sine_table = rope_tables(jnp.arange(length, dtype=jnp.int32), width_here)
    grad_q = grad_q.reshape(seq_count, length, width_here)
    grad_k = grad_k.reshape(seq_count, length, width_here)
    grad_v = grad_v.reshape(seq_count, length, width_here)
    raw_q = grad_q * cosine + rotate_back(grad_q * sine_table)
    raw_k = grad_k * cosine + rotate_back(grad_k * sine_table)
    return jnp.stack([raw_q, raw_k, grad_v]).astype(jnp.bfloat16)


def body(residual_in, attn_gain, mlp_gain, w_qkv, w_out, w_gate_up, w_down, cotangent):
    seq_count, shard_len, model_width = residual_in.shape
    tokens = seq_count * shard_len
    seq_index = lax.axis_index("seq")
    positions = seq_index * shard_len + jnp.arange(tokens, dtype=jnp.int32) % shard_len
    cosine, sine_table = rope_tables(positions, model_width)
    inputs = residual_in.reshape(tokens, model_width).astype(jnp.float32)
    gain_one = attn_gain.astype(jnp.float32)
    gain_two = mlp_gain.astype(jnp.float32)
    scale_one = rms_scale(inputs)
    normed_one = (inputs * scale_one * gain_one).astype(jnp.bfloat16)
    qkv_full, out_full = (
        lax.all_gather(w_qkv, "fsdp", axis=0, tiled=True),
        lax.all_gather(w_out, "fsdp", axis=0, tiled=True),
    )
    projected = jnp.einsum("td,fpd->ptf", normed_one, qkv_full, preferred_element_type=jnp.float32)
    queries = (projected[0] * cosine + rotate(projected[0]) * sine_table).astype(jnp.bfloat16)
    key_rows = (projected[1] * cosine + rotate(projected[1]) * sine_table).astype(jnp.bfloat16)
    values = projected[2].astype(jnp.bfloat16)
    stacked = jnp.stack([queries, key_rows, values]).reshape(3, seq_count, shard_len, model_width)
    head_view = lax.all_to_all(stacked, "seq", split_axis=3, concat_axis=2, tiled=True)
    attended, totals = attend_forward(head_view[0], head_view[1], head_view[2])
    attended_heads = attended.astype(jnp.bfloat16)
    sent_back = lax.all_to_all(attended_heads, "seq", split_axis=1, concat_axis=2, tiled=True)
    attended_low = sent_back.reshape(tokens, model_width)
    branch = jnp.einsum("ti,fi->tf", attended_low, out_full, preferred_element_type=jnp.float32)
    residual = inputs + branch
    scale_two = rms_scale(residual)
    normed_two = (residual * scale_two * gain_two).astype(jnp.bfloat16)
    up_full, down_full = (
        lax.all_gather(w_gate_up, "fsdp", axis=0, tiled=True),
        lax.all_gather(w_down, "fsdp", axis=0, tiled=True),
    )
    gate_up = jnp.einsum("td,jpd->ptj", normed_two, up_full, preferred_element_type=jnp.float32)
    hidden = (jax.nn.silu(gate_up[0]) * gate_up[1]).astype(jnp.bfloat16)
    mlp_term = jnp.einsum("tj,fj->tf", hidden, down_full, preferred_element_type=jnp.float32)
    layer_out = (
        (residual + mlp_term).astype(jnp.bfloat16).reshape(seq_count, shard_len, model_width)
    )
    grad_out = cotangent.reshape(tokens, model_width)
    up_again, down_again = (
        lax.all_gather(w_gate_up, "fsdp", axis=0, tiled=True),
        lax.all_gather(w_down, "fsdp", axis=0, tiled=True),
    )
    grad_hidden = jnp.einsum("tf,fj->tj", grad_out, down_again, preferred_element_type=jnp.float32)
    sigmoid_gate = jax.nn.sigmoid(gate_up[0])
    grad_gate = grad_hidden * gate_up[1] * sigmoid_gate * (1.0 + gate_up[0] * (1.0 - sigmoid_gate))
    grad_up = grad_hidden * jax.nn.silu(gate_up[0])
    grad_gu = jnp.stack([grad_gate, grad_up]).astype(jnp.bfloat16)
    grad_normed_two = jnp.einsum(
        "ptj,jpd->td", grad_gu, up_again, preferred_element_type=jnp.float32
    )
    ff_width = grad_gu.shape[2]
    unit_rows = jnp.concatenate([grad_gu, hidden[None]], axis=0).reshape(
        3, seq_count, shard_len, ff_width
    )
    unit_cols = lax.all_to_all(unit_rows, "seq", split_axis=3, concat_axis=2, tiled=True)
    normed_piece = lax.all_gather(
        normed_two.reshape(seq_count, shard_len, model_width), "seq", axis=1, tiled=True
    )
    grad_piece = lax.all_gather(cotangent, "seq", axis=1, tiled=True)
    gu_part = jnp.einsum(
        "psnj,snd->jpd", unit_cols[:2], normed_piece, preferred_element_type=jnp.float32
    )
    down_part = jnp.einsum(
        "snf,snj->fj", grad_piece, unit_cols[2], preferred_element_type=jnp.float32
    )
    gu_part, down_part = (gu_part, down_part)
    grad_gate_up, grad_down = (
        lax.psum_scatter(
            gu_part.astype(jnp.bfloat16), "fsdp", scatter_dimension=0, tiled=True
        ).astype(jnp.float32),
        lax.psum_scatter(
            down_part.astype(jnp.bfloat16), "fsdp", scatter_dimension=1, tiled=True
        ).astype(jnp.float32),
    )
    grad_norm_two, grad_gain_two = rms_back(grad_normed_two, residual, scale_two, gain_two)
    grad_residual = grad_out.astype(jnp.float32) + grad_norm_two
    qkv_back, out_back = (
        lax.all_gather(w_qkv, "fsdp", axis=0, tiled=True),
        lax.all_gather(w_out, "fsdp", axis=0, tiled=True),
    )
    grad_branch = grad_residual.astype(jnp.bfloat16)
    grad_attended = jnp.einsum(
        "tf,fi->ti", grad_branch, out_back, preferred_element_type=jnp.float32
    )
    grad_attended = grad_attended.astype(jnp.bfloat16).reshape(seq_count, shard_len, model_width)
    grad_heads = lax.all_to_all(grad_attended, "seq", split_axis=2, concat_axis=1, tiled=True)
    grad_stacked = attend_backward(
        head_view[0], head_view[1], head_view[2], attended, totals, grad_heads
    )
    normed_piece = lax.all_gather(
        normed_one.reshape(seq_count, shard_len, model_width), "seq", axis=1, tiled=True
    )
    branch_piece = lax.all_gather(
        grad_branch.reshape(seq_count, shard_len, model_width), "seq", axis=1, tiled=True
    )
    grad_piece = grad_stacked
    qkv_part = jnp.einsum(
        "psnf,snd->fpd", grad_piece, normed_piece, preferred_element_type=jnp.float32
    )
    out_part = jnp.einsum(
        "snf,sni->fi", branch_piece, attended_heads, preferred_element_type=jnp.float32
    )
    qkv_part, out_part = (qkv_part, out_part)
    grad_qkv, grad_out_proj = (
        lax.psum_scatter(
            qkv_part.astype(jnp.bfloat16), "fsdp", scatter_dimension=0, tiled=True
        ).astype(jnp.float32),
        lax.psum_scatter(
            out_part.astype(jnp.bfloat16), "fsdp", scatter_dimension=1, tiled=True
        ).astype(jnp.float32),
    )
    grad_projected = lax.all_to_all(grad_stacked, "seq", split_axis=2, concat_axis=3, tiled=True)
    grad_projected = grad_projected.reshape(3, tokens, model_width)
    grad_normed_one = jnp.einsum(
        "ptf,fpd->td", grad_projected, qkv_back, preferred_element_type=jnp.float32
    )
    grad_norm_one, grad_gain_one = rms_back(grad_normed_one, inputs, scale_one, gain_one)
    grad_input = (grad_residual + grad_norm_one).reshape(seq_count, shard_len, model_width)
    grad_attn_gain, grad_mlp_gain = (
        lax.psum_scatter(grad_gain_one, ("fsdp", "seq"), scatter_dimension=0, tiled=True),
        lax.psum_scatter(grad_gain_two, ("fsdp", "seq"), scatter_dimension=0, tiled=True),
    )
    return (
        layer_out,
        grad_input,
        grad_attn_gain,
        grad_mlp_gain,
        grad_qkv,
        grad_out_proj,
        grad_gate_up,
        grad_down,
    )


def solution(mesh):
    return jax.shard_map(
        body,
        mesh=mesh,
        in_specs=(
            P("fsdp", "seq", None),
            P(),
            P(),
            P("fsdp", None, None),
            P("fsdp", None),
            P("fsdp", None, None),
            P("fsdp", None),
            P("fsdp", "seq", None),
        ),
        out_specs=(
            P("fsdp", "seq", None),
            P("fsdp", "seq", None),
            P(("fsdp", "seq")),
            P(("fsdp", "seq")),
            P(("seq", "fsdp"), None, None),
            P(None, ("seq", "fsdp")),
            P(("seq", "fsdp"), None, None),
            P(None, ("seq", "fsdp")),
        ),
        check_vma=False,
    )
```

profile of v0, /device:TPU:6, one launch (start us, length us, event | category | flops | bytes accessed | tf_op | source)
XLA Modules:
  0.0 1825.3 jit_solution(5378411040820716253)
XLA Ops:
  8.7 18.1 copy.202
  28.9 208.9 %all-gather.11.cloned.1.call-done = bf16[2048,3,2048]{2,0,1:T(8,128)(2,1)} async-done(((bf16[512,3,2048]{2,0,1:T(8,128)(2,1)}), bf16[2048,3,2048]{2,0,1:T(8,128)(2,1)}) %all-gather.11.cloned.1.call-update) | async-done | bytes 25165840 | tf_op jit(solution)/shard_map/all_gather | solution.py:195
  237.7 13.5 convolution_bitcast_fusion.3
  268.4 5.3 fusion.111
  276.4 4.8 all-to-all-start
  281.2 49.0 %all-to-all-done = bf16[3,1,128,2048]{2,0,1,3:T(4,128)(2,1)S(1)} async-done(((bf16[3,1,128,2048]{2,0,1,3:T(4,128)(2,1)}), bf16[3,1,128,2048]{2,0,1,3:T(4,128)(2,1)S(1)}, u32[]{:S(2)}, u32[]{:S(2)}) %all-to-all-start) | async-done | bytes 1572896 | tf_op jit(solution)/shard_map/all_to_all | solution.py:203
  337.3 16.9 while.118
  338.2 5.0 while.121
  344.2 10.0 while.121
  355.2 3.6 copy.200
  359.4 5.9 reduce.3
  367.3 4.2 all-to-all-start.1
  372.9 13.9 all-to-all-done.1
  392.0 6.5 multiply_reduce_fusion.3
  398.7 506.9 %all-gather.15.cloned.1.call-done = bf16[8192,2,2048]{2,0,1:T(8,128)(2,1)} async-done(((bf16[2048,2,2048]{2,0,1:T(8,128)(2,1)}), bf16[8192,2,2048]{2,0,1:T(8,128)(2,1)}) %all-gather.15.cloned.1.call-update) | async-done | bytes 67108880 | tf_op jit(solution)/shard_map/all_gather | solution.py:213
  905.6 37.2 %convolution_bitcast_fusion.2 = f32[2,128,8192]{2,1,0:T(8,128)} fusion(bf16[8192,2,2048]{2,0,1:T(8,128)(2,1)} %all-gather.15.cloned.1.call-done, bf16[128,2048]{1,0:T(8,128)(2,1)S(1)} %multiply_convert_fusion.2), kind=kOutput, calls=%fused_computation.67 | convolution fusion | flops 8589934592 | bytes 76021760 | tf_op jit(solution)/shard_map/td,jpd->ptj/dot_general | solution.py:216
  942.8 261.6 %all-gather.17.cloned.1.call-done = bf16[2048,8192]{1,0:T(8,128)(2,1)} async-done(((bf16[512,8192]{1,0:T(8,128)(2,1)}), bf16[2048,8192]{1,0:T(8,128)(2,1)}) %all-gather.17.cloned.1.call-update) | async-done | bytes 33554448 | tf_op jit(solution)/shard_map/all_gather | solution.py:214
  1204.4 18.9 %fusion.83 = (bf16[1,128,8192]{2,1,0:T(8,128)(2,1)}, bf16[1,128,8192]{2,1,0:T(8,128)(2,1)}) fusion(f32[2,128,8192]{2,1,0:T(8,128)} %convolution_bitcast_fusion.2, bf16[2048,8192]{1,0:T(8,128)(2,1)} %all-gather.17.cloned.1.call-done, bf16[1,128,2048]{2,1,0:T(8,128)(2,1)} %param.23), kind=kOutput, calls=%fused_computation.108 | convolution fusion | flops 4308598784 | bytes 46661632 | tf_op jit(solution)/shard_map/tf,fj->tj/dot_general | solution.py:227
  1223.3 25.3 %multiply_reduce_fusion = (f32[2048]{0:T(1024)}, f32[128]{0:T(128)S(1)}, f32[128,2048]{1,0:T(8,128)S(1)}) fusion(f32[128,2048]{1,0:T(8,128)S(1)} %get-tuple-element.716, f32[128]{0:T(128)S(1)} %get-tuple-element.714, f32[2048]{0:T(1024)S(1)} %convert_element_type.212, bf16[8192,2,2048]{2,0,1:T(8,128)(2,1)} %all-gather.15.cloned.1.call-done, ...), kind=kOutput, calls=%fused_computation.151 | convolution fusion | flops 8593602560 | bytes 73417728 | tf_op jit(solution)/shard_map/ptj,jpd->td/dot_general | solution.py:232
  1251.7 6.0 multiply_convert_fusion
  1257.7 4.6 fusion.79
  1263.1 11.5 reduce.4
  1275.5 4.6 all-to-all-start.2
  1280.1 6.4 maximum_bitcast_fusion
  1286.5 13.2 copy.216
  1299.7 9.5 all-to-all-done.2
  1309.2 4.9 all-to-all-start.4
  1326.9 37.3 %while.120 = (s32[]{:T(128)}, f32[1,1024,4,64]{1,3,2,0:T(8,128)}, f32[1,1024,4,64]{1,3,2,0:T(8,128)S(1)}, f32[1,1024,4,64]{1,3,2,0:T(8,128)}, bf16[1,1024,4,64]{...) while((s32[]{:T(128)}, f32[1,1024,4,64]{1,3,2,0:T(8,128)}, ...), condition=%wide.region_12.13_spmd, body=%wide.region_9.12_spmd.sunk | while | flops 340329248 | bytes 17070880 | solution.py:173
  1328.7 10.7 while.122
  1342.0 21.4 %while.122 = (s32[]{:T(128)}, f32[1,512,4,64]{1,3,2,0:T(8,128)S(1)}, f32[1,1024,4,64]{1,3,2,0:T(8,128)S(1)}, f32[1,1024,4,64]{1,3,2,0:T(8,128)}, s32[]{:T(128)},...) while((s32[]{:T(128)}, f32[1,512,4,64]{1,3,2,0:T(8,128)S(1)}, ...), condition=%wide.region_11.11_spmd.clone, body=%wide.region_10.10_spmd.clone.sunk | while | flops 340329216 | bytes 14432507 | solution.py:166
  1365.5 4.7 fusion.115
  1382.5 5.2 add_convert_fusion.1
  1387.7 7.5 fusion.72
  1395.2 8.0 copy.215
  1403.3 4.4 convolution_convert_fusion
  1407.8 157.6 %all-to-all-done.4 = bf16[3,1,128,8192]{2,0,1,3:T(4,128)(2,1)} async-done(((bf16[3,1,128,8192]{2,0,1,3:T(4,128)(2,1)}), bf16[3,1,128,8192]{2,0,1,3:T(4,128)(2,1)}, u32[]{:S(2)}, u32[]{:S(2)}) %all-to-all-start.4) | async-done | bytes 6291488 | tf_op jit(solution)/shard_map/all_to_all | solution.py:239
  1565.4 4.3 copy.217
  1575.1 9.5 convert_bitcast_fusion.1
  1584.7 4.6 slice.103
  1589.3 6.4 copy.218
  1595.7 14.1 convert_bitcast_fusion
  1613.7 3.8 all-to-all-start.3
  1618.8 19.0 %fusion.80 = bf16[1,128,2048]{2,1,0:T(8,128)(2,1)} fusion(f32[128,2048]{1,0:T(8,128)S(1)} %copy-done.5, bf16[2048,8192]{1,0:T(8,128)(2,1)} %all-gather.17.cloned.1.call-done, f32[2,128,8192]{2,1,0:T(8,128)} %convolution_bitcast_fusion.2), kind=kOutput, calls=%fused_computation.106 | convolution fusion | flops 4301783040 | bytes 43515904 | tf_op jit(solution)/shard_map/tj,fj->tf/dot_general | solution.py:218
  1637.8 28.7 %all-to-all-done.3 = bf16[3,1,1024,256]{3,0,1,2:T(4,128)(2,1)S(1)} async-done(((bf16[3,1,1024,256]{3,0,1,2:T(4,128)(2,1)}), bf16[3,1,1024,256]{3,0,1,2:T(4,128)(2,1)S(1)}, u32[]{:S(2)}, u32[]{:S(2)}) %all-to-all-start.3) | async-done | bytes 1572896 | tf_op jit(solution)/shard_map/all_to_all | solution.py:296
  1671.4 13.6 fusion.107
  1685.0 39.4 %all-reduce.3 = (f32[2048]{0:T(1024)S(1)}, f32[2048]{0:T(1024)S(1)}) all-reduce(f32[2048]{0:T(1024)S(1)} %get-tuple-element.610, f32[2048]{0:T(1024)S(1)} %copy-done.22), channel_id=4, replica_groups=mesh['fsdp'=4,'seq'=8] {'fsdp','seq'}, use_global_device_ids=true, to_apply=%region_15.16.clone | all-reduce | flops 4096 | bytes 32768
  1736.0 75.9 %reduce-scatter.6.cloned.1.call-done = bf16[256,2,2048]{0,2,1:T(8,128)(2,1)} async-done(((bf16[1024,2,2048]{0,2,1:T(8,128)(2,1)}), bf16[256,2,2048]{0,2,1:T(8,128)(2,1)}) %reduce-scatter.6.cloned.1.call-update) | async-done | bytes 2097168 | tf_op jit(solution)/shard_map/reduce_scatter | solution.py:252
  1811.9 6.4 copy.222
  (280 shorter events, 151.4 us)
Async XLA Ops:
  7.2 230.5 %all-gather.11.cloned.1.call-start = ((), (), s32[]{:S(2)}) async-start(), calls=%async_computation.8 | async-start | bytes 31457280 | tf_op jit(solution)/shard_map/all_gather | solution.py:195
  7.9 384.1 %all-gather.13.cloned.1.call-start = ((), (), s32[]{:S(2)}) async-start(), calls=%async_computation.9 | async-start | bytes 10485760 | tf_op jit(solution)/shard_map/all_gather | solution.py:196
  8.7 897.0 %all-gather.15.cloned.1.call-start = ((), (), s32[]{:S(2)}) async-start(), calls=%async_computation.10 | async-start | bytes 83886080 | tf_op jit(solution)/shard_map/all_gather | solution.py:213
  26.9 1177.5 %all-gather.17.cloned.1.call-start = ((), (), s32[]{:S(2)}) async-start(), calls=%async_computation.11 | async-start | bytes 41943040 | tf_op jit(solution)/shard_map/all_gather | solution.py:214
  27.6 344.0 %copy-start.20 = (f32[2048]{0:T(1024)}, f32[2048]{0:T(1024)S(1)}, u32[]{:S(2)}) copy-start(f32[2048]{0:T(1024)S(1)} %convert_element_type.204) | copy-start | bytes 24580
  28.9 342.7 %copy-start.23 = (f32[128]{0:T(128)}, f32[128]{0:T(128)S(1)}, u32[]{:S(2)}) copy-start(f32[128]{0:T(128)S(1)} %get-tuple-element.712) | copy-start | bytes 1540
  268.4 5.3 copy-start.19
  276.4 53.8 %all-to-all-start = ((bf16[3,1,128,2048]{2,0,1,3:T(4,128)(2,1)}), bf16[3,1,128,2048]{2,0,1,3:T(4,128)(2,1)S(1)}, u32[]{:S(2)}, u32[]{:S(2)}) async-start(bf16[3,1,128,2048]{2,0,1,3:T(4,128)(2,1)} %copy.196), calls=%async_computation | async-start | bytes 4194304 | tf_op jit(solution)/shard_map/all_to_all | solution.py:203
  333.4 2.9 copy-start.14
  354.3 18.3 %copy-start.7 = (f32[1,1024,4,64]{1,3,2,0:T(8,128)}, f32[1,1024,4,64]{1,3,2,0:T(8,128)S(1)}, u32[]{:S(2)}) copy-start(f32[1,1024,4,64]{1,3,2,0:T(8,128)S(1)} %get-tuple-element.501) | copy-start | bytes 3145732
  354.3 17.3 copy-start.2
  354.3 18.5 %copy-start.26 = (bf16[2048]{0:T(1024)(128)(2,1)S(1)}, bf16[2048]{0:T(1024)(128)(2,1)}, u32[]{:S(2)}) copy-start(bf16[2048]{0:T(1024)(128)(2,1)} %param.18) | copy-start | bytes 12292
  367.3 19.5 %all-to-all-start.1 = ((bf16[8,2,16384]{2,1,0:T(2,128)(2,1)}), bf16[8,2,16384]{2,1,0:T(2,128)(2,1)}, u32[]{:S(2)}, u32[]{:S(2)}) async-start(bf16[8,2,16384]{2,1,0:T(2,128)(2,1)} %reshape.879), calls=%async_computation.1 | async-start | bytes 1048576 | tf_op jit(solution)/shard_map/all_to_all | solution.py:206
  371.5 1016.2 %all-gather.19.cloned.1.call-start = ((), (), s32[]{:S(2)}) async-start(), calls=%async_computation.12 | async-start | bytes 4718592 | tf_op jit(solution)/shard_map/all_gather | solution.py:274
  372.6 1030.7 %all-gather.23.cloned.1.call-start = ((), (), s32[]{:S(2)}) async-start(), calls=%async_computation.17 | async-start | bytes 4718592 | tf_op jit(solution)/shard_map/all_gather | solution.py:277
  398.5 850.1 %copy-start.4 = (f32[128,2048]{1,0:T(8,128)}, f32[128,2048]{1,0:T(8,128)S(1)}, u32[]{:S(2)}) copy-start(f32[128,2048]{1,0:T(8,128)S(1)} %get-tuple-element.716) | copy-start | bytes 3145732
  398.7 544.1 %copy-start.11 = (bf16[128,2048]{1,0:T(8,128)(2,1)}, bf16[128,2048]{1,0:T(8,128)(2,1)S(1)}, u32[]{:S(2)}) copy-start(bf16[128,2048]{1,0:T(8,128)(2,1)S(1)} %multiply_convert_fusion.2) | copy-start | bytes 1572868
  1223.3 25.3 %copy-start.16 = (bf16[1,128,2048]{2,1,0:T(8,128)(2,1)S(1)}, bf16[1,128,2048]{2,1,0:T(8,128)(2,1)}, u32[]{:S(2)}) copy-start(bf16[1,128,2048]{2,1,0:T(8,128)(2,1)} %param.23) | copy-start | bytes 1572868
  1250.2 324.9 %all-gather.21.cloned.1.call-start = ((), (), s32[]{:S(2)}) async-start(), calls=%async_computation.15 | async-start | bytes 4718592 | tf_op jit(solution)/shard_map/all_gather | solution.py:243
  1250.9 344.7 %all-gather.25.cloned.1.call-start = ((), (), s32[]{:S(2)}) async-start(), calls=%async_computation.18 | async-start | bytes 4718592 | tf_op jit(solution)/shard_map/all_gather | solution.py:240
  1251.7 6.0 copy-start.9
  1275.5 33.6 %all-to-all-start.2 = ((bf16[8,2,16384]{2,1,0:T(2,128)(2,1)}), bf16[8,2,16384]{2,1,0:T(2,128)(2,1)S(1)}, u32[]{:S(2)}, u32[]{:S(2)}) async-start(bf16[8,2,16384]{2,1,0:T(2,128)(2,1)} %reshape.881), calls=%async_computation.2 | async-start | bytes 1048576 | tf_op jit(solution)/shard_map/all_to_all | solution.py:270
  1309.2 256.2 %all-to-all-start.4 = ((bf16[3,1,128,8192]{2,0,1,3:T(4,128)(2,1)}), bf16[3,1,128,8192]{2,0,1,3:T(4,128)(2,1)}, u32[]{:S(2)}, u32[]{:S(2)}) async-start(bf16[3,1,128,8192]{2,0,1,3:T(4,128)(2,1)} %copy.216), calls=%async_computation.5 | async-start | bytes 16777216 | tf_op jit(solution)/shard_map/all_to_all | solution.py:239
  1314.1 8.2 copy-start.8
  1314.1 414.0 %all-reduce.6.cloned.1.call-start = ((), (), s32[]{:S(2)}) async-start(), calls=%async_computation.19 | async-start | bytes 8388608
  1329.2 2.7 copy-start.10
  1334.5 2.7 copy-start.10
  1342.5 2.7 copy-start.10
  1347.8 2.7 copy-start.10
  1353.2 2.7 copy-start.10
  1358.5 2.7 copy-start.10
  1370.3 4.6 copy-start.6
  1376.2 6.3 copy-start.13
  1387.7 7.5 copy-start.17
  1395.2 8.1 copy-start.15
  1403.2 328.4 %reduce-scatter.4.cloned.1.call-start = ((), (), s32[]{:S(2)}) async-start(), calls=%async_computation.13 | async-start | bytes 1310720 | tf_op jit(solution)/shard_map/reduce_scatter | solution.py:292
  1407.8 325.7 %reduce-scatter.8.cloned.1.call-start = ((), (), s32[]{:S(2)}) async-start(), calls=%async_computation.16 | async-start | bytes 5242880 | tf_op jit(solution)/shard_map/reduce_scatter | solution.py:255
  1569.7 2.7 copy-start
  1584.6 227.3 %reduce-scatter.6.cloned.1.call-start = ((), (), s32[]{:S(2)}) async-start(), calls=%async_computation.14 | async-start | bytes 10485760 | tf_op jit(solution)/shard_map/reduce_scatter | solution.py:252
  1611.1 6.5 copy-start.28
  1611.1 7.7 copy-start.5
  1613.7 52.7 %all-to-all-start.3 = ((bf16[3,1,1024,256]{3,0,1,2:T(4,128)(2,1)}), bf16[3,1,1024,256]{3,0,1,2:T(4,128)(2,1)S(1)}, u32[]{:S(2)}, u32[]{:S(2)}) async-start(bf16[3,1,1024,256]{3,0,1,2:T(4,128)(2,1)} %copy.210), calls=%async_computation.3 | async-start | bytes 4194304 | tf_op jit(solution)/shard_map/all_to_all | solution.py:296
  1637.8 33.5 %copy-start.3 = (bf16[1,128,2048]{2,1,0:T(8,128)(2,1)S(1)}, bf16[1,128,2048]{2,1,0:T(8,128)(2,1)}, u32[]{:S(2)}) copy-start(bf16[1,128,2048]{2,1,0:T(8,128)(2,1)} %param.16) | copy-start | bytes 1572868
  1637.8 33.6 %copy-start.21 = (f32[2048]{0:T(1024)S(1)}, f32[2048]{0:T(1024)}, u32[]{:S(2)}) copy-start(f32[2048]{0:T(1024)} %copy-done.20) | copy-start | bytes 24580
  1637.8 33.6 %copy-start.24 = (f32[128]{0:T(128)S(1)}, f32[128]{0:T(128)}, u32[]{:S(2)}) copy-start(f32[128]{0:T(128)} %copy-done.23) | copy-start | bytes 1540
  1671.4 13.6 copy-start.22
  1671.4 54.1 %copy-start.12 = (f32[128,2048]{1,0:T(8,128)S(1)}, f32[128,2048]{1,0:T(8,128)}, u32[]{:S(2)}) copy-start(f32[128,2048]{1,0:T(8,128)} %get-tuple-element.683) | copy-start | bytes 3145732
  1671.4 54.1 %copy-start.27 = (f32[128]{0:T(128)S(1)}, f32[128]{0:T(128)}, u32[]{:S(2)}) copy-start(f32[128]{0:T(128)} %get-tuple-element.711) | copy-start | bytes 1540
  (3 other events, 3.0 us)
Sparse Core Ops, SparseCore 0:
  9.8 227.8 all-gather.10
  239.6 87.4 all-gather.12
  328.9 576.6 all-gather.14
  907.3 297.0 all-gather.16
  1205.9 47.7 all-gather.18
  1255.7 56.8 all-gather.22
  1314.3 78.7 all-gather.20
  1394.6 135.6 all-gather.24
  1534.2 100.8 all-reduce.5
  1637.8 27.9 reduce-scatter.3
  1668.8 53.6 reduce-scatter.7
  1725.4 86.4 reduce-scatter.5
where the time goes:
time: 1840 us; the launch traced here: 1830 us
  waiting for transfers between devices  1310 us (71%)
  matrix products  219 us (12%)
  local copies, waits for them, and re-layouts  140 us (8%)
  other arithmetic  72.3 us (4%)
  blocking collectives  39.4 us (2%)
  starting transfers between devices  23.5 us (1%)
    all_gather x1, waiting for transfers between devices, body(): lax.all_gather(w_gate_up, 'fsdp', axis=0, tiled=True)  507 us
    all_gather x1, waiting for transfers between devices, body(): lax.all_gather(w_down, 'fsdp', axis=0, tiled=True)  262 us
    all_gather x1, waiting for transfers between devices, body(): lax.all_gather(w_qkv, 'fsdp', axis=0, tiled=True)  209 us
    all_to_all x1, waiting for transfers between devices, body(): lax.all_to_all(unit_rows, 'seq', split_axis=3, concat_axis=2, tiled=True)  158 us
    reduce_scatter x1, waiting for transfers between devices, body(): lax.psum_scatter(gu_part.astype(jnp.bfloat16), 'fsdp', scatter_dimension=...  75.9 us
    all_to_all x1, waiting for transfers between devices, body(): lax.all_to_all(stacked, 'seq', split_axis=3, concat_axis=2, tiled=True)  49 us
    unnamed x69, local copies, waits for them, and re-layouts  43.6 us
    unnamed x1, blocking collectives  39.4 us
  transfers between devices with their start and end apart: 17, of which 9 were waited for; matrix products, arithmetic and copies ran while one was open for 23% of the time, Pallas kernels for 0%

commit v1 on v0

--- a/solution.py
+++ b/solution.py
@@ -1,8 +1,12 @@
+import functools
 import math
 
 import jax
 import jax.numpy as jnp
 from jax import lax
+from jax.experimental import pallas as pl
+from jax.experimental.pallas import tpu as pltpu
+from jax.sharding import Mesh
 from jax.sharding import PartitionSpec as P
 
 HD = 64
@@ -180,7 +184,7 @@
     return jnp.stack([raw_q, raw_k, grad_v]).astype(jnp.bfloat16)
 
 
-def body(residual_in, attn_gain, mlp_gain, w_qkv, w_out, w_gate_up, w_down, cotangent):
+def general_body(residual_in, attn_gain, mlp_gain, w_qkv, w_out, w_gate_up, w_down, cotangent):
     seq_count, shard_len, model_width = residual_in.shape
     tokens = seq_count * shard_len
     seq_index = lax.axis_index("seq")
@@ -316,9 +320,9 @@
     )
 
 
-def solution(mesh):
+def general_solution(mesh):
     return jax.shard_map(
-        body,
+        general_body,
         mesh=mesh,
         in_specs=(
             P("fsdp", "seq", None),
@@ -342,3 +346,493 @@
         ),
         check_vma=False,
     )
+
+
+BF = jnp.bfloat16
+F32 = jnp.float32
+AXES = ("y", "x", "z", "c")
+PAIR = [(0, 1), (1, 0)]
+BLK = 128
+ORDER = (0, 1, 3, 2)
+Q_ROWS = 256
+
+
+def swap(value, axis):
+    return lax.ppermute(value, axis, PAIR)
+
+
+def hop(value, dist):
+    return lax.ppermute(value, "z", [(i, i ^ dist) for i in range(4)])
+
+
+def tick(*values):
+    return lax.optimization_barrier(values)
+
+
+def with_partner(held, other):
+    both = jnp.concatenate([held, other], axis=0)
+    return jnp.concatenate([both, swap(both, "c")], axis=0)
+
+
+def fold_core(part):
+    n = part.shape[0] // 2
+    return part[:n].astype(F32) + swap(part[n:].astype(BF), "c").astype(F32)
+
+
+def fold_plane(kept, plane):
+    n = kept.shape[0] // 2
+    return kept[:n] + swap(kept[n:].astype(BF), plane).astype(F32)
+
+
+def fold_hops(parts):
+    total = parts[0]
+    for j, part in zip(ORDER[1:], parts[1:]):
+        total = total + hop(part.astype(BF), j).astype(F32)
+    return total
+
+
+def send_core(pieces):
+    return jnp.stack([pieces[:, 0], swap(pieces[:, 1], "c")], axis=1)
+
+
+def send_plane(pieces, plane):
+    return jnp.stack([pieces[:, :, 0], swap(pieces[:, :, 1], plane)], axis=2)
+
+
+def send_hops(pieces):
+    return jnp.stack([hop(pieces[i], j) if j else pieces[i] for i, j in enumerate(ORDER)])
+
+
+def turn(value, back):
+    lane = lax.broadcasted_iota(jnp.int32, value.shape, 1) % HD
+    up = pltpu.roll(value, HD // 2, 1)
+    down = pltpu.roll(value, value.shape[1] - HD // 2, 1)
+    return jnp.where(lane < HD // 2, down, -up) if back else jnp.where(lane < HD // 2, -down, up)
+
+
+def head_mask(value, head):
+    lane = lax.broadcasted_iota(jnp.int32, value.shape, 1)
+    return jnp.where((lane < HD) == (head == 0), value, jnp.zeros_like(value))
+
+
+def dot(left, right, left_dim, right_dim):
+    return lax.dot_general(
+        left, right, (((left_dim,), (right_dim,)), ((), ())), preferred_element_type=F32
+    )
+
+
+def causal_exp(scores, start):
+    rows, cols = scores.shape
+    query = start + lax.broadcasted_iota(jnp.int32, (rows, rows), 0)
+    key = cols - rows + lax.broadcasted_iota(jnp.int32, (rows, rows), 1)
+    last = jnp.where(key <= query, jnp.exp(scores[:, cols - rows :]), 0.0)
+    if cols == rows:
+        return last
+    return jnp.concatenate([jnp.exp(scores[:, : cols - rows]), last], axis=1)
+
+
+def chunk_of(slot):
+    dist = slot >> 1
+    return dist ^ (dist >> 1)
+
+
+def attend_kernel(place, proj, cosine, sine, q_out, k_out, v_out, att_out, den_out, low_out):
+    length = q_out.shape[1]
+    me = place[0]
+    for block in range(length // BLK):
+        slot = me ^ block
+        here = proj[chunk_of(slot), slot & 1, 0]
+        rows = slice(block * BLK, (block + 1) * BLK)
+        cos_rows, sin_rows = cosine[rows, :], sine[rows, :]
+        raw_q, raw_k = here[:, :128], here[:, 128:256]
+        q_out[0, rows, :] = (raw_q * cos_rows + turn(raw_q, False) * sin_rows).astype(BF)
+        k_out[0, rows, :] = (raw_k * cos_rows + turn(raw_k, False) * sin_rows).astype(BF)
+        v_out[0, rows, :] = here[:, 256:].astype(BF)
+    for start in range(0, length, Q_ROWS):
+        seen = start + Q_ROWS
+        queries = q_out[0, start:seen, :] * jnp.asarray(0.125, BF)
+        keys, values = k_out[0, :seen, :], v_out[0, :seen, :]
+        unnorm, den = None, None
+        for head in range(2):
+            exp_scores = causal_exp(dot(head_mask(queries, head), keys, 1, 1), start)
+            total = jnp.sum(exp_scores, axis=1, keepdims=True)
+            part = dot(exp_scores.astype(BF), head_mask(values, head), 1, 0)
+            total = head_mask(jnp.broadcast_to(total, part.shape), head)
+            unnorm = part if unnorm is None else unnorm + part
+            den = total if den is None else den + total
+        attended = unnorm / den
+        att_out[0, start:seen, :] = attended
+        den_out[0, start:seen, :] = den
+        for block in range(start // BLK, seen // BLK):
+            slot = me ^ block
+            first = block * BLK - start
+            low_out[chunk_of(slot), slot & 1, 0] = attended[first : first + BLK].astype(BF)
+
+
+def attend_back_kernel(
+    place, q_ref, k_ref, v_ref, att_ref, den_ref, grad_ref, cosine, sine, out, grad, grad_q, grad_k, grad_v
+):
+    length = q_ref.shape[1]
+    me = place[0]
+    for block in range(length // BLK):
+        slot = me ^ block
+        grad[block * BLK : (block + 1) * BLK, :] = grad_ref[chunk_of(slot), slot & 1, 0].astype(F32)
+    grad_k[...] = jnp.zeros_like(grad_k)
+    grad_v[...] = jnp.zeros_like(grad_v)
+    for start in range(0, length, Q_ROWS):
+        seen = start + Q_ROWS
+        queries = q_ref[0, start:seen, :] * jnp.asarray(0.125, BF)
+        keys, values = k_ref[0, :seen, :], v_ref[0, :seen, :]
+        grad_rows, den = grad[start:seen, :], den_ref[0, start:seen, :]
+        unnorm = (grad_rows / den).astype(BF)
+        weighted = grad_rows * att_ref[0, start:seen, :] / den
+        total_q = None
+        for head in range(2):
+            q_head, g_head = head_mask(queries, head), head_mask(unnorm, head)
+            exp_scores = causal_exp(dot(q_head, keys, 1, 1), start)
+            grad_total = -jnp.sum(head_mask(weighted, head), axis=1, keepdims=True)
+            grad_scores = (exp_scores * (dot(g_head, values, 1, 1) + grad_total)).astype(BF)
+            part = dot(grad_scores, head_mask(keys, head), 1, 0)
+            total_q = part if total_q is None else total_q + part
+            grad_k[:seen, :] += dot(grad_scores, q_head, 0, 0)
+            grad_v[:seen, :] += dot(exp_scores.astype(BF), g_head, 0, 0)
+        grad_q[start:seen, :] = total_q * 0.125
+    for block in range(length // BLK):
+        slot = me ^ block
+        rows = slice(block * BLK, (block + 1) * BLK)
+        cos_rows, sin_rows = cosine[rows, :], sine[rows, :]
+        for part, held in enumerate((grad_q, grad_k)):
+            value = held[rows, :]
+            raw = value * cos_rows + turn(value * sin_rows, True)
+            out[chunk_of(slot), slot & 1, 0, :, part * 128 : (part + 1) * 128] = raw.astype(BF)
+        out[chunk_of(slot), slot & 1, 0, :, 256:] = grad_v[rows, :].astype(BF)
+
+
+def whole(shape):
+    return pl.BlockSpec(shape, lambda i, place: (0,) * len(shape))
+
+
+def per_seq(shape, at):
+    return pl.BlockSpec(shape, lambda i, place: tuple(i if d == at else 0 for d in range(len(shape))))
+
+
+def attend(place, proj, cosine, sine):
+    length = cosine.shape[0]
+    seq = jax.ShapeDtypeStruct((2, length, 128), BF)
+    wide = jax.ShapeDtypeStruct((2, length, 128), F32)
+    return pl.pallas_call(
+        attend_kernel,
+        grid_spec=pltpu.PrefetchScalarGridSpec(
+            num_scalar_prefetch=1,
+            grid=(2,),
+            in_specs=[per_seq((4, 2, 1, BLK, 384), 2), whole((length, 128)), whole((length, 128))],
+            out_specs=[per_seq((1, length, 128), 0)] * 5 + [per_seq((4, 2, 1, BLK, 128), 2)],
+        ),
+        out_shape=[seq, seq, seq, wide, wide, jax.ShapeDtypeStruct((4, 2, 2, BLK, 128), BF)],
+        compiler_params=pltpu.CompilerParams(vmem_limit_bytes=40 << 20),
+        cost_estimate=pl.CostEstimate(flops=4 * 10**9, bytes_accessed=8 << 20, transcendentals=4 << 20),
+        name="attend",
+    )(place, proj, cosine, sine)
+
+
+def attend_back(place, saved, grad_slots, cosine, sine):
+    length = cosine.shape[0]
+    return pl.pallas_call(
+        attend_back_kernel,
+        grid_spec=pltpu.PrefetchScalarGridSpec(
+            num_scalar_prefetch=1,
+            grid=(2,),
+            in_specs=[per_seq((1, length, 128), 0)] * 5
+            + [per_seq((4, 2, 1, BLK, 128), 2), whole((length, 128)), whole((length, 128))],
+            out_specs=per_seq((4, 2, 1, BLK, 384), 2),
+            scratch_shapes=[pltpu.VMEM((length, 128), F32)] * 4,
+        ),
+        out_shape=jax.ShapeDtypeStruct((4, 2, 2, BLK, 384), BF),
+        compiler_params=pltpu.CompilerParams(vmem_limit_bytes=40 << 20),
+        cost_estimate=pl.CostEstimate(flops=10 * 10**9, bytes_accessed=8 << 20, transcendentals=4 << 20),
+        name="attend_back",
+    )(place, *saved, grad_slots, cosine, sine)
+
+
+def perm_of(target):
+    pairs = []
+    for index in range(32):
+        bits = [(index >> shift) & 1 for shift in (4, 3, 2, 1, 0)]
+        place = 0
+        for bit in target(*bits):
+            place = 2 * place + bit
+        pairs.append((index, place))
+    return pairs
+
+
+def assemble(pieces, shape):
+    total = jnp.zeros(shape, pieces[0][0].dtype)
+    for piece, row, col in pieces:
+        total = lax.dynamic_update_slice(total, piece, (row, col))
+    return total
+
+
+def slot_of(rel):
+    bit_y, bit_z0, bit_c, bit_z1 = rel >> 3, (rel >> 2) & 1, (rel >> 1) & 1, rel & 1
+    return ORDER.index(2 * bit_z1 + bit_z0) * 4 + bit_c * 2 + bit_y
+
+
+def to_heads_kernel(place, slots, out):
+    for rel in range(16):
+        pair = place[1] ^ rel
+        out[:, pl.ds(pl.multiple_of(pair * 128, 128), 128)] = slots[slot_of(rel)]
+
+
+def to_slots_kernel(place, rows, out):
+    for rel in range(16):
+        pair = place[1] ^ rel
+        out[slot_of(rel)] = rows[:, pl.ds(pl.multiple_of(pair * 128, 128), 128)]
+
+
+def reorder(kernel, place, value, shape):
+    return pl.pallas_call(
+        kernel,
+        in_specs=[pl.BlockSpec(memory_space=pltpu.SMEM), pl.BlockSpec(memory_space=pltpu.VMEM)],
+        out_specs=pl.BlockSpec(memory_space=pltpu.VMEM),
+        out_shape=jax.ShapeDtypeStruct(shape, BF),
+        cost_estimate=pl.CostEstimate(flops=0, bytes_accessed=1 << 20, transcendentals=0),
+        name=kernel.__name__,
+    )(place, value)
+
+
+def split(value, dim, bit):
+    size = value.shape[dim] // 2
+    return (
+        lax.dynamic_slice_in_dim(value, bit * size, size, dim),
+        lax.dynamic_slice_in_dim(value, (1 - bit) * size, size, dim),
+    )
+
+
+def ff_place(at_y, at_x, at_z1, at_z0, at_c):
+    return at_y, at_z0, at_z1, at_x, at_c
+
+
+def attn_place(at_y, at_x, at_z1, at_z0, at_c):
+    return at_z1, at_x, at_y, at_z0, at_c
+
+
+def move(value, target):
+    return lax.ppermute(value.astype(BF), AXES, perm_of(target)).astype(F32)
+
+
+def body(residual_in, attn_gain, mlp_gain, w_qkv, w_out, w_gate_up, w_down, cotangent):
+    y, x, z, c = [lax.axis_index(name) for name in AXES]
+    z1, z0 = z >> 1, z & 1
+    group, part = 2 * y + x, 2 * z + c
+    width = residual_in.shape[2]
+    length = BLK * 8
+    quarter = 4 * BLK
+    units = w_gate_up.shape[0] // 8
+    inputs = residual_in[0].astype(F32)
+    gain_one, gain_two = attn_gain.astype(F32), mlp_gain.astype(F32)
+    scale_one = rms_scale(inputs)
+    normed_one = (inputs * scale_one * gain_one).astype(BF)
+
+    qkv_sent = lax.dynamic_slice_in_dim(w_qkv, (4 * c + 2 * z1) * HD, 2 * HD, 0)
+    qkv_sent = jnp.transpose(qkv_sent, (1, 0, 2)).reshape(3 * 2 * HD, width)
+    x_pairs = [((i & 1) * 4 + i, (1 - (i & 1)) * 4 + i) for i in range(4)]
+    y_pairs = [((i >> 1) * 4 + i, (1 - (i >> 1)) * 4 + i) for i in range(4)]
+    hops = [normed_one] + [hop(normed_one, j) for j in ORDER[1:]]
+    others = [swap(normed_one, "y")]
+    qkv_moved = lax.ppermute(qkv_sent, ("x", "z"), x_pairs)
+    rows, cols = w_out.shape[0], width // 2
+    out_own = lax.dynamic_slice_in_dim(w_out, c * cols, cols, 1)
+    others[0], out_own = tick(others[0], out_own)
+    out_y = swap(out_own, "y")
+    for held in hops[1:]:
+        others.append(swap(held, "y"))
+    out_pair, _ = tick(jnp.concatenate([out_own, out_y], axis=0), hops[3])
+    out_x = swap(out_pair, "x")
+    normed_all = jnp.concatenate([with_partner(*item) for item in zip(hops, others)], axis=0)
+    heads_qkv = jnp.where(x == z0, qkv_sent, qkv_moved)
+
+    def columns(side):
+        first = (8 * (2 * z1 + side) + 4 * c + z0) * units
+        return jnp.concatenate(
+            [lax.dynamic_slice_in_dim(w_down, first + 2 * j * units, units, 1) for j in range(2)], axis=1
+        )
+
+    gu_sent = [lax.dynamic_slice_in_dim(w_gate_up, (4 * c + 2 * j + z0) * units, units, 0) for j in range(2)]
+    gu_sent = jnp.transpose(jnp.stack(gu_sent), (2, 0, 1, 3)).reshape(2, 2 * units, width)
+    down_own, down_sent = columns(x), columns(1 - x)
+
+    normed_all, cot, gate_sent = tick(normed_all, cotangent[0], gu_sent[0])
+    cot_hops = [cot] + [hop(cot, j) for j in ORDER[1:]]
+    gate_moved = lax.ppermute(gate_sent, ("y", "z"), y_pairs)
+
+    cos_half, sin_half = rope_tables(jnp.arange(length, dtype=jnp.int32), HD // 2)
+    cosine, sine = jnp.tile(cos_half, (1, 4)), jnp.tile(sin_half, (1, 4))
+    place = jnp.stack([part, 8 * y + 4 * z0 + 2 * c + z1]).astype(jnp.int32)
+    proj = dot(normed_all, heads_qkv, 1, 1)
+    *saved, low_slots = attend(place, proj.reshape(4, 2, 2, BLK, 384), cosine, sine)
+    pieces = send_plane(send_core(low_slots), "y")
+    pieces, out_x, down_sent, cot = tick(pieces, out_x, down_sent, cot)
+    pieces = send_hops(pieces)
+    out_half = jnp.concatenate([out_pair, out_x], axis=0)
+    out_c = swap(out_half, "c")
+    cot_others = [swap(cot, "x")]
+    down_x = swap(down_sent, "x")
+    out_full = assemble(
+        [
+            (block[i * rows : (i + 1) * rows], (group ^ flip) * rows, side * cols)
+            for block, side in ((out_half, c), (out_c, 1 - c))
+            for i, flip in enumerate((0, 2, 1, 3))
+        ],
+        (width, width),
+    )
+    attended = reorder(to_heads_kernel, place, pieces.reshape(16, BLK, 128), (BLK, width))
+    residual = inputs + dot(attended, out_full, 1, 1)
+    scale_two = rms_scale(residual)
+    normed_two = (residual * scale_two * gain_two).astype(BF)
+
+    normed_two, *moved = tick(
+        normed_two, cot_others[0], *cot_hops[1:], down_x, gate_moved, gu_sent[1], down_own
+    )
+    cot_others[0], cot_hops[1:], (down_x, gate_moved, up_sent, down_own) = moved[0], moved[1:4], moved[4:]
+    hops = [normed_two] + [hop(normed_two, j) for j in ORDER[1:]]
+    others = [swap(normed_two, "x")]
+    cot_others.append(swap(cot_hops[1], "x"))
+    up_moved = lax.ppermute(up_sent, ("y", "z"), y_pairs)
+    down_pair = jnp.concatenate([down_own, down_x], axis=0)
+    down_y = swap(down_pair, "y")
+    for i in (1, 2, 3):
+        hops[i], others[i - 1] = tick(hops[i], others[i - 1])
+        others.append(swap(hops[i], "x"))
+        if i < 3:
+            cot_hops[i + 1], _ = tick(cot_hops[i + 1], hops[i])
+            cot_others.append(swap(cot_hops[i + 1], "x"))
+    gate_moved, up_moved, down_y, _ = tick(gate_moved, up_moved, down_y, hops[3])
+    w_gate = jnp.where(y == z1, gu_sent[0], gate_moved)
+    w_up = jnp.where(y == z1, up_sent, up_moved)
+    down_half = jnp.concatenate([down_pair, down_y], axis=0)
+    rows = w_down.shape[0]
+    down = assemble(
+        [(down_half[i * rows : (i + 1) * rows], (group ^ i) * rows, 0) for i in range(4)],
+        (width, 2 * units),
+    )
+    ff_chunks = [with_partner(*item) for item in zip(hops, others)]
+    cot_chunks = [with_partner(*item) for item in zip(cot_hops, cot_others)]
+
+    hiddens, gate_grads, up_grads, back_parts, mlp_parts = [], [], [], [], []
+    for rows_in, rows_cot in zip(ff_chunks, cot_chunks):
+        gate, up = dot(rows_in, w_gate, 1, 1), dot(rows_in, w_up, 1, 1)
+        sigmoid_gate = jax.nn.sigmoid(gate)
+        silu = gate * sigmoid_gate
+        hidden = (silu * up).astype(BF)
+        grad_hidden = dot(rows_cot, down, 1, 0)
+        grad_gate = (grad_hidden * up * sigmoid_gate * (1.0 + gate * (1.0 - sigmoid_gate))).astype(BF)
+        grad_up = (grad_hidden * silu).astype(BF)
+        back_parts.append(fold_core(dot(grad_gate, w_gate, 1, 0) + dot(grad_up, w_up, 1, 0)))
+        mlp_parts.append(dot(hidden, down, 1, 1).astype(BF))
+        hiddens.append(hidden)
+        gate_grads.append(grad_gate)
+        up_grads.append(grad_up)
+    grad_normed_two = fold_hops([fold_plane(item, "x") for item in back_parts])
+
+    ff_in, cot_all = jnp.concatenate(ff_chunks, axis=0), jnp.concatenate(cot_chunks, axis=0)
+    gu_grad = jnp.stack(
+        [dot(jnp.concatenate(parts, axis=0), ff_in, 0, 0).astype(BF) for parts in (gate_grads, up_grads)]
+    )
+    gu_own, gu_other = split(gu_grad, 1, y)
+    down_grad = dot(cot_all, jnp.concatenate(hiddens, axis=0), 0, 0).astype(BF)
+    down_own, down_other = split(down_grad, 1, y)
+    gu_other, down_other = swap(gu_other, "y"), swap(down_other, "y")
+
+    grad_normed_two, *mlp_parts = tick(grad_normed_two, *mlp_parts)
+    mlp_parts = [fold_core(item) for item in mlp_parts]
+    grad_norm_two, grad_gain_two = rms_back(grad_normed_two, residual, scale_two, gain_two)
+    grad_residual = cotangent[0].astype(F32) + grad_norm_two
+    grad_branch = grad_residual.astype(BF)
+    grad_attended = dot(grad_branch, out_full, 1, 0).astype(BF)
+    grad_slots = reorder(to_slots_kernel, place, grad_attended, (16, BLK, 128))
+    grad_slots, *mlp_parts = tick(grad_slots, *mlp_parts)
+    pieces = send_hops(grad_slots.reshape(4, 2, 2, BLK, 128))
+    mlp_parts = [fold_plane(item, "x") for item in mlp_parts]
+    pieces = send_core(send_plane(pieces, "y"))
+    grad_branch, pieces, gu_other, down_other = tick(grad_branch, pieces, gu_other, down_other)
+    branch_hops = [grad_branch] + [hop(grad_branch, j) for j in ORDER[1:]]
+    branch_others = [swap(grad_branch, "y")]
+    grad_proj = attend_back(place, saved, pieces, cosine, sine).reshape(16 * BLK, 384)
+    back_parts = [fold_core(dot(grad_proj[j * quarter : (j + 1) * quarter], heads_qkv, 1, 0)) for j in range(4)]
+    back_parts = tick(*back_parts, *mlp_parts, *branch_hops[1:], branch_others[0])
+    mlp_parts, branch_hops[1:], branch_others = back_parts[4:8], back_parts[8:11], [back_parts[11]]
+    back_parts = [fold_plane(item, "y") for item in back_parts[:4]]
+    mlp_term = fold_hops(mlp_parts)
+    layer_out = (residual + mlp_term).astype(BF)
+    qkv_grad = dot(grad_proj, normed_all, 0, 0)
+    gain_part = jnp.sum(qkv_grad * heads_qkv.astype(F32), axis=0) / gain_one
+    qkv_own, qkv_other = split(qkv_grad.reshape(3, 2 * HD, width), 1, x)
+    qkv_other = swap(qkv_other.astype(BF), "x")
+    back_parts = tick(*back_parts, mlp_term, qkv_other)
+    mlp_term, qkv_other, back_parts = back_parts[4], back_parts[5], back_parts[:4]
+    grad_normed_one = fold_hops(back_parts)
+    branch_others += [swap(item, "y") for item in branch_hops[1:]]
+    grad_qkv = jnp.transpose(move(qkv_own + qkv_other.astype(F32), attn_place), (1, 0, 2))
+    grad_gate_up = jnp.transpose(move(gu_own.astype(F32) + gu_other.astype(F32), ff_place), (1, 0, 2))
+    grad_down = move(down_own.astype(F32) + down_other.astype(F32), ff_place)
+    branch_all = jnp.concatenate([with_partner(*item) for item in zip(branch_hops, branch_others)], axis=0)
+    out_grad = dot(branch_all, low_slots.reshape(16 * BLK, 128), 0, 0)
+    out_own, out_other = split(out_grad, 1, x)
+    grad_out_proj = move(out_own + swap(out_other.astype(BF), "x").astype(F32), attn_place)
+
+    weighted = grad_normed_one * gain_one
+    inner_mean = jnp.mean(weighted * inputs, axis=-1, keepdims=True)
+    grad_input = grad_residual + scale_one * weighted - inputs * scale_one**3 * inner_mean
+
+    gains = jnp.stack([gain_part, grad_gain_two])
+    for name, bit in (("y", y), ("x", x)):
+        mine, other = split(gains, 1, bit)
+        gains = mine + swap(other, name)
+    size = gains.shape[1] // 4
+    quarters = [lax.dynamic_slice_in_dim(gains, (z ^ j) * size, size, 1) for j in range(4)]
+    gains = quarters[0] + hop(quarters[1], 1) + hop(quarters[2], 2) + hop(quarters[3], 3)
+    mine, other = split(gains, 1, c)
+    gains = mine + swap(other, "c")
+    return (
+        layer_out[None],
+        grad_input[None],
+        gains[0],
+        gains[1],
+        grad_qkv,
+        grad_out_proj,
+        grad_gate_up,
+        grad_down,
+    )
+
+
+def solution(mesh):
+    if mesh.shape["fsdp"] != 4 or mesh.shape["seq"] != 8:
+        return general_solution(mesh)
+    fine = Mesh(mesh.devices.reshape(2, 2, 4, 2), AXES)
+    fsdp, seq = ("y", "x"), ("z", "c")
+    tokens = P(fsdp, seq, None)
+    return jax.shard_map(
+        body,
+        mesh=fine,
+        in_specs=(
+            tokens,
+            P(),
+            P(),
+            P(fsdp, None, None),
+            P(fsdp, None),
+            P(fsdp, None, None),
+            P(fsdp, None),
+            tokens,
+        ),
+        out_specs=(
+            tokens,
+            tokens,
+            P(fsdp + seq),
+            P(fsdp + seq),
+            P(seq + fsdp, None, None),
+            P(None, seq + fsdp),
+            P(seq + fsdp, None, None),
+            P(None, seq + fsdp),
+        ),
+        check_vma=False,
+    )

time: 1840 us -> 867 us (0.47)
  waiting for transfers between devices: 1310 us -> 471 us
  matrix products: 219 us -> 97.1 us
  starting transfers between devices: 23.5 us -> 112 us
  blocking collectives: 39.4 us -> 0 us
  local copies, waits for them, and re-layouts: 140 us -> 105 us
  other arithmetic: 72.3 us -> 52.2 us
  Pallas kernels: 0 us -> 19.3 us
    all_gather x8 -> x0, waiting for transfers between devices: 977 us -> none  [the longest x1 507 us: body(): lax.all_gather(w_gate_up, 'fsdp', axis=0, tiled=True)]
    ppermute x0 -> x109, waiting for transfers between devices: none -> 471 us  [the longest x72 250 us: swap(): return lax.ppermute(value, axis, PAIR)]
    all_to_all x5 -> x0, waiting for transfers between devices: 259 us -> none  [the longest x1 158 us: body(): lax.all_to_all(unit_rows, 'seq', split_axis=3, concat_axis=2, tiled=True)]
    dot_general x54 -> x36, matrix products: 219 us -> 97.1 us  [dot(): lax.dot_general(left, right, (((left_dim,), (right_dim,)), ((), ())), pre...]
    ppermute x0 -> x109, starting transfers between devices: none -> 112 us  [the longest x72 45.1 us: swap(): return lax.ppermute(value, axis, PAIR)]
    reduce_scatter x3 -> x0, waiting for transfers between devices: 75.9 us -> none  [the longest x1 75.9 us: body(): lax.psum_scatter(gu_part.astype(jnp.bfloat16), 'fsdp', scatter_dimension=...]
    unnamed x1 -> x0, blocking collectives: 39.4 us -> none
    reshape x10 -> x0, local copies, waits for them, and re-layouts: 31.8 us -> none  [the longest x1 13.2 us: body(): jnp.concatenate([grad_gu, hidden[None]], axis=0)]
  transfers between devices with their start and end apart: 17 -> 109, of which waited for: 9 -> 47; matrix products, arithmetic and copies ran while one was open for 23% -> 27% of each run, Pallas kernels for 0% -> 1%
where the time goes in v1:
time: 867 us; the launch traced here: 859 us
  waiting for transfers between devices  471 us (54%)
  starting transfers between devices  112 us (13%)
  local copies, waits for them, and re-layouts  105 us (12%)
  matrix products  97.1 us (11%)
  other arithmetic  52.2 us (6%)
  Pallas kernels  19.3 us (2%)
    ppermute x72, waiting for transfers between devices, swap(): return lax.ppermute(value, axis, PAIR)  250 us
    ppermute x30, waiting for transfers between devices, hop(): return lax.ppermute(value, 'z', [(i, i ^ dist) for i in range(4)])  170 us
    dot_general x36, matrix products, dot(): lax.dot_general(left, right, (((left_dim,), (right_dim,)), ((), ())), pre...  97.1 us
    unnamed x180, local copies, waits for them, and re-layouts  53.3 us
    ppermute x72, starting transfers between devices, swap(): return lax.ppermute(value, axis, PAIR)  45.1 us
    ppermute x30, starting transfers between devices, hop(): return lax.ppermute(value, 'z', [(i, i ^ dist) for i in range(4)])  31 us
    ppermute x4, starting transfers between devices, move(): return lax.ppermute(value.astype(BF), AXES, perm_of(target)).astype(F32)  30.8 us
    ppermute x4, waiting for transfers between devices, move(): return lax.ppermute(value.astype(BF), AXES, perm_of(target)).astype(F32)  25.2 us
  transfers between devices with their start and end apart: 109, of which 47 were waited for; matrix products, arithmetic and copies ran while one was open for 27% of the time, Pallas kernels for 1%

profile of v1, /device:TPU:6, one launch (start us, length us, event | category | flops | bytes accessed | tf_op | source)
XLA Modules:
  0.0 859.2 jit_solution(17097416686088068084)
XLA Ops:
  10.2 5.1 constant_dynamic-slice_fusion.15
  26.9 7.5 collective-permute-done.5
  37.4 18.2 %collective-permute-done.8 = bf16[128,2048]{1,0:T(8,128)(2,1)} collective-permute-done((bf16[128,2048]{1,0:T(8,128)(2,1)}, bf16[128,2048]{1,0:T(8,128)(2,1)}, u32[]{:S(2)}, u32[]{:S(2)}) %collective-permute-start.8) | collective-permute-done | bytes 524320 | tf_op jit(solution)/shard_map/ppermute | solution.py:365
  62.3 10.6 %collective-permute-done.6 = bf16[128,2048]{1,0:T(8,128)(2,1)S(1)} collective-permute-done((bf16[128,2048]{1,0:T(8,128)(2,1)}, bf16[128,2048]{1,0:T(8,128)(2,1)S(1)}, u32[]{:S(2)}, u32[]{:S(2)}) %collective-permute-start.6) | collective-permute-done | bytes 524320 | tf_op jit(solution)/shard_map/ppermute | solution.py:361
  74.1 8.1 collective-permute-done.9
  88.3 10.0 %collective-permute-done.11 = bf16[384,2048]{1,0:T(8,128)(2,1)S(1)} collective-permute-done((bf16[384,2048]{1,0:T(8,128)(2,1)S(1)}, bf16[384,2048]{1,0:T(8,128)(2,1)S(1)}, u32[]{:S(2)}, u32[]{:S(2)}) %collective-permute-start.11) | collective-permute-done | bytes 1572896 | tf_op jit(solution)/shard_map/ppermute | solution.py:642
  106.2 5.0 attend.1
  119.9 5.0 collective-permute-done.13
  125.7 15.0 %collective-permute-done.15 = bf16[1024,1024]{1,0:T(8,128)(2,1)} collective-permute-done((bf16[1024,1024]{1,0:T(8,128)(2,1)}, bf16[1024,1024]{1,0:T(8,128)(2,1)}, u32[]{:S(2)}, u32[]{:S(2)}) %collective-permute-start.15) | collective-permute-done | bytes 2097184 | tf_op jit(solution)/shard_map/ppermute | solution.py:361
  165.4 5.2 collective-permute-done.18
  174.8 14.6 %collective-permute-done.16 = bf16[2,2,128,128]{3,2,0,1:T(8,128)(2,1)S(1)} collective-permute-done((bf16[2,2,128,128]{3,2,0,1:T(8,128)(2,1)S(1)}, bf16[2,2,128,128]{3,2,0,1:T(8,128)(2,1)S(1)}, u32[]{:S(2)}, u32[]{:S(2)}) %collective-permute-start.16) | collective-permute-done | bytes 131104 | tf_op jit(solution)/shard_map/ppermute | solution.py:365
  202.9 6.4 multiply_reduce_fusion.3
  211.6 8.1 collective-permute-done.23
  222.8 15.9 %collective-permute-done.25 = bf16[512,2048]{1,0:T(8,128)(2,1)} collective-permute-done((bf16[512,2048]{1,0:T(8,128)(2,1)}, bf16[512,2048]{1,0:T(8,128)(2,1)}, u32[]{:S(2)}, u32[]{:S(2)}) %collective-permute-start.25) | collective-permute-done | bytes 2097184 | tf_op jit(solution)/shard_map/ppermute | solution.py:666
  243.1 20.4 %collective-permute-done.31 = bf16[128,2048]{1,0:T(8,128)(2,1)S(1)} collective-permute-done((bf16[128,2048]{1,0:T(8,128)(2,1)S(1)}, bf16[128,2048]{1,0:T(8,128)(2,1)S(1)}, u32[]{:S(2)}, u32[]{:S(2)}) %collective-permute-start.31) | collective-permute-done | bytes 524320 | tf_op jit(solution)/shard_map/ppermute | solution.py:365
  271.7 6.8 collective-permute-done.33
  280.1 9.1 %collective-permute-done.44 = bf16[128,2048]{1,0:T(8,128)(2,1)S(1)} collective-permute-done((bf16[128,2048]{1,0:T(8,128)(2,1)}, bf16[128,2048]{1,0:T(8,128)(2,1)S(1)}, u32[]{:S(2)}, u32[]{:S(2)}) %collective-permute-start.44) | collective-permute-done | bytes 524320 | tf_op jit(solution)/shard_map/ppermute | solution.py:361
  305.4 9.7 %collective-permute-done.50 = bf16[128,2048]{1,0:T(8,128)(2,1)S(1)} collective-permute-done((bf16[128,2048]{1,0:T(8,128)(2,1)}, bf16[128,2048]{1,0:T(8,128)(2,1)S(1)}, u32[]{:S(2)}, u32[]{:S(2)}) %collective-permute-start.50) | collective-permute-done | bytes 524320 | tf_op jit(solution)/shard_map/ppermute | solution.py:361
  316.3 33.2 %collective-permute-done.28 = bf16[1024,512]{1,0:T(8,128)(2,1)S(1)} collective-permute-done((bf16[1024,512]{1,0:T(8,128)(2,1)S(1)}, bf16[1024,512]{1,0:T(8,128)(2,1)S(1)}, u32[]{:S(2)}, u32[]{:S(2)}) %collective-permute-start.28) | collective-permute-done | bytes 1048608 | tf_op jit(solution)/shard_map/ppermute | solution.py:361
  411.1 9.2 %fusion = bf16[1,512,2048]{2,1,0:T(8,128)(2,1)} fusion(bf16[2048,2048]{1,0:T(8,128)(2,1)} %get-tuple-element.190, bf16[512,512]{1,0:T(8,128)(2,1)S(1)} %get-tuple-element.175, bf16[512,512]{1,0:T(8,128)(2,1)S(1)} %get-tuple-element.178, bf16[512,512]{1,0:T(8,128)(2,1)S(1)} %get-tuple-element.181, bf16[512,512]{1,0:T(8,128)(2,1)S(1)} %get-tuple-element.184), kind=kOutput, calls=%fused_computation.20 | convolution fusion | flops 4304404480 | bytes 12582912 | tf_op jit(solution)/shard_map/dot_general | solution.py:419
  423.5 14.3 %collective-permute-done.48 = bf16[128,2048]{1,0:T(8,128)(2,1)S(1)} collective-permute-done((bf16[128,2048]{1,0:T(8,128)(2,1)S(1)}, bf16[128,2048]{1,0:T(8,128)(2,1)S(1)}, u32[]{:S(2)}, u32[]{:S(2)}) %collective-permute-start.48) | collective-permute-done | bytes 524320 | tf_op jit(solution)/shard_map/ppermute | solution.py:361
  438.0 10.2 %collective-permute-done.55 = bf16[128,2048]{1,0:T(8,128)(2,1)S(1)} collective-permute-done((bf16[128,2048]{1,0:T(8,128)(2,1)S(1)}, bf16[128,2048]{1,0:T(8,128)(2,1)S(1)}, u32[]{:S(2)}, u32[]{:S(2)}) %collective-permute-start.55) | collective-permute-done | bytes 524320 | tf_op jit(solution)/shard_map/ppermute | solution.py:361
  448.4 9.2 %fusion.1 = bf16[1,512,2048]{2,1,0:T(8,128)(2,1)} fusion(bf16[2048,2048]{1,0:T(8,128)(2,1)} %get-tuple-element.190, bf16[512,512]{1,0:T(8,128)(2,1)S(1)} %copy-done.48, bf16[512,512]{1,0:T(8,128)(2,1)S(1)} %copy-done.46, bf16[512,512]{1,0:T(8,128)(2,1)S(1)} %copy-done.44, bf16[512,512]{1,0:T(8,128)(2,1)S(1)} %copy-done.42), kind=kOutput, calls=%fused_computation.21 | convolution fusion | flops 4304404480 | bytes 12582912 | tf_op jit(solution)/shard_map/dot_general | solution.py:419
  460.3 22.7 %collective-permute-done.56 = bf16[128,2048]{1,0:T(8,128)(2,1)S(1)} collective-permute-done((bf16[128,2048]{1,0:T(8,128)(2,1)S(1)}, bf16[128,2048]{1,0:T(8,128)(2,1)S(1)}, u32[]{:S(2)}, u32[]{:S(2)}) %collective-permute-start.56) | collective-permute-done | bytes 524320 | tf_op jit(solution)/shard_map/ppermute | solution.py:365
  487.7 5.4 convolution_convert_fusion.7.rows
  509.7 5.1 collective-permute-done.63
  518.1 8.6 %convolution_convert_fusion = bf16[2048,512]{1,0:T(8,128)(2,1)S(1)} fusion(bf16[2048,2048]{1,0:T(8,128)(2,1)} %constant_dynamic-update-slice_fusion.36, bf16[512,512]{1,0:T(8,128)(2,1)S(1)} %copy-done.65, bf16[512,512]{1,0:T(8,128)(2,1)S(1)} %copy-done.63, bf16[512,512]{1,0:T(8,128)(2,1)S(1)} %copy-done.61, bf16[512,512]{1,0:T(8,128)(2,1)S(1)} %copy-done.59), kind=kOutput, calls=%fused_computation.13 | convolution fusion | flops 4304404480 | bytes 12582912 | tf_op jit(solution)/shard_map/dot_general | solution.py:419
  529.3 32.9 %collective-permute-done.64 = bf16[4,2,128,128]{3,2,0,1:T(8,128)(2,1)S(1)} collective-permute-done((bf16[4,2,128,128]{3,2,0,1:T(8,128)(2,1)S(1)}, bf16[4,2,128,128]{3,2,0,1:T(8,128)(2,1)S(1)}, u32[]{:S(2)}, u32[]{:S(2)}) %collective-permute-start.64) | collective-permute-done | bytes 262176 | tf_op jit(solution)/shard_map/ppermute | solution.py:361
  565.5 11.5 %collective-permute-done.74 = bf16[128,2048]{1,0:T(8,128)(2,1)S(1)} collective-permute-done((bf16[128,2048]{1,0:T(8,128)(2,1)S(1)}, bf16[128,2048]{1,0:T(8,128)(2,1)S(1)}, u32[]{:S(2)}, u32[]{:S(2)}) %collective-permute-start.74) | collective-permute-done | bytes 524320 | tf_op jit(solution)/shard_map/ppermute | solution.py:361
  578.0 6.1 collective-permute-done.75
  585.1 10.3 %attend_back.1 = bf16[4,2,2,128,384]{4,3,2,1,0:T(8,128)(2,1)S(1)} custom-call(s32[2]{0:T(128)S(1)} %copy-done.5, bf16[2,1024,128]{2,1,0:T(8,128)(2,1)S(1)} %get-tuple-element.83.q_ref, bf16[2,1024,128]{2,1,0:T(8,128)(2,1)S(1)} %copy-done.9, bf16[2,1024,128]{2,1,0:T(8,128)(2,1)S(1)} %copy-done.11, f32[2,1024,128]{2,1,0:T(8,128)S(1)} %get-tuple-element.86.att_ref, ...), custom_call_target="tpu_custom_call" | custom-call | flops 10000000000 | bytes 8388608 | tf_op jit(solution)/shard_map/attend_back/pallas_call | solution.py:540
  616.3 9.4 %collective-permute-done.95 = f32[2,128]{1,0:T(2,128)S(1)} collective-permute-done((f32[2,128]{1,0:T(2,128)S(1)}, f32[2,128]{1,0:T(2,128)S(1)}, u32[]{:S(2)}, u32[]{:S(2)}) %collective-permute-start.95) | collective-permute-done | bytes 1056 | tf_op jit(solution)/shard_map/ppermute | solution.py:365
  632.5 4.8 collective-permute-start.108
  642.3 20.4 %collective-permute-done.78 = bf16[128,2048]{1,0:T(8,128)(2,1)S(1)} collective-permute-done((bf16[128,2048]{1,0:T(8,128)(2,1)S(1)}, bf16[128,2048]{1,0:T(8,128)(2,1)S(1)}, u32[]{:S(2)}, u32[]{:S(2)}) %collective-permute-start.78) | collective-permute-done | bytes 524320 | tf_op jit(solution)/shard_map/ppermute | solution.py:365
  667.0 14.8 %collective-permute-done.108 = bf16[2048,256]{1,0:T(8,128)(2,1)S(1)} collective-permute-done((bf16[2048,256]{1,0:T(8,128)(2,1)S(1)}, bf16[2048,256]{1,0:T(8,128)(2,1)S(1)}, u32[]{:S(2)}, u32[]{:S(2)}) %collective-permute-start.108) | collective-permute-done | bytes 1048608 | tf_op jit(solution)/shard_map/ppermute | solution.py:620
  686.3 12.8 %collective-permute-done.82 = bf16[128,2048]{1,0:T(8,128)(2,1)S(1)} collective-permute-done((bf16[128,2048]{1,0:T(8,128)(2,1)}, bf16[128,2048]{1,0:T(8,128)(2,1)S(1)}, u32[]{:S(2)}, u32[]{:S(2)}) %collective-permute-start.82) | collective-permute-done | bytes 524320 | tf_op jit(solution)/shard_map/ppermute | solution.py:365
  701.2 5.9 collective-permute-done.80
  715.5 9.6 %collective-permute-done.84 = bf16[128,2048]{1,0:T(8,128)(2,1)S(1)} collective-permute-done((bf16[128,2048]{1,0:T(8,128)(2,1)S(1)}, bf16[128,2048]{1,0:T(8,128)(2,1)S(1)}, u32[]{:S(2)}, u32[]{:S(2)}) %collective-permute-start.84) | collective-permute-done | bytes 524320 | tf_op jit(solution)/shard_map/ppermute | solution.py:361
  726.7 9.7 %collective-permute-done.85 = bf16[128,2048]{1,0:T(8,128)(2,1)S(1)} collective-permute-done((bf16[128,2048]{1,0:T(8,128)(2,1)S(1)}, bf16[128,2048]{1,0:T(8,128)(2,1)S(1)}, u32[]{:S(2)}, u32[]{:S(2)}) %collective-permute-start.85) | collective-permute-done | bytes 524320 | tf_op jit(solution)/shard_map/ppermute | solution.py:361
  738.0 9.7 %collective-permute-done.86 = bf16[128,2048]{1,0:T(8,128)(2,1)S(1)} collective-permute-done((bf16[128,2048]{1,0:T(8,128)(2,1)S(1)}, bf16[128,2048]{1,0:T(8,128)(2,1)S(1)}, u32[]{:S(2)}, u32[]{:S(2)}) %collective-permute-start.86) | collective-permute-done | bytes 524320 | tf_op jit(solution)/shard_map/ppermute | solution.py:361
  749.3 9.6 %collective-permute-done.99 = bf16[128,2048]{1,0:T(8,128)(2,1)S(1)} collective-permute-done((bf16[128,2048]{1,0:T(8,128)(2,1)S(1)}, bf16[128,2048]{1,0:T(8,128)(2,1)S(1)}, u32[]{:S(2)}, u32[]{:S(2)}) %collective-permute-start.99) | collective-permute-done | bytes 524320 | tf_op jit(solution)/shard_map/ppermute | solution.py:361
  760.7 9.4 %collective-permute-done.101 = bf16[128,2048]{1,0:T(8,128)(2,1)S(1)} collective-permute-done((bf16[128,2048]{1,0:T(8,128)(2,1)S(1)}, bf16[128,2048]{1,0:T(8,128)(2,1)S(1)}, u32[]{:S(2)}, u32[]{:S(2)}) %collective-permute-start.101) | collective-permute-done | bytes 524320 | tf_op jit(solution)/shard_map/ppermute | solution.py:361
  774.4 5.9 collective-permute-done.103
  785.7 5.3 copy.43
  794.9 10.5 %collective-permute-done.88 = bf16[128,2048]{1,0:T(8,128)(2,1)S(1)} collective-permute-done((bf16[128,2048]{1,0:T(8,128)(2,1)S(1)}, bf16[128,2048]{1,0:T(8,128)(2,1)S(1)}, u32[]{:S(2)}, u32[]{:S(2)}) %collective-permute-start.88) | collective-permute-done | bytes 524320 | tf_op jit(solution)/shard_map/ppermute | solution.py:365
  819.8 6.7 collective-permute-done.105
  826.5 19.9 %collective-permute-start.106 = (bf16[2048,64]{0,1:T(8,128)(2,1)S(1)}, bf16[2048,64]{0,1:T(8,128)(2,1)S(1)}, u32[]{:S(2)}, u32[]{:S(2)}) collective-permute-start(bf16[2048,64]{0,1:T(8,128)(2,1)S(1)} %add_convert_fusion.4), channel_id=1, source_target_pairs={{0,0},{1,1},{2,2},{3,3},{4,16},{5,17},{6,18},{7,19},{8,8},{9,9},{1... | collective-permute-start | bytes 786440 | tf_op jit(solution)/shard_map/ppermute | solution.py:620
  847.8 10.4 %collective-permute-done.106 = bf16[2048,64]{0,1:T(8,128)(2,1)S(1)} collective-permute-done((bf16[2048,64]{0,1:T(8,128)(2,1)S(1)}, bf16[2048,64]{0,1:T(8,128)(2,1)S(1)}, u32[]{:S(2)}, u32[]{:S(2)}) %collective-permute-start.106) | collective-permute-done | bytes 262176 | tf_op jit(solution)/shard_map/ppermute | solution.py:620
  (550 shorter events, 321.8 us)
Async XLA Ops:
  10.0 45.5 %collective-permute-start.8 = (bf16[128,2048]{1,0:T(8,128)(2,1)}, bf16[128,2048]{1,0:T(8,128)(2,1)}, u32[]{:S(2)}, u32[]{:S(2)}) collective-permute-start(bf16[128,2048]{1,0:T(8,128)(2,1)} %get-tuple-element.165), channel_id=1, source_target_pairs={{0,4},{2,6},{4,0},{6,2},{1,5},{3,7},{5,1},{7,3},{8,12},{10,14},{12... | collective-permute-start | bytes 1572872 | tf_op jit(solution)/shard_map/ppermute | solution.py:365
  24.2 34.7 %collective-permute-start.3 = (bf16[128,2048]{1,0:T(8,128)(2,1)}, bf16[128,2048]{1,0:T(8,128)(2,1)}, u32[]{:S(2)}, u32[]{:S(2)}) collective-permute-start(bf16[128,2048]{1,0:T(8,128)(2,1)} %collective-permute-done.2), channel_id=1, source_target_pairs={{0,16},{16,0},{1,17},{17,1},{2,18},{18,2},{3,19},{19,3},{4,20},{20... | collective-permute-start | bytes 1572872 | tf_op jit(solution)/shard_map/ppermute | solution.py:361
  26.4 57.0 %collective-permute-start.14 = (bf16[512,1024]{1,0:T(8,128)(2,1)}, bf16[512,1024]{1,0:T(8,128)(2,1)S(1)}, u32[]{:S(2)}, u32[]{:S(2)}) collective-permute-start(bf16[512,1024]{1,0:T(8,128)(2,1)} %constant_dynamic-slice_fusion.16), channel_id=1, source_target_pairs={{0,16},{16,0},{1,17},{17,1},{2,18},{18,2},{3,19},{19,3},{4,20},{20... | collective-permute-start | bytes 3145736 | tf_op jit(solution)/shard_map/ppermute | solution.py:361
  34.5 38.5 %collective-permute-start.6 = (bf16[128,2048]{1,0:T(8,128)(2,1)}, bf16[128,2048]{1,0:T(8,128)(2,1)S(1)}, u32[]{:S(2)}, u32[]{:S(2)}) collective-permute-start(bf16[128,2048]{1,0:T(8,128)(2,1)} %collective-permute-done.5), channel_id=1, source_target_pairs={{0,16},{16,0},{1,17},{17,1},{2,18},{18,2},{3,19},{19,3},{4,20},{20... | collective-permute-start | bytes 1572872 | tf_op jit(solution)/shard_map/ppermute | solution.py:361
  37.3 48.2 %collective-permute-start.1 = (bf16[256,2048]{1,0:T(8,128)(2,1)S(1)}, bf16[256,2048]{1,0:T(8,128)(2,1)S(1)}, u32[]{:S(2)}, u32[]{:S(2)}) collective-permute-start(bf16[256,2048]{1,0:T(8,128)(2,1)S(1)} %pad_maximum_fusion.2), channel_id=1, source_target_pairs={{0,1},{1,0},{2,3},{3,2},{4,5},{5,4},{6,7},{7,6},{8,9},{9,8},{10,11... | collective-permute-start | bytes 3145736 | tf_op jit(solution)/shard_map/ppermute | solution.py:361
  59.0 39.3 %collective-permute-start.11 = (bf16[384,2048]{1,0:T(8,128)(2,1)S(1)}, bf16[384,2048]{1,0:T(8,128)(2,1)S(1)}, u32[]{:S(2)}, u32[]{:S(2)}) collective-permute-start(bf16[384,2048]{1,0:T(8,128)(2,1)S(1)} %bitcast.163), channel_id=1, source_target_pairs={{0,8},{10,2},{4,12},{14,6},{1,9},{11,3},{5,13},{15,7},{16,24},{26,... | collective-permute-start | bytes 4718600 | tf_op jit(solution)/shard_map/ppermute | solution.py:642
  85.4 55.3 %collective-permute-start.15 = (bf16[1024,1024]{1,0:T(8,128)(2,1)}, bf16[1024,1024]{1,0:T(8,128)(2,1)}, u32[]{:S(2)}, u32[]{:S(2)}) collective-permute-start(bf16[1024,1024]{1,0:T(8,128)(2,1)} %pad_maximum_fusion.1), channel_id=1, source_target_pairs={{0,8},{8,0},{1,9},{9,1},{2,10},{10,2},{3,11},{11,3},{4,12},{12,4},... | collective-permute-start | bytes 6291464 | tf_op jit(solution)/shard_map/ppermute | solution.py:361
  145.4 48.1 %collective-permute-start.19 = (bf16[2048,1024]{1,0:T(8,128)(2,1)}, bf16[2048,1024]{1,0:T(8,128)(2,1)}, u32[]{:S(2)}, u32[]{:S(2)}) collective-permute-start(bf16[2048,1024]{1,0:T(8,128)(2,1)} %pad_maximum_fusion), channel_id=1, source_target_pairs={{0,1},{1,0},{2,3},{3,2},{4,5},{5,4},{6,7},{7,6},{8,9},{9,8},{10,11... | collective-permute-start | bytes 12582920 | tf_op jit(solution)/shard_map/ppermute | solution.py:361
  155.4 53.9 %collective-permute-start.21 = (bf16[128,2048]{1,0:T(8,128)(2,1)S(1)}, bf16[128,2048]{1,0:T(8,128)(2,1)}, u32[]{:S(2)}, u32[]{:S(2)}) collective-permute-start(bf16[128,2048]{1,0:T(8,128)(2,1)S(1)} %bitcast.164), channel_id=1, source_target_pairs={{0,2},{2,0},{4,6},{6,4},{1,3},{3,1},{5,7},{7,5},{8,10},{10,8},{12,... | collective-permute-start | bytes 1572872 | tf_op jit(solution)/shard_map/ppermute | solution.py:365
  160.8 28.6 %collective-permute-start.16 = (bf16[2,2,128,128]{3,2,0,1:T(8,128)(2,1)S(1)}, bf16[2,2,128,128]{3,2,0,1:T(8,128)(2,1)S(1)}, u32[]{:S(2)}, u32[]{:S(2)}) collective-permute-start(bf16[2,2,128,128]{3,2,0,1:T(8,128)(2,1)S(1)} %get-tuple-element.224), channel_id=1, source_target_pairs={{0,2},{2,0},{4,6},{6,4},{1,3},{3,1},{5,7},{7,5},{8,10},{10,8},{12,... | collective-permute-start | bytes 393224 | tf_op jit(solution)/shard_map/ppermute | solution.py:365
  170.5 41.1 %collective-permute-start.22 = (bf16[128,2048]{1,0:T(8,128)(2,1)S(1)}, bf16[128,2048]{1,0:T(8,128)(2,1)}, u32[]{:S(2)}, u32[]{:S(2)}) collective-permute-start(bf16[128,2048]{1,0:T(8,128)(2,1)S(1)} %bitcast.166), channel_id=1, source_target_pairs={{0,6},{2,4},{4,2},{6,0},{1,7},{3,5},{5,3},{7,1},{8,14},{10,12},{12... | collective-permute-start | bytes 1572872 | tf_op jit(solution)/shard_map/ppermute | solution.py:365
  174.8 44.9 %collective-permute-start.23 = (bf16[128,2048]{1,0:T(8,128)(2,1)S(1)}, bf16[128,2048]{1,0:T(8,128)(2,1)}, u32[]{:S(2)}, u32[]{:S(2)}) collective-permute-start(bf16[128,2048]{1,0:T(8,128)(2,1)S(1)} %bitcast.167), channel_id=1, source_target_pairs={{0,4},{2,6},{4,0},{6,2},{1,5},{3,7},{5,1},{7,3},{8,12},{10,14},{12... | collective-permute-start | bytes 1572872 | tf_op jit(solution)/shard_map/ppermute | solution.py:365
  189.4 49.4 %collective-permute-start.25 = (bf16[512,2048]{1,0:T(8,128)(2,1)}, bf16[512,2048]{1,0:T(8,128)(2,1)}, u32[]{:S(2)}, u32[]{:S(2)}) collective-permute-start(bf16[512,2048]{1,0:T(8,128)(2,1)} %bitcast.8), channel_id=1, source_target_pairs={{0,16},{2,18},{20,4},{22,6},{1,17},{3,19},{21,5},{23,7},{8,24},{10... | collective-permute-start | bytes 6291464 | tf_op jit(solution)/shard_map/ppermute | solution.py:666
  239.7 32.1 %collective-permute-start.30 = (bf16[128,2048]{1,0:T(8,128)(2,1)S(1)}, bf16[128,2048]{1,0:T(8,128)(2,1)S(1)}, u32[]{:S(2)}, u32[]{:S(2)}) collective-permute-start(bf16[128,2048]{1,0:T(8,128)(2,1)S(1)} %multiply_convert_fusion.12), channel_id=1, source_target_pairs={{0,6},{2,4},{4,2},{6,0},{1,7},{3,5},{5,3},{7,1},{8,14},{10,12},{12... | collective-permute-start | bytes 1572872 | tf_op jit(solution)/shard_map/ppermute | solution.py:365
  271.7 28.8 %collective-permute-start.29 = (bf16[128,2048]{1,0:T(8,128)(2,1)S(1)}, bf16[128,2048]{1,0:T(8,128)(2,1)S(1)}, u32[]{:S(2)}, u32[]{:S(2)}) collective-permute-start(bf16[128,2048]{1,0:T(8,128)(2,1)S(1)} %multiply_convert_fusion.12), channel_id=1, source_target_pairs={{0,4},{2,6},{4,0},{6,2},{1,5},{3,7},{5,1},{7,3},{8,12},{10,14},{12... | collective-permute-start | bytes 1572872 | tf_op jit(solution)/shard_map/ppermute | solution.py:365
  278.6 71.5 %collective-permute-start.27 = (bf16[512,2048]{1,0:T(8,128)(2,1)S(1)}, bf16[512,2048]{1,0:T(8,128)(2,1)S(1)}, u32[]{:S(2)}, u32[]{:S(2)}) collective-permute-start(bf16[512,2048]{1,0:T(8,128)(2,1)S(1)} %bitcast.161), channel_id=1, source_target_pairs={{0,16},{2,18},{20,4},{22,6},{1,17},{3,19},{21,5},{23,7},{8,24},{10... | collective-permute-start | bytes 6291464 | tf_op jit(solution)/shard_map/ppermute | solution.py:700
  289.3 60.2 %collective-permute-start.28 = (bf16[1024,512]{1,0:T(8,128)(2,1)S(1)}, bf16[1024,512]{1,0:T(8,128)(2,1)S(1)}, u32[]{:S(2)}, u32[]{:S(2)}) collective-permute-start(bf16[1024,512]{1,0:T(8,128)(2,1)S(1)} %pad_maximum_fusion.7), channel_id=1, source_target_pairs={{0,16},{16,0},{1,17},{17,1},{2,18},{18,2},{3,19},{19,3},{4,20},{20... | collective-permute-start | bytes 3145736 | tf_op jit(solution)/shard_map/ppermute | solution.py:361
  300.6 59.6 %collective-permute-start.40 = (bf16[256,2048]{1,0:T(8,128)(2,1)S(1)}, bf16[256,2048]{1,0:T(8,128)(2,1)S(1)}, u32[]{:S(2)}, u32[]{:S(2)}) collective-permute-start(bf16[256,2048]{1,0:T(8,128)(2,1)S(1)} %pad_maximum_fusion.10), channel_id=1, source_target_pairs={{0,1},{1,0},{2,3},{3,2},{4,5},{5,4},{6,7},{7,6},{8,9},{9,8},{10,11... | collective-permute-start | bytes 3145736 | tf_op jit(solution)/shard_map/ppermute | solution.py:361
  305.3 70.6 %collective-permute-start.45 = (bf16[256,2048]{1,0:T(8,128)(2,1)S(1)}, bf16[256,2048]{1,0:T(8,128)(2,1)S(1)}, u32[]{:S(2)}, u32[]{:S(2)}) collective-permute-start(bf16[256,2048]{1,0:T(8,128)(2,1)S(1)} %pad_maximum_fusion.11), channel_id=1, source_target_pairs={{0,1},{1,0},{2,3},{3,2},{4,5},{5,4},{6,7},{7,6},{8,9},{9,8},{10,11... | collective-permute-start | bytes 3145736 | tf_op jit(solution)/shard_map/ppermute | solution.py:361
  315.1 68.6 %collective-permute-start.46 = (bf16[256,2048]{1,0:T(8,128)(2,1)S(1)}, bf16[256,2048]{1,0:T(8,128)(2,1)S(1)}, u32[]{:S(2)}, u32[]{:S(2)}) collective-permute-start(bf16[256,2048]{1,0:T(8,128)(2,1)S(1)} %pad_maximum_fusion.12), channel_id=1, source_target_pairs={{0,1},{1,0},{2,3},{3,2},{4,5},{5,4},{6,7},{7,6},{8,9},{9,8},{10,11... | collective-permute-start | bytes 3145736 | tf_op jit(solution)/shard_map/ppermute | solution.py:361
  349.5 33.0 %collective-permute-start.52 = (bf16[128,2048]{1,0:T(8,128)(2,1)S(1)}, bf16[128,2048]{1,0:T(8,128)(2,1)S(1)}, u32[]{:S(2)}, u32[]{:S(2)}) collective-permute-start(bf16[128,2048]{1,0:T(8,128)(2,1)S(1)} %collective-permute-done.29), channel_id=1, source_target_pairs={{0,8},{8,0},{1,9},{9,1},{2,10},{10,2},{3,11},{11,3},{4,12},{12,4},... | collective-permute-start | bytes 1572872 | tf_op jit(solution)/shard_map/ppermute | solution.py:361
  350.1 46.5 %collective-permute-start.51 = (bf16[256,2048]{1,0:T(8,128)(2,1)S(1)}, bf16[256,2048]{1,0:T(8,128)(2,1)S(1)}, u32[]{:S(2)}, u32[]{:S(2)}) collective-permute-start(bf16[256,2048]{1,0:T(8,128)(2,1)S(1)} %pad_maximum_fusion.13), channel_id=1, source_target_pairs={{0,1},{1,0},{2,3},{3,2},{4,5},{5,4},{6,7},{7,6},{8,9},{9,8},{10,11... | collective-permute-start | bytes 3145736 | tf_op jit(solution)/shard_map/ppermute | solution.py:361
  360.2 41.8 %collective-permute-start.36 = (bf16[256,2048]{1,0:T(8,128)(2,1)S(1)}, bf16[256,2048]{1,0:T(8,128)(2,1)S(1)}, u32[]{:S(2)}, u32[]{:S(2)}) collective-permute-start(bf16[256,2048]{1,0:T(8,128)(2,1)S(1)} %slice.523), channel_id=1, source_target_pairs={{0,1},{1,0},{2,3},{3,2},{4,5},{5,4},{6,7},{7,6},{8,9},{9,8},{10,11... | collective-permute-start | bytes 3145736 | tf_op jit(solution)/shard_map/ppermute | solution.py:361
  402.4 57.9 %collective-permute-start.37 = (bf16[128,2048]{1,0:T(8,128)(2,1)S(1)}, bf16[128,2048]{1,0:T(8,128)(2,1)S(1)}, u32[]{:S(2)}, u32[]{:S(2)}) collective-permute-start(bf16[128,2048]{1,0:T(8,128)(2,1)S(1)} %slice.535), channel_id=1, source_target_pairs={{0,8},{8,0},{1,9},{9,1},{2,10},{10,2},{3,11},{11,3},{4,12},{12,4},... | collective-permute-start | bytes 1572872 | tf_op jit(solution)/shard_map/ppermute | solution.py:361
  423.4 36.9 %collective-permute-start.43 = (bf16[128,2048]{1,0:T(8,128)(2,1)S(1)}, bf16[128,2048]{1,0:T(8,128)(2,1)S(1)}, u32[]{:S(2)}, u32[]{:S(2)}) collective-permute-start(bf16[128,2048]{1,0:T(8,128)(2,1)S(1)} %fusion.58), channel_id=1, source_target_pairs={{0,2},{2,0},{4,6},{6,4},{1,3},{3,1},{5,7},{7,5},{8,10},{10,8},{12,... | collective-permute-start | bytes 1572872 | tf_op jit(solution)/shard_map/ppermute | solution.py:365
  448.3 34.6 %collective-permute-start.56 = (bf16[128,2048]{1,0:T(8,128)(2,1)S(1)}, bf16[128,2048]{1,0:T(8,128)(2,1)S(1)}, u32[]{:S(2)}, u32[]{:S(2)}) collective-permute-start(bf16[128,2048]{1,0:T(8,128)(2,1)S(1)} %fusion.56), channel_id=1, source_target_pairs={{0,4},{2,6},{4,0},{6,2},{1,5},{3,7},{5,1},{7,3},{8,12},{10,14},{12... | collective-permute-start | bytes 1572872 | tf_op jit(solution)/shard_map/ppermute | solution.py:365
  508.0 77.0 %collective-permute-start.66 = (bf16[2,256,2048]{2,1,0:T(8,128)(2,1)S(1)}, bf16[2,256,2048]{2,1,0:T(8,128)(2,1)}, u32[]{:S(2)}, u32[]{:S(2)}) collective-permute-start(bf16[2,256,2048]{2,1,0:T(8,128)(2,1)S(1)} %fusion.3), channel_id=1, source_target_pairs={{0,16},{16,0},{1,17},{17,1},{2,18},{18,2},{3,19},{19,3},{4,20},{20... | collective-permute-start | bytes 6291464 | tf_op jit(solution)/shard_map/ppermute | solution.py:361
  508.4 55.3 %collective-permute-start.72 = (bf16[128,2048]{1,0:T(8,128)(2,1)S(1)}, bf16[128,2048]{1,0:T(8,128)(2,1)S(1)}, u32[]{:S(2)}, u32[]{:S(2)}) collective-permute-start(bf16[128,2048]{1,0:T(8,128)(2,1)S(1)} %slice.531), channel_id=1, source_target_pairs={{0,8},{8,0},{1,9},{9,1},{2,10},{10,2},{3,11},{11,3},{4,12},{12,4},... | collective-permute-start | bytes 1572872 | tf_op jit(solution)/shard_map/ppermute | solution.py:361
  516.7 45.6 %collective-permute-start.64 = (bf16[4,2,128,128]{3,2,0,1:T(8,128)(2,1)S(1)}, bf16[4,2,128,128]{3,2,0,1:T(8,128)(2,1)S(1)}, u32[]{:S(2)}, u32[]{:S(2)}) collective-permute-start(bf16[4,2,128,128]{3,2,0,1:T(8,128)(2,1)S(1)} %get-tuple-element.217), channel_id=1, source_target_pairs={{0,16},{16,0},{1,17},{17,1},{2,18},{18,2},{3,19},{19,3},{4,20},{20... | collective-permute-start | bytes 786440 | tf_op jit(solution)/shard_map/ppermute | solution.py:361
  526.9 58.2 %collective-permute-start.67 = (bf16[2048,256]{1,0:T(8,128)(2,1)S(1)}, bf16[2048,256]{1,0:T(8,128)(2,1)S(1)}, u32[]{:S(2)}, u32[]{:S(2)}) collective-permute-start(bf16[2048,256]{1,0:T(8,128)(2,1)S(1)} %constant_dynamic-slice_fusion.8), channel_id=1, source_target_pairs={{0,16},{16,0},{1,17},{17,1},{2,18},{18,2},{3,19},{19,3},{4,20},{20... | collective-permute-start | bytes 3145736 | tf_op jit(solution)/shard_map/ppermute | solution.py:361
  527.6 36.9 %collective-permute-start.73 = (bf16[128,2048]{1,0:T(8,128)(2,1)S(1)}, bf16[128,2048]{1,0:T(8,128)(2,1)S(1)}, u32[]{:S(2)}, u32[]{:S(2)}) collective-permute-start(bf16[128,2048]{1,0:T(8,128)(2,1)S(1)} %slice.530), channel_id=1, source_target_pairs={{0,8},{8,0},{1,9},{9,1},{2,10},{10,2},{3,11},{11,3},{4,12},{12,4},... | collective-permute-start | bytes 1572872 | tf_op jit(solution)/shard_map/ppermute | solution.py:361
  598.2 31.6 %collective-permute-start.68 = (bf16[256,2048]{1,0:T(8,128)(2,1)S(1)}, bf16[256,2048]{1,0:T(8,128)(2,1)S(1)}, u32[]{:S(2)}, u32[]{:S(2)}) collective-permute-start(bf16[256,2048]{1,0:T(8,128)(2,1)S(1)} %slice.519), channel_id=1, source_target_pairs={{0,1},{1,0},{2,3},{3,2},{4,5},{5,4},{6,7},{7,6},{8,9},{9,8},{10,11... | collective-permute-start | bytes 3145736 | tf_op jit(solution)/shard_map/ppermute | solution.py:361
  629.8 33.0 %collective-permute-start.78 = (bf16[128,2048]{1,0:T(8,128)(2,1)S(1)}, bf16[128,2048]{1,0:T(8,128)(2,1)S(1)}, u32[]{:S(2)}, u32[]{:S(2)}) collective-permute-start(bf16[128,2048]{1,0:T(8,128)(2,1)S(1)} %get-tuple-element.122), channel_id=1, source_target_pairs={{0,4},{2,6},{4,0},{6,2},{1,5},{3,7},{5,1},{7,3},{8,12},{10,14},{12... | collective-permute-start | bytes 1572872 | tf_op jit(solution)/shard_map/ppermute | solution.py:365
  632.5 49.3 %collective-permute-start.108 = (bf16[2048,256]{1,0:T(8,128)(2,1)S(1)}, bf16[2048,256]{1,0:T(8,128)(2,1)S(1)}, u32[]{:S(2)}, u32[]{:S(2)}) collective-permute-start(bf16[2048,256]{1,0:T(8,128)(2,1)S(1)} %add_convert_fusion.1), channel_id=1, source_target_pairs={{0,0},{1,1},{2,8},{3,9},{4,4},{5,5},{6,12},{7,13},{8,2},{9,3},{10,... | collective-permute-start | bytes 3145736 | tf_op jit(solution)/shard_map/ppermute | solution.py:620
  639.4 109.8 %collective-permute-start.87 = (bf16[3,64,2048]{2,1,0:T(8,128)(2,1)S(1)}, bf16[3,64,2048]{2,1,0:T(8,128)(2,1)S(1)}, u32[]{:S(2)}, u32[]{:S(2)}) collective-permute-start(bf16[3,64,2048]{2,1,0:T(8,128)(2,1)S(1)} %dynamic-slice_convert_fusion), channel_id=1, source_target_pairs={{0,8},{8,0},{1,9},{9,1},{2,10},{10,2},{3,11},{11,3},{4,12},{12,4},... | collective-permute-start | bytes 2359304 | tf_op jit(solution)/shard_map/ppermute | solution.py:361
  662.7 36.4 %collective-permute-start.82 = (bf16[128,2048]{1,0:T(8,128)(2,1)}, bf16[128,2048]{1,0:T(8,128)(2,1)S(1)}, u32[]{:S(2)}, u32[]{:S(2)}) collective-permute-start(bf16[128,2048]{1,0:T(8,128)(2,1)} %convert_add_fusion.9), channel_id=1, source_target_pairs={{0,4},{2,6},{4,0},{6,2},{1,5},{3,7},{5,1},{7,3},{8,12},{10,14},{12... | collective-permute-start | bytes 1572872 | tf_op jit(solution)/shard_map/ppermute | solution.py:365
  662.7 37.8 %collective-permute-start.81 = (bf16[128,2048]{1,0:T(8,128)(2,1)}, bf16[128,2048]{1,0:T(8,128)(2,1)S(1)}, u32[]{:S(2)}, u32[]{:S(2)}) collective-permute-start(bf16[128,2048]{1,0:T(8,128)(2,1)} %convert_add_fusion.10), channel_id=1, source_target_pairs={{0,6},{2,4},{4,2},{6,0},{1,7},{3,5},{5,3},{7,1},{8,14},{10,12},{12... | collective-permute-start | bytes 1572872 | tf_op jit(solution)/shard_map/ppermute | solution.py:365
  665.0 42.1 %collective-permute-start.80 = (bf16[128,2048]{1,0:T(8,128)(2,1)}, bf16[128,2048]{1,0:T(8,128)(2,1)S(1)}, u32[]{:S(2)}, u32[]{:S(2)}) collective-permute-start(bf16[128,2048]{1,0:T(8,128)(2,1)} %convert_add_fusion.11), channel_id=1, source_target_pairs={{0,2},{2,0},{4,6},{6,4},{1,3},{3,1},{5,7},{7,5},{8,10},{10,8},{12,... | collective-permute-start | bytes 1572872 | tf_op jit(solution)/shard_map/ppermute | solution.py:365
  681.8 99.4 %collective-permute-start.107 = (bf16[2,256,2048]{2,1,0:T(8,128)(2,1)S(1)}, bf16[2,256,2048]{2,1,0:T(8,128)(2,1)S(1)}, u32[]{:S(2)}, u32[]{:S(2)}) collective-permute-start(bf16[2,256,2048]{2,1,0:T(8,128)(2,1)S(1)} %add_convert_fusion), channel_id=1, source_target_pairs={{0,0},{1,1},{2,8},{3,9},{4,4},{5,5},{6,12},{7,13},{8,2},{9,3},{10,... | collective-permute-start | bytes 6291464 | tf_op jit(solution)/shard_map/ppermute | solution.py:620
  707.1 29.3 %collective-permute-start.85 = (bf16[128,2048]{1,0:T(8,128)(2,1)S(1)}, bf16[128,2048]{1,0:T(8,128)(2,1)S(1)}, u32[]{:S(2)}, u32[]{:S(2)}) collective-permute-start(bf16[128,2048]{1,0:T(8,128)(2,1)S(1)} %slice.525), channel_id=1, source_target_pairs={{0,16},{16,0},{1,17},{17,1},{2,18},{18,2},{3,19},{19,3},{4,20},{20... | collective-permute-start | bytes 1572872 | tf_op jit(solution)/shard_map/ppermute | solution.py:361
  713.9 33.7 %collective-permute-start.86 = (bf16[128,2048]{1,0:T(8,128)(2,1)S(1)}, bf16[128,2048]{1,0:T(8,128)(2,1)S(1)}, u32[]{:S(2)}, u32[]{:S(2)}) collective-permute-start(bf16[128,2048]{1,0:T(8,128)(2,1)S(1)} %slice.524), channel_id=1, source_target_pairs={{0,16},{16,0},{1,17},{17,1},{2,18},{18,2},{3,19},{19,3},{4,20},{20... | collective-permute-start | bytes 1572872 | tf_op jit(solution)/shard_map/ppermute | solution.py:361
  725.2 33.7 %collective-permute-start.99 = (bf16[128,2048]{1,0:T(8,128)(2,1)S(1)}, bf16[128,2048]{1,0:T(8,128)(2,1)S(1)}, u32[]{:S(2)}, u32[]{:S(2)}) collective-permute-start(bf16[128,2048]{1,0:T(8,128)(2,1)S(1)} %collective-permute-done.76), channel_id=1, source_target_pairs={{0,16},{16,0},{1,17},{17,1},{2,18},{18,2},{3,19},{19,3},{4,20},{20... | collective-permute-start | bytes 1572872 | tf_op jit(solution)/shard_map/ppermute | solution.py:361
  736.4 33.7 %collective-permute-start.101 = (bf16[128,2048]{1,0:T(8,128)(2,1)S(1)}, bf16[128,2048]{1,0:T(8,128)(2,1)S(1)}, u32[]{:S(2)}, u32[]{:S(2)}) collective-permute-start(bf16[128,2048]{1,0:T(8,128)(2,1)S(1)} %collective-permute-done.77), channel_id=1, source_target_pairs={{0,16},{16,0},{1,17},{17,1},{2,18},{18,2},{3,19},{19,3},{4,20},{20... | collective-permute-start | bytes 1572872 | tf_op jit(solution)/shard_map/ppermute | solution.py:361
  747.6 32.7 %collective-permute-start.103 = (bf16[128,2048]{1,0:T(8,128)(2,1)S(1)}, bf16[128,2048]{1,0:T(8,128)(2,1)S(1)}, u32[]{:S(2)}, u32[]{:S(2)}) collective-permute-start(bf16[128,2048]{1,0:T(8,128)(2,1)S(1)} %collective-permute-done.78), channel_id=1, source_target_pairs={{0,16},{16,0},{1,17},{17,1},{2,18},{18,2},{3,19},{19,3},{4,20},{20... | collective-permute-start | bytes 1572872 | tf_op jit(solution)/shard_map/ppermute | solution.py:361
  749.2 41.7 %collective-permute-start.98 = (bf16[256,2048]{1,0:T(8,128)(2,1)S(1)}, bf16[256,2048]{1,0:T(8,128)(2,1)S(1)}, u32[]{:S(2)}, u32[]{:S(2)}) collective-permute-start(bf16[256,2048]{1,0:T(8,128)(2,1)S(1)} %pad_maximum_fusion.15), channel_id=1, source_target_pairs={{0,1},{1,0},{2,3},{3,2},{4,5},{5,4},{6,7},{7,6},{8,9},{9,8},{10,11... | collective-permute-start | bytes 3145736 | tf_op jit(solution)/shard_map/ppermute | solution.py:361
  758.9 35.5 %collective-permute-start.90 = (bf16[128,2048]{1,0:T(8,128)(2,1)S(1)}, bf16[128,2048]{1,0:T(8,128)(2,1)S(1)}, u32[]{:S(2)}, u32[]{:S(2)}) collective-permute-start(bf16[128,2048]{1,0:T(8,128)(2,1)S(1)} %convert_add_fusion.4), channel_id=1, source_target_pairs={{0,4},{2,6},{4,0},{6,2},{1,5},{3,7},{5,1},{7,3},{8,12},{10,14},{12... | collective-permute-start | bytes 1572872 | tf_op jit(solution)/shard_map/ppermute | solution.py:365
  781.2 65.3 %collective-permute-start.97 = (bf16[3,64,2048]{2,1,0:T(8,128)(2,1)S(1)}, bf16[3,64,2048]{2,1,0:T(8,128)(2,1)S(1)}, u32[]{:S(2)}, u32[]{:S(2)}) collective-permute-start(bf16[3,64,2048]{2,1,0:T(8,128)(2,1)S(1)} %add_convert_fusion.2), channel_id=1, source_target_pairs={{0,0},{1,1},{2,2},{3,3},{4,16},{5,17},{6,18},{7,19},{8,8},{9,9},{1... | collective-permute-start | bytes 2359304 | tf_op jit(solution)/shard_map/ppermute | solution.py:620
  826.5 31.6 %collective-permute-start.106 = (bf16[2048,64]{0,1:T(8,128)(2,1)S(1)}, bf16[2048,64]{0,1:T(8,128)(2,1)S(1)}, u32[]{:S(2)}, u32[]{:S(2)}) collective-permute-start(bf16[2048,64]{0,1:T(8,128)(2,1)S(1)} %add_convert_fusion.4), channel_id=1, source_target_pairs={{0,0},{1,1},{2,2},{3,3},{4,16},{5,17},{6,18},{7,19},{8,8},{9,9},{1... | collective-permute-start | bytes 786440 | tf_op jit(solution)/shard_map/ppermute | solution.py:620
  (129 other events, 2289.6 us)

commit v2 on v1

--- a/solution.py
+++ b/solution.py
@@ -530,7 +530,7 @@
         ),
         out_shape=[seq, seq, seq, wide, wide, jax.ShapeDtypeStruct((4, 2, 2, BLK, 128), BF)],
         compiler_params=pltpu.CompilerParams(vmem_limit_bytes=40 << 20),
-        cost_estimate=pl.CostEstimate(flops=4 * 10**9, bytes_accessed=8 << 20, transcendentals=4 << 20),
+        cost_estimate=pl.CostEstimate(flops=0, bytes_accessed=1 << 20, transcendentals=0),
         name="attend",
     )(place, proj, cosine, sine)
 
@@ -549,7 +549,7 @@
         ),
         out_shape=jax.ShapeDtypeStruct((4, 2, 2, BLK, 384), BF),
         compiler_params=pltpu.CompilerParams(vmem_limit_bytes=40 << 20),
-        cost_estimate=pl.CostEstimate(flops=10 * 10**9, bytes_accessed=8 << 20, transcendentals=4 << 20),
+        cost_estimate=pl.CostEstimate(flops=0, bytes_accessed=1 << 20, transcendentals=0),
         name="attend_back",
     )(place, *saved, grad_slots, cosine, sine)
 
@@ -565,11 +565,57 @@
     return pairs
 
 
-def assemble(pieces, shape):
-    total = jnp.zeros(shape, pieces[0][0].dtype)
-    for piece, row, col in pieces:
-        total = lax.dynamic_update_slice(total, piece, (row, col))
-    return total
+def join_kernel(place, half, other, out):
+    cols = half.shape[1]
+
+    @pl.when(place[3] == 0)
+    def _():
+        out[:, :cols] = half[...]
+        out[:, cols:] = other[...]
+
+    @pl.when(place[3] != 0)
+    def _():
+        out[:, :cols] = other[...]
+        out[:, cols:] = half[...]
+
+
+def join_out(place, half, other):
+    rows, cols = half.shape[0] // 4, half.shape[1]
+    block = pl.BlockSpec((rows, cols), lambda i, place: (i, 0))
+    return pl.pallas_call(
+        join_kernel,
+        grid_spec=pltpu.PrefetchScalarGridSpec(
+            num_scalar_prefetch=1,
+            grid=(4,),
+            in_specs=[block, block],
+            out_specs=pl.BlockSpec(
+                (rows, 2 * cols), lambda i, place: (place[2] ^ (((i & 1) << 1) | (i >> 1)), 0)
+            ),
+        ),
+        out_shape=jax.ShapeDtypeStruct((4 * rows, 2 * cols), BF),
+        cost_estimate=pl.CostEstimate(flops=0, bytes_accessed=1 << 20, transcendentals=0),
+        name="join_out",
+    )(place, half, other)
+
+
+def order_kernel(place, block, out):
+    out[...] = block[...]
+
+
+def order_rows(place, value):
+    rows, cols = value.shape[0] // 4, value.shape[1]
+    return pl.pallas_call(
+        order_kernel,
+        grid_spec=pltpu.PrefetchScalarGridSpec(
+            num_scalar_prefetch=1,
+            grid=(4,),
+            in_specs=[pl.BlockSpec((rows, cols), lambda i, place: (i, 0))],
+            out_specs=pl.BlockSpec((rows, cols), lambda i, place: (place[2] ^ i, 0)),
+        ),
+        out_shape=jax.ShapeDtypeStruct(value.shape, BF),
+        cost_estimate=pl.CostEstimate(flops=0, bytes_accessed=1 << 20, transcendentals=0),
+        name="order_rows",
+    )(place, value)
 
 
 def slot_of(rel):
@@ -640,14 +686,10 @@
     hops = [normed_one] + [hop(normed_one, j) for j in ORDER[1:]]
     others = [swap(normed_one, "y")]
     qkv_moved = lax.ppermute(qkv_sent, ("x", "z"), x_pairs)
-    rows, cols = w_out.shape[0], width // 2
+    cols = width // 2
     out_own = lax.dynamic_slice_in_dim(w_out, c * cols, cols, 1)
-    others[0], out_own = tick(others[0], out_own)
-    out_y = swap(out_own, "y")
-    for held in hops[1:]:
-        others.append(swap(held, "y"))
-    out_pair, _ = tick(jnp.concatenate([out_own, out_y], axis=0), hops[3])
-    out_x = swap(out_pair, "x")
+    hops[3], qkv_moved = tick(hops[3], qkv_moved)
+    others += [swap(held, "y") for held in hops[1:]]
     normed_all = jnp.concatenate([with_partner(*item) for item in zip(hops, others)], axis=0)
     heads_qkv = jnp.where(x == z0, qkv_sent, qkv_moved)
 
@@ -658,127 +700,173 @@
         )
 
     gu_sent = [lax.dynamic_slice_in_dim(w_gate_up, (4 * c + 2 * j + z0) * units, units, 0) for j in range(2)]
-    gu_sent = jnp.transpose(jnp.stack(gu_sent), (2, 0, 1, 3)).reshape(2, 2 * units, width)
+    gate_sent = [jnp.reshape(item[:, 0], (units, width)) for item in gu_sent]
+    up_sent = [jnp.reshape(item[:, 1], (units, width)) for item in gu_sent]
     down_own, down_sent = columns(x), columns(1 - x)
 
-    normed_all, cot, gate_sent = tick(normed_all, cotangent[0], gu_sent[0])
-    cot_hops = [cot] + [hop(cot, j) for j in ORDER[1:]]
-    gate_moved = lax.ppermute(gate_sent, ("y", "z"), y_pairs)
+    def to_y(value):
+        return lax.ppermute(value, ("y", "z"), y_pairs)
 
     cos_half, sin_half = rope_tables(jnp.arange(length, dtype=jnp.int32), HD // 2)
     cosine, sine = jnp.tile(cos_half, (1, 4)), jnp.tile(sin_half, (1, 4))
-    place = jnp.stack([part, 8 * y + 4 * z0 + 2 * c + z1]).astype(jnp.int32)
+    place = jnp.stack([part, 8 * y + 4 * z0 + 2 * c + z1, group, c]).astype(jnp.int32)
+
+    *firsts, cot, out_own, down_sent, down_own = tick(
+        normed_all, heads_qkv, *gate_sent, *up_sent, cosine, sine, place, cotangent[0], out_own, down_sent, down_own
+    )
+    normed_all, heads_qkv, gate_sent, up_sent = firsts[0], firsts[1], firsts[2:4], firsts[4:6]
+    cosine, sine, place = firsts[6:]
+    cot_hops = [cot, hop(cot, 1), hop(cot, 3), None]
+    cot_others = [swap(cot, "x")]
+    down_x = swap(down_sent, "x")
+    out_y = swap(out_own, "y")
+
     proj = dot(normed_all, heads_qkv, 1, 1)
     *saved, low_slots = attend(place, proj.reshape(4, 2, 2, BLK, 384), cosine, sine)
-    pieces = send_plane(send_core(low_slots), "y")
-    pieces, out_x, down_sent, cot = tick(pieces, out_x, down_sent, cot)
+    pieces = send_core(low_slots)
+    pieces, out_y, cot_hops[1], cot_others[0], down_x = tick(pieces, out_y, cot_hops[1], cot_others[0], down_x)
+    out_pair = jnp.concatenate([out_own, out_y], axis=0)
+    out_x = swap(out_pair, "x")
+    down_pair = jnp.concatenate([down_own, down_x], axis=0)
+    down_y = swap(down_pair, "y")
+    pieces = send_plane(pieces, "y")
+    pieces, cot_hops[2] = tick(pieces, cot_hops[2])
     pieces = send_hops(pieces)
+    pieces, out_x, down_y, gate_sent[0], cot = tick(pieces, out_x, down_y, gate_sent[0], cot)
+    cot_hops[3] = hop(cot, 2)
+    gate_moved = [to_y(gate_sent[0])]
     out_half = jnp.concatenate([out_pair, out_x], axis=0)
     out_c = swap(out_half, "c")
-    cot_others = [swap(cot, "x")]
-    down_x = swap(down_sent, "x")
-    out_full = assemble(
-        [
-            (block[i * rows : (i + 1) * rows], (group ^ flip) * rows, side * cols)
-            for block, side in ((out_half, c), (out_c, 1 - c))
-            for i, flip in enumerate((0, 2, 1, 3))
-        ],
-        (width, width),
-    )
     attended = reorder(to_heads_kernel, place, pieces.reshape(16, BLK, 128), (BLK, width))
+    out_full = join_out(place, out_half, out_c)
+    attended, out_full, cot_hops[1], cot_hops[2] = tick(attended, out_full, cot_hops[1], cot_hops[2])
+    cot_others += [swap(item, "x") for item in cot_hops[1:3]]
     residual = inputs + dot(attended, out_full, 1, 1)
     scale_two = rms_scale(residual)
     normed_two = (residual * scale_two * gain_two).astype(BF)
 
-    normed_two, *moved = tick(
-        normed_two, cot_others[0], *cot_hops[1:], down_x, gate_moved, gu_sent[1], down_own
-    )
-    cot_others[0], cot_hops[1:], (down_x, gate_moved, up_sent, down_own) = moved[0], moved[1:4], moved[4:]
+    normed_two, cot_hops[3], gate_moved[0], gate_sent[1] = tick(normed_two, cot_hops[3], gate_moved[0], gate_sent[1])
+    gate_moved.append(to_y(gate_sent[1]))
     hops = [normed_two] + [hop(normed_two, j) for j in ORDER[1:]]
     others = [swap(normed_two, "x")]
-    cot_others.append(swap(cot_hops[1], "x"))
-    up_moved = lax.ppermute(up_sent, ("y", "z"), y_pairs)
-    down_pair = jnp.concatenate([down_own, down_x], axis=0)
-    down_y = swap(down_pair, "y")
-    for i in (1, 2, 3):
-        hops[i], others[i - 1] = tick(hops[i], others[i - 1])
-        others.append(swap(hops[i], "x"))
-        if i < 3:
-            cot_hops[i + 1], _ = tick(cot_hops[i + 1], hops[i])
-            cot_others.append(swap(cot_hops[i + 1], "x"))
-    gate_moved, up_moved, down_y, _ = tick(gate_moved, up_moved, down_y, hops[3])
-    w_gate = jnp.where(y == z1, gu_sent[0], gate_moved)
-    w_up = jnp.where(y == z1, up_sent, up_moved)
-    down_half = jnp.concatenate([down_pair, down_y], axis=0)
-    rows = w_down.shape[0]
-    down = assemble(
-        [(down_half[i * rows : (i + 1) * rows], (group ^ i) * rows, 0) for i in range(4)],
-        (width, 2 * units),
-    )
+    hops[1], gate_moved[1], up_sent[0], cot_others[1] = tick(hops[1], gate_moved[1], up_sent[0], cot_others[1])
+    up_moved = [to_y(up_sent[0])]
+    others.append(swap(hops[1], "x"))
+    hops[2], up_moved[0], up_sent[1], cot_others[2], cot_hops[3] = tick(
+        hops[2], up_moved[0], up_sent[1], cot_others[2], cot_hops[3]
+    )
+    up_moved.append(to_y(up_sent[1]))
+    others.append(swap(hops[2], "x"))
+    cot_others.append(swap(cot_hops[3], "x"))
+    others.append(swap(hops[3], "x"))
+    w_gate, w_up = [
+        jnp.concatenate([jnp.where(y == z1, own, moved) for own, moved in zip(held, arrived)], axis=0)
+        for held, arrived in ((gate_sent, gate_moved), (up_sent, up_moved))
+    ]
+    down = order_rows(place, jnp.concatenate([down_pair, down_y], axis=0))
     ff_chunks = [with_partner(*item) for item in zip(hops, others)]
     cot_chunks = [with_partner(*item) for item in zip(cot_hops, cot_others)]
 
-    hiddens, gate_grads, up_grads, back_parts, mlp_parts = [], [], [], [], []
-    for rows_in, rows_cot in zip(ff_chunks, cot_chunks):
-        gate, up = dot(rows_in, w_gate, 1, 1), dot(rows_in, w_up, 1, 1)
+    hiddens, gate_grads, up_grads, back_parts, mlp_parts = [[None] * 4 for _ in range(5)]
+    first, second, third, last = turns = (2, 3, 1, 0)
+    for i in turns:
+        if i == third:
+            ff_chunks[i], back_parts[first] = tick(ff_chunks[i], back_parts[first])
+            back_parts[first] = fold_plane(back_parts[first], "x")
+        if i == last:
+            ff_chunks[i], back_parts[second], back_parts[first] = tick(
+                ff_chunks[i], back_parts[second], back_parts[first]
+            )
+            back_parts[second] = fold_plane(back_parts[second], "x")
+        gate, up = dot(ff_chunks[i], w_gate, 1, 1), dot(ff_chunks[i], w_up, 1, 1)
         sigmoid_gate = jax.nn.sigmoid(gate)
         silu = gate * sigmoid_gate
         hidden = (silu * up).astype(BF)
-        grad_hidden = dot(rows_cot, down, 1, 0)
+        grad_hidden = dot(cot_chunks[i], down, 1, 0)
         grad_gate = (grad_hidden * up * sigmoid_gate * (1.0 + gate * (1.0 - sigmoid_gate))).astype(BF)
         grad_up = (grad_hidden * silu).astype(BF)
-        back_parts.append(fold_core(dot(grad_gate, w_gate, 1, 0) + dot(grad_up, w_up, 1, 0)))
-        mlp_parts.append(dot(hidden, down, 1, 1).astype(BF))
-        hiddens.append(hidden)
-        gate_grads.append(grad_gate)
-        up_grads.append(grad_up)
-    grad_normed_two = fold_hops([fold_plane(item, "x") for item in back_parts])
-
-    ff_in, cot_all = jnp.concatenate(ff_chunks, axis=0), jnp.concatenate(cot_chunks, axis=0)
-    gu_grad = jnp.stack(
-        [dot(jnp.concatenate(parts, axis=0), ff_in, 0, 0).astype(BF) for parts in (gate_grads, up_grads)]
-    )
-    gu_own, gu_other = split(gu_grad, 1, y)
-    down_grad = dot(cot_all, jnp.concatenate(hiddens, axis=0), 0, 0).astype(BF)
+        back_parts[i] = dot(grad_gate, w_gate, 1, 0) + dot(grad_up, w_up, 1, 0)
+        if i == last:
+            tied = tick(back_parts[i], *gate_grads[1:], *up_grads[1:], *hiddens[1:], grad_gate, grad_up, hidden)
+            back_parts[i], gate_grads[1:], up_grads[1:], hiddens[1:] = tied[0], tied[1:4], tied[4:7], tied[7:10]
+            grad_gate, grad_up, hidden = tied[10:]
+        back_parts[i] = fold_core(back_parts[i])
+        hiddens[i], gate_grads[i], up_grads[i] = hidden, grad_gate, grad_up
+
+    def over_chunks(left, right):
+        return sum(dot(left[i], right[i], 0, 0) for i in range(4)).astype(BF)
+
+    back_hops = [None] * 4
+
+    def send_back(i):
+        back_hops[i] = hop(back_parts[i].astype(BF), ORDER[i]).astype(F32)
+
+    send_back(first)
+    gate_grad = over_chunks(gate_grads, ff_chunks)
+    gate_grad, *up_grads, back_parts[third], back_parts[second] = tick(
+        gate_grad, *up_grads, back_parts[third], back_parts[second]
+    )
+    back_parts[third] = fold_plane(back_parts[third], "x")
+    send_back(second)
+    up_grad = over_chunks(up_grads, ff_chunks)
+    up_grad, *hiddens, back_parts[last], back_parts[third] = tick(up_grad, *hiddens, back_parts[last], back_parts[third])
+    back_parts[last] = fold_plane(back_parts[last], "x")
+    send_back(third)
+    gu_own, gu_other = split(jnp.stack([gate_grad, up_grad]), 1, y)
+    gu_other = swap(gu_other, "y")
+    mlp_parts = [dot(item, down, 1, 1).astype(BF) for item in hiddens]
+    mlp_parts = [fold_core(item) for item in mlp_parts]
+    down_grad = over_chunks(cot_chunks, hiddens)
     down_own, down_other = split(down_grad, 1, y)
-    gu_other, down_other = swap(gu_other, "y"), swap(down_other, "y")
-
-    grad_normed_two, *mlp_parts = tick(grad_normed_two, *mlp_parts)
-    mlp_parts = [fold_core(item) for item in mlp_parts]
+    back_parts[last], down_other, *mlp_parts = tick(back_parts[last], down_other, *mlp_parts)
+    down_other = swap(down_other, "y")
+    mlp_parts = [fold_plane(item, "x") for item in mlp_parts]
+    back_parts[last], *back_hops[1:], mlp_parts[0], mlp_parts[1] = tick(
+        back_parts[last], *back_hops[1:], mlp_parts[0], mlp_parts[1]
+    )
+    grad_normed_two = back_parts[last] + back_hops[1] + back_hops[2] + back_hops[3]
+
     grad_norm_two, grad_gain_two = rms_back(grad_normed_two, residual, scale_two, gain_two)
     grad_residual = cotangent[0].astype(F32) + grad_norm_two
     grad_branch = grad_residual.astype(BF)
     grad_attended = dot(grad_branch, out_full, 1, 0).astype(BF)
     grad_slots = reorder(to_slots_kernel, place, grad_attended, (16, BLK, 128))
-    grad_slots, *mlp_parts = tick(grad_slots, *mlp_parts)
     pieces = send_hops(grad_slots.reshape(4, 2, 2, BLK, 128))
-    mlp_parts = [fold_plane(item, "x") for item in mlp_parts]
+    pieces, *mlp_parts = tick(pieces, *mlp_parts)
+    mlp_hops = [mlp_parts[0]] + [hop(item.astype(BF), j) for j, item in zip(ORDER[1:], mlp_parts[1:])]
     pieces = send_core(send_plane(pieces, "y"))
-    grad_branch, pieces, gu_other, down_other = tick(grad_branch, pieces, gu_other, down_other)
-    branch_hops = [grad_branch] + [hop(grad_branch, j) for j in ORDER[1:]]
-    branch_others = [swap(grad_branch, "y")]
     grad_proj = attend_back(place, saved, pieces, cosine, sine).reshape(16 * BLK, 384)
     back_parts = [fold_core(dot(grad_proj[j * quarter : (j + 1) * quarter], heads_qkv, 1, 0)) for j in range(4)]
-    back_parts = tick(*back_parts, *mlp_parts, *branch_hops[1:], branch_others[0])
-    mlp_parts, branch_hops[1:], branch_others = back_parts[4:8], back_parts[8:11], [back_parts[11]]
-    back_parts = [fold_plane(item, "y") for item in back_parts[:4]]
-    mlp_term = fold_hops(mlp_parts)
+    qkv_grad = dot(grad_proj, normed_all, 0, 0)
+    qkv_own, qkv_other = split(qkv_grad.reshape(3, 2 * HD, width), 1, x)
+    tied = tick(*back_parts, qkv_other.astype(BF), grad_branch, gu_other, down_other, *mlp_hops)
+    back_parts, (qkv_other, grad_branch, gu_other, down_other), mlp_hops = list(tied[:4]), tied[4:8], tied[8:]
+    qkv_other = swap(qkv_other, "x")
+    back_parts = [fold_plane(item, "y") for item in back_parts]
+    gu_moved = lax.ppermute((gu_own.astype(F32) + gu_other.astype(F32)).astype(BF), AXES, perm_of(ff_place))
+    down_moved = lax.ppermute((down_own.astype(F32) + down_other.astype(F32)).astype(BF), AXES, perm_of(ff_place))
+    branch_hops = [grad_branch] + [hop(grad_branch, j) for j in ORDER[1:]]
+    back_parts[first], branch_hops[1] = tick(back_parts[first], branch_hops[1])
+    send_back(first)
+    back_parts[second], branch_hops[2], qkv_other = tick(back_parts[second], branch_hops[2], qkv_other)
+    send_back(second)
+    qkv_moved = lax.ppermute((qkv_own + qkv_other.astype(F32)).astype(BF), AXES, perm_of(attn_place))
+    back_parts[third], branch_hops[3], down_moved = tick(back_parts[third], branch_hops[3], down_moved)
+    send_back(third)
+    branch_others = [swap(item, "y") for item in branch_hops]
+    branch_chunks = [with_partner(*item) for item in zip(branch_hops, branch_others)]
+    back_hops[3], gu_moved, qkv_grad, *mlp_hops = tick(back_hops[3], gu_moved, qkv_grad, *mlp_hops)
+    mlp_term = mlp_hops[0] + sum(item.astype(F32) for item in mlp_hops[1:])
     layer_out = (residual + mlp_term).astype(BF)
-    qkv_grad = dot(grad_proj, normed_all, 0, 0)
     gain_part = jnp.sum(qkv_grad * heads_qkv.astype(F32), axis=0) / gain_one
-    qkv_own, qkv_other = split(qkv_grad.reshape(3, 2 * HD, width), 1, x)
-    qkv_other = swap(qkv_other.astype(BF), "x")
-    back_parts = tick(*back_parts, mlp_term, qkv_other)
-    mlp_term, qkv_other, back_parts = back_parts[4], back_parts[5], back_parts[:4]
-    grad_normed_one = fold_hops(back_parts)
-    branch_others += [swap(item, "y") for item in branch_hops[1:]]
-    grad_qkv = jnp.transpose(move(qkv_own + qkv_other.astype(F32), attn_place), (1, 0, 2))
-    grad_gate_up = jnp.transpose(move(gu_own.astype(F32) + gu_other.astype(F32), ff_place), (1, 0, 2))
-    grad_down = move(down_own.astype(F32) + down_other.astype(F32), ff_place)
-    branch_all = jnp.concatenate([with_partner(*item) for item in zip(branch_hops, branch_others)], axis=0)
-    out_grad = dot(branch_all, low_slots.reshape(16 * BLK, 128), 0, 0)
+    low_chunks = low_slots.reshape(4, quarter, 128)
+    out_grad = sum(dot(item, low_chunks[i], 0, 0) for i, item in enumerate(branch_chunks))
     out_own, out_other = split(out_grad, 1, x)
     grad_out_proj = move(out_own + swap(out_other.astype(BF), "x").astype(F32), attn_place)
+    grad_normed_one = back_parts[last] + back_hops[1] + back_hops[2] + back_hops[3]
+    grad_qkv = jnp.transpose(qkv_moved.astype(F32), (1, 0, 2))
+    grad_gate_up = jnp.transpose(gu_moved.astype(F32), (1, 0, 2))
+    grad_down = down_moved.astype(F32)
 
     weighted = grad_normed_one * gain_one
     inner_mean = jnp.mean(weighted * inputs, axis=-1, keepdims=True)

time: 867 us -> 780 us (0.90)
  waiting for transfers between devices: 471 us -> 355 us
  starting transfers between devices: 112 us -> 153 us
  local copies, waits for them, and re-layouts: 105 us -> 74.4 us
  Pallas kernels: 19.3 us -> 31.8 us
  other arithmetic: 52.2 us -> 61.6 us
    ppermute x30, waiting for transfers between devices: 170 us -> 95.8 us  [hop(): return lax.ppermute(value, 'z', [(i, i ^ dist) for i in range(4)])]
    ppermute x30, starting transfers between devices: 31 us -> 68.2 us  [hop(): return lax.ppermute(value, 'z', [(i, i ^ dist) for i in range(4)])]
    ppermute x72, waiting for transfers between devices: 250 us -> 223 us  [swap(): return lax.ppermute(value, axis, PAIR)]
    ppermute x4 -> x1, starting transfers between devices: 30.8 us -> 5.71 us  [move(): return lax.ppermute(value.astype(BF), AXES, perm_of(target)).astype(F32)]
    dynamic_update_slice x12 -> x0, local copies, waits for them, and re-layouts: 18.7 us -> none  [assemble(): total = lax.dynamic_update_slice(total, piece, (row, col))]
    unnamed x180 -> x207, local copies, waits for them, and re-layouts: 53.3 us -> 35.1 us
    ppermute x72, starting transfers between devices: 45.1 us -> 62.6 us  [swap(): return lax.ppermute(value, axis, PAIR)]
    ppermute x4 -> x1, waiting for transfers between devices: 25.2 us -> 8.89 us  [move(): return lax.ppermute(value.astype(BF), AXES, perm_of(target)).astype(F32)]
  transfers between devices with their start and end apart: 109 -> 111, of which waited for: 47 -> 51; matrix products, arithmetic and copies ran while one was open for 27% -> 26% of each run, Pallas kernels for 1% -> 4%
where the time goes in v2:
time: 780 us; the launch traced here: 769 us
  waiting for transfers between devices  355 us (46%)
  starting transfers between devices  153 us (20%)
  matrix products  90.4 us (12%)
  local copies, waits for them, and re-layouts  74.4 us (10%)
  other arithmetic  61.6 us (8%)
  Pallas kernels  31.8 us (4%)
    ppermute x72, waiting for transfers between devices, swap(): return lax.ppermute(value, axis, PAIR)  223 us
    ppermute x30, waiting for transfers between devices, hop(): return lax.ppermute(value, 'z', [(i, i ^ dist) for i in range(4)])  95.8 us
    dot_general x48, matrix products, dot(): lax.dot_general(left, right, (((left_dim,), (right_dim,)), ((), ())), pre...  90.4 us
    ppermute x30, starting transfers between devices, hop(): return lax.ppermute(value, 'z', [(i, i ^ dist) for i in range(4)])  68.2 us
    ppermute x72, starting transfers between devices, swap(): return lax.ppermute(value, axis, PAIR)  62.6 us
    unnamed x207, local copies, waits for them, and re-layouts  35.1 us
    ppermute x4, waiting for transfers between devices, to_y(): return lax.ppermute(value, ('y', 'z'), y_pairs)  15.7 us
  transfers between devices with their start and end apart: 111, of which 51 were waited for; matrix products, arithmetic and copies ran while one was open for 26% of the time, Pallas kernels for 4%

profile of v2, /device:TPU:6, one launch (start us, length us, event | category | flops | bytes accessed | tf_op | source)
XLA Modules:
  0.0 769.0 jit_solution(11797229686939269191)
XLA Ops:
  14.2 8.9 %constant_dynamic-slice_fusion.16 = (bf16[256,1,2048]{2,1,0:T(2,128)(2,1)S(1)}, bf16[256,1,2048]{2,1,0:T(2,128)(2,1)S(1)}, bf16[256,1,2048]{2,1,0:T(2,128)(2,1)S(1)}, bf16[256,1,2048]{2,1,0:T(2,128)(2,1)S(1)}) fusion(bf16[2048,2,2048]{2,1,0:T(2,128)(2,1)} %param.13, s32[]{:T(128)S(6)} %select_n.115, s32[]{:T(128)S(6)} %add.488, s32[]{:T(128)S(6)} %select_n.114), kind=kLoop, calls=%fused_computation.247 | loop fusion | bytes 8388620 | tf_op jit(solution)/shard_map/slice | solution.py:704
  36.4 7.8 %collective-permute-done.2 = bf16[128,2048]{1,0:T(8,128)(2,1)} collective-permute-done((bf16[128,2048]{1,0:T(8,128)(2,1)}, bf16[128,2048]{1,0:T(8,128)(2,1)}, u32[]{:S(2)}, u32[]{:S(2)}) %collective-permute-start.2) | collective-permute-done | bytes 524320 | tf_op jit(solution)/shard_map/ppermute | solution.py:365
  48.7 9.2 %collective-permute-done.3 = bf16[128,2048]{1,0:T(8,128)(2,1)S(1)} collective-permute-done((bf16[128,2048]{1,0:T(8,128)(2,1)}, bf16[128,2048]{1,0:T(8,128)(2,1)S(1)}, u32[]{:S(2)}, u32[]{:S(2)}) %collective-permute-start.3) | collective-permute-done | bytes 524320 | tf_op jit(solution)/shard_map/ppermute | solution.py:361
  67.8 10.9 %collective-permute-done.10 = bf16[128,2048]{1,0:T(8,128)(2,1)S(1)} collective-permute-done((bf16[128,2048]{1,0:T(8,128)(2,1)}, bf16[128,2048]{1,0:T(8,128)(2,1)S(1)}, u32[]{:S(2)}, u32[]{:S(2)}) %collective-permute-start.10) | collective-permute-done | bytes 524320 | tf_op jit(solution)/shard_map/ppermute | solution.py:361
  92.3 18.7 %collective-permute-start.14 = (bf16[128,2048]{1,0:T(8,128)(2,1)}, bf16[128,2048]{1,0:T(8,128)(2,1)}, u32[]{:S(2)}, u32[]{:S(2)}) collective-permute-start(bf16[128,2048]{1,0:T(8,128)(2,1)} %bitcast.15), channel_id=1, source_target_pairs={{0,2},{2,0},{4,6},{6,4},{1,3},{3,1},{5,7},{7,5},{8,10},{10,8},{12,... | collective-permute-start | bytes 1572872 | tf_op jit(solution)/shard_map/ppermute | solution.py:365
  114.5 6.9 fusion.75
  121.5 5.2 attend.1
  128.4 10.5 %collective-permute-done.13 = bf16[512,1024]{1,0:T(8,128)(2,1)S(1)} collective-permute-done((bf16[512,1024]{1,0:T(8,128)(2,1)}, bf16[512,1024]{1,0:T(8,128)(2,1)S(1)}, u32[]{:S(2)}, u32[]{:S(2)}) %collective-permute-start.13) | collective-permute-done | bytes 1048608 | tf_op jit(solution)/shard_map/ppermute | solution.py:361
  146.4 5.9 collective-permute-done.17
  157.6 11.8 %collective-permute-start.19 = (bf16[2,2,128,128]{3,2,0,1:T(8,128)(2,1)S(1)}, bf16[2,2,128,128]{3,2,0,1:T(8,128)(2,1)S(1)}, u32[]{:S(2)}, u32[]{:S(2)}) collective-permute-start(bf16[2,2,128,128]{3,2,0,1:T(8,128)(2,1)S(1)} %get-tuple-element.323), channel_id=1, source_target_pairs={{0,2},{2,0},{4,6},{6,4},{1,3},{3,1},{5,7},{7,5},{8,10},{10,8},{12,... | collective-permute-start | bytes 393224 | tf_op jit(solution)/shard_map/ppermute | solution.py:365
  172.6 5.1 collective-permute-done.21
  179.6 6.0 collective-permute-done.22
  206.4 4.5 order_rows.1
  212.1 4.5 fusion.76
  216.6 8.0 %join_out.1 = bf16[2048,2048]{1,0:T(8,128)(2,1)} custom-call(s32[4]{0:T(128)} %copy-done.10, bf16[2048,1024]{1,0:T(8,128)(2,1)} %constant_dynamic-update-slice_fusion.12.half, bf16[2048,1024]{1,0:T(8,128)(2,1)} %collective-permute-done.24.other), custom_call_target="tpu_custom_call" | custom-call | bytes 1048576 | tf_op jit(solution)/shard_map/join_out/pallas_call | solution.py:585
  224.7 6.6 multiply_reduce_fusion.3
  231.5 6.5 collective-permute-done.27
  245.3 8.9 %collective-permute-done.28 = bf16[128,2048]{1,0:T(8,128)(2,1)S(1)} collective-permute-done((bf16[128,2048]{1,0:T(8,128)(2,1)S(1)}, bf16[128,2048]{1,0:T(8,128)(2,1)S(1)}, u32[]{:S(2)}, u32[]{:S(2)}) %collective-permute-start.28) | collective-permute-done | bytes 524320 | tf_op jit(solution)/shard_map/ppermute | solution.py:361
  257.3 8.6 %collective-permute-done.38 = bf16[128,2048]{1,0:T(8,128)(2,1)S(1)} collective-permute-done((bf16[128,2048]{1,0:T(8,128)(2,1)S(1)}, bf16[128,2048]{1,0:T(8,128)(2,1)S(1)}, u32[]{:S(2)}, u32[]{:S(2)}) %collective-permute-start.38) | collective-permute-done | bytes 524320 | tf_op jit(solution)/shard_map/ppermute | solution.py:365
  270.7 10.1 %collective-permute-done.39 = bf16[128,2048]{1,0:T(8,128)(2,1)S(1)} collective-permute-done((bf16[128,2048]{1,0:T(8,128)(2,1)S(1)}, bf16[128,2048]{1,0:T(8,128)(2,1)S(1)}, u32[]{:S(2)}, u32[]{:S(2)}) %collective-permute-start.39) | collective-permute-done | bytes 524320 | tf_op jit(solution)/shard_map/ppermute | solution.py:361
  281.6 10.5 %collective-permute-done.43 = bf16[128,2048]{1,0:T(8,128)(2,1)S(1)} collective-permute-done((bf16[128,2048]{1,0:T(8,128)(2,1)S(1)}, bf16[128,2048]{1,0:T(8,128)(2,1)S(1)}, u32[]{:S(2)}, u32[]{:S(2)}) %collective-permute-start.43) | collective-permute-done | bytes 524320 | tf_op jit(solution)/shard_map/ppermute | solution.py:361
  293.0 9.8 %collective-permute-done.35 = bf16[128,2048]{1,0:T(8,128)(2,1)S(1)} collective-permute-done((bf16[128,2048]{1,0:T(8,128)(2,1)S(1)}, bf16[128,2048]{1,0:T(8,128)(2,1)S(1)}, u32[]{:S(2)}, u32[]{:S(2)}) %collective-permute-start.35) | collective-permute-done | bytes 524320 | tf_op jit(solution)/shard_map/ppermute | solution.py:361
  313.9 3.9 collective-permute-done.36
  319.0 8.7 %collective-permute-done.46 = bf16[128,2048]{1,0:T(8,128)(2,1)S(1)} collective-permute-done((bf16[128,2048]{1,0:T(8,128)(2,1)S(1)}, bf16[128,2048]{1,0:T(8,128)(2,1)S(1)}, u32[]{:S(2)}, u32[]{:S(2)}) %collective-permute-start.46) | collective-permute-done | bytes 524320 | tf_op jit(solution)/shard_map/ppermute | solution.py:361
  328.4 9.2 %collective-permute-done.41 = bf16[256,2048]{1,0:T(8,128)(2,1)S(1)} collective-permute-done((bf16[256,2048]{1,0:T(8,128)(2,1)S(1)}, bf16[256,2048]{1,0:T(8,128)(2,1)S(1)}, u32[]{:S(2)}, u32[]{:S(2)}) %collective-permute-start.41) | collective-permute-done | bytes 1048608 | tf_op jit(solution)/shard_map/ppermute | solution.py:708
  361.8 5.5 collective-permute-done.49
  399.0 4.0 collective-permute-done.54
  441.1 6.1 collective-permute-done.64
  448.1 10.3 %collective-permute-done.63 = bf16[128,2048]{1,0:T(8,128)(2,1)S(1)} collective-permute-done((bf16[128,2048]{1,0:T(8,128)(2,1)S(1)}, bf16[128,2048]{1,0:T(8,128)(2,1)S(1)}, u32[]{:S(2)}, u32[]{:S(2)}) %collective-permute-start.63) | collective-permute-done | bytes 524320 | tf_op jit(solution)/shard_map/ppermute | solution.py:361
  486.8 6.0 collective-permute-done.70
  498.4 10.1 %attend_back.1 = bf16[4,2,2,128,384]{4,3,2,1,0:T(8,128)(2,1)S(1)} custom-call(s32[4]{0:T(128)S(1)} %copy-done.11, bf16[2,1024,128]{2,1,0:T(8,128)(2,1)S(1)} %get-tuple-element.157.q_ref, bf16[2,1024,128]{2,1,0:T(8,128)(2,1)S(1)} %copy-done.7, bf16[2,1024,128]{2,1,0:T(8,128)(2,1)S(1)} %copy-done.9, f32[2,1024,128]{2,1,0:T(8,128)S(1)} %get-tuple-element.160.att_ref, ...), custom_call_target="tpu_custom_call" | custom-call | bytes 1048576 | tf_op jit(solution)/shard_map/attend_back/pallas_call | solution.py:540
  525.3 19.0 %collective-permute-done.76 = bf16[2,256,2048]{2,1,0:T(8,128)(2,1)S(1)} collective-permute-done((bf16[2,256,2048]{2,1,0:T(8,128)(2,1)S(1)}, bf16[2,256,2048]{2,1,0:T(8,128)(2,1)S(1)}, u32[]{:S(2)}, u32[]{:S(2)}) %collective-permute-start.76) | collective-permute-done | bytes 2097184 | tf_op jit(solution)/shard_map/ppermute | solution.py:361
  544.3 22.0 %collective-permute-done.77 = bf16[2048,256]{1,0:T(8,128)(2,1)S(1)} collective-permute-done((bf16[2048,256]{1,0:T(8,128)(2,1)S(1)}, bf16[2048,256]{1,0:T(8,128)(2,1)S(1)}, u32[]{:S(2)}, u32[]{:S(2)}) %collective-permute-start.77) | collective-permute-done | bytes 1048608 | tf_op jit(solution)/shard_map/ppermute | solution.py:361
  576.3 10.8 %collective-permute-done.91 = bf16[128,2048]{1,0:T(8,128)(2,1)S(1)} collective-permute-done((bf16[128,2048]{1,0:T(8,128)(2,1)S(1)}, bf16[128,2048]{1,0:T(8,128)(2,1)S(1)}, u32[]{:S(2)}, u32[]{:S(2)}) %collective-permute-start.91) | collective-permute-done | bytes 524320 | tf_op jit(solution)/shard_map/ppermute | solution.py:361
  588.5 9.8 %collective-permute-done.87 = bf16[128,2048]{1,0:T(8,128)(2,1)S(1)} collective-permute-done((bf16[128,2048]{1,0:T(8,128)(2,1)S(1)}, bf16[128,2048]{1,0:T(8,128)(2,1)S(1)}, u32[]{:S(2)}, u32[]{:S(2)}) %collective-permute-start.87) | collective-permute-done | bytes 524320 | tf_op jit(solution)/shard_map/ppermute | solution.py:361
  603.2 4.5 collective-permute-done.81
  613.6 23.3 %collective-permute-done.88 = bf16[128,2048]{1,0:T(8,128)(2,1)S(1)} collective-permute-done((bf16[128,2048]{1,0:T(8,128)(2,1)S(1)}, bf16[128,2048]{1,0:T(8,128)(2,1)S(1)}, u32[]{:S(2)}, u32[]{:S(2)}) %collective-permute-start.88) | collective-permute-done | bytes 524320 | tf_op jit(solution)/shard_map/ppermute | solution.py:365
  640.3 4.5 collective-permute-done.89
  644.8 17.1 %collective-permute-start.105 = (bf16[128,2048]{1,0:T(8,128)(2,1)S(1)}, bf16[128,2048]{1,0:T(8,128)(2,1)S(1)}, u32[]{:S(2)}, u32[]{:S(2)}) collective-permute-start(bf16[128,2048]{1,0:T(8,128)(2,1)S(1)} %collective-permute-done.82), channel_id=1, source_target_pairs={{0,16},{16,0},{1,17},{17,1},{2,18},{18,2},{3,19},{19,3},{4,20},{20... | collective-permute-start | bytes 1572872 | tf_op jit(solution)/shard_map/ppermute | solution.py:361
  666.0 27.1 %collective-permute-done.84 = bf16[128,2048]{1,0:T(8,128)(2,1)S(1)} collective-permute-done((bf16[128,2048]{1,0:T(8,128)(2,1)S(1)}, bf16[128,2048]{1,0:T(8,128)(2,1)S(1)}, u32[]{:S(2)}, u32[]{:S(2)}) %collective-permute-start.84) | collective-permute-done | bytes 524320 | tf_op jit(solution)/shard_map/ppermute | solution.py:365
  693.5 9.4 %collective-permute-done.107 = bf16[128,2048]{1,0:T(8,128)(2,1)S(1)} collective-permute-done((bf16[128,2048]{1,0:T(8,128)(2,1)S(1)}, bf16[128,2048]{1,0:T(8,128)(2,1)S(1)}, u32[]{:S(2)}, u32[]{:S(2)}) %collective-permute-start.107) | collective-permute-done | bytes 524320 | tf_op jit(solution)/shard_map/ppermute | solution.py:361
  702.9 7.1 collective-permute-done.100
  715.6 4.2 collective-permute-done.93
  719.8 7.5 collective-permute-done.90
  729.1 5.2 copy.45
  747.6 4.9 collective-permute-done.109
  752.6 5.7 collective-permute-start.110
  758.9 8.9 %collective-permute-done.110 = bf16[2048,64]{0,1:T(8,128)(2,1)S(1)} collective-permute-done((bf16[2048,64]{0,1:T(8,128)(2,1)S(1)}, bf16[2048,64]{0,1:T(8,128)(2,1)S(1)}, u32[]{:S(2)}, u32[]{:S(2)}) %collective-permute-start.110) | collective-permute-done | bytes 262176 | tf_op jit(solution)/shard_map/ppermute | solution.py:666
  (596 shorter events, 325.7 us)
Async XLA Ops:
  5.5 58.7 %collective-permute-start.8 = (bf16[128,2048]{1,0:T(8,128)(2,1)}, bf16[128,2048]{1,0:T(8,128)(2,1)}, u32[]{:S(2)}, u32[]{:S(2)}) collective-permute-start(bf16[128,2048]{1,0:T(8,128)(2,1)} %get-tuple-element.284), channel_id=1, source_target_pairs={{0,4},{2,6},{4,0},{6,2},{1,5},{3,7},{5,1},{7,3},{8,12},{10,14},{12... | collective-permute-start | bytes 1572872 | tf_op jit(solution)/shard_map/ppermute | solution.py:365
  8.1 25.7 %collective-permute-start.5 = (bf16[128,2048]{1,0:T(8,128)(2,1)}, bf16[128,2048]{1,0:T(8,128)(2,1)S(1)}, u32[]{:S(2)}, u32[]{:S(2)}) collective-permute-start(bf16[128,2048]{1,0:T(8,128)(2,1)} %get-tuple-element.284), channel_id=1, source_target_pairs={{0,6},{2,4},{4,2},{6,0},{1,7},{3,5},{5,3},{7,1},{8,14},{10,12},{12... | collective-permute-start | bytes 1572872 | tf_op jit(solution)/shard_map/ppermute | solution.py:365
  9.4 34.8 %collective-permute-start.2 = (bf16[128,2048]{1,0:T(8,128)(2,1)}, bf16[128,2048]{1,0:T(8,128)(2,1)}, u32[]{:S(2)}, u32[]{:S(2)}) collective-permute-start(bf16[128,2048]{1,0:T(8,128)(2,1)} %get-tuple-element.284), channel_id=1, source_target_pairs={{0,2},{2,0},{4,6},{6,4},{1,3},{3,1},{5,7},{7,5},{8,10},{10,8},{12,... | collective-permute-start | bytes 1572872 | tf_op jit(solution)/shard_map/ppermute | solution.py:365
  12.9 51.3 %collective-permute-start.9 = (bf16[384,2048]{1,0:T(8,128)(2,1)}, bf16[384,2048]{1,0:T(8,128)(2,1)}, u32[]{:S(2)}, u32[]{:S(2)}) collective-permute-start(bf16[384,2048]{1,0:T(8,128)(2,1)} %bitcast.3), channel_id=1, source_target_pairs={{0,8},{10,2},{4,12},{14,6},{1,9},{11,3},{5,13},{15,7},{16,24},{26,... | collective-permute-start | bytes 4718600 | tf_op jit(solution)/shard_map/ppermute | solution.py:688
  32.3 26.8 %collective-permute-start.1 = (bf16[256,2048]{1,0:T(8,128)(2,1)}, bf16[256,2048]{1,0:T(8,128)(2,1)}, u32[]{:S(2)}, u32[]{:S(2)}) collective-permute-start(bf16[256,2048]{1,0:T(8,128)(2,1)} %pad_maximum_fusion.6), channel_id=1, source_target_pairs={{0,1},{1,0},{2,3},{3,2},{4,5},{5,4},{6,7},{7,6},{8,9},{9,8},{10,11... | collective-permute-start | bytes 3145736 | tf_op jit(solution)/shard_map/ppermute | solution.py:361
  48.6 34.1 %collective-permute-start.7 = (bf16[256,2048]{1,0:T(8,128)(2,1)S(1)}, bf16[256,2048]{1,0:T(8,128)(2,1)S(1)}, u32[]{:S(2)}, u32[]{:S(2)}) collective-permute-start(bf16[256,2048]{1,0:T(8,128)(2,1)S(1)} %pad_maximum_fusion.8), channel_id=1, source_target_pairs={{0,1},{1,0},{2,3},{3,2},{4,5},{5,4},{6,7},{7,6},{8,9},{9,8},{10,11... | collective-permute-start | bytes 3145736 | tf_op jit(solution)/shard_map/ppermute | solution.py:361
  88.4 40.0 %collective-permute-start.15 = (bf16[128,2048]{1,0:T(8,128)(2,1)}, bf16[128,2048]{1,0:T(8,128)(2,1)}, u32[]{:S(2)}, u32[]{:S(2)}) collective-permute-start(bf16[128,2048]{1,0:T(8,128)(2,1)} %bitcast.15), channel_id=1, source_target_pairs={{0,8},{8,0},{1,9},{9,1},{2,10},{10,2},{3,11},{11,3},{4,12},{12,4},... | collective-permute-start | bytes 1572872 | tf_op jit(solution)/shard_map/ppermute | solution.py:361
  92.3 36.1 %collective-permute-start.14 = (bf16[128,2048]{1,0:T(8,128)(2,1)}, bf16[128,2048]{1,0:T(8,128)(2,1)}, u32[]{:S(2)}, u32[]{:S(2)}) collective-permute-start(bf16[128,2048]{1,0:T(8,128)(2,1)} %bitcast.15), channel_id=1, source_target_pairs={{0,2},{2,0},{4,6},{6,4},{1,3},{3,1},{5,7},{7,5},{8,10},{10,8},{12,... | collective-permute-start | bytes 1572872 | tf_op jit(solution)/shard_map/ppermute | solution.py:365
  139.2 46.4 %collective-permute-start.22 = (bf16[1024,1024]{1,0:T(8,128)(2,1)S(1)}, bf16[1024,1024]{1,0:T(8,128)(2,1)S(1)}, u32[]{:S(2)}, u32[]{:S(2)}) collective-permute-start(bf16[1024,1024]{1,0:T(8,128)(2,1)S(1)} %pad_maximum_fusion), channel_id=1, source_target_pairs={{0,8},{8,0},{1,9},{9,1},{2,10},{10,2},{3,11},{11,3},{4,12},{12,4},... | collective-permute-start | bytes 6291464 | tf_op jit(solution)/shard_map/ppermute | solution.py:361
  143.7 34.8 %collective-permute-start.23 = (bf16[1024,512]{1,0:T(8,128)(2,1)S(1)}, bf16[1024,512]{1,0:T(8,128)(2,1)S(1)}, u32[]{:S(2)}, u32[]{:S(2)}) collective-permute-start(bf16[1024,512]{1,0:T(8,128)(2,1)S(1)} %pad_maximum_fusion.10), channel_id=1, source_target_pairs={{0,16},{16,0},{1,17},{17,1},{2,18},{18,2},{3,19},{19,3},{4,20},{20... | collective-permute-start | bytes 3145736 | tf_op jit(solution)/shard_map/ppermute | solution.py:361
  187.1 29.6 %collective-permute-start.24 = (bf16[2048,1024]{1,0:T(8,128)(2,1)}, bf16[2048,1024]{1,0:T(8,128)(2,1)}, u32[]{:S(2)}, u32[]{:S(2)}) collective-permute-start(bf16[2048,1024]{1,0:T(8,128)(2,1)} %constant_dynamic-update-slice_fusion.12.half), channel_id=1, source_target_pairs={{0,1},{1,0},{2,3},{3,2},{4,5},{5,4},{6,7},{7,6},{8,9},{9,8},{10,11... | collective-permute-start | bytes 12582920 | tf_op jit(solution)/shard_map/ppermute | solution.py:361
  201.2 30.3 %collective-permute-start.26 = (bf16[128,2048]{1,0:T(8,128)(2,1)}, bf16[128,2048]{1,0:T(8,128)(2,1)}, u32[]{:S(2)}, u32[]{:S(2)}) collective-permute-start(bf16[128,2048]{1,0:T(8,128)(2,1)} %bitcast.15), channel_id=1, source_target_pairs={{0,4},{2,6},{4,0},{6,2},{1,5},{3,7},{5,1},{7,3},{8,12},{10,14},{12... | collective-permute-start | bytes 1572872 | tf_op jit(solution)/shard_map/ppermute | solution.py:365
  210.9 27.1 %collective-permute-start.27 = (bf16[256,2048]{1,0:T(8,128)(2,1)}, bf16[256,2048]{1,0:T(8,128)(2,1)}, u32[]{:S(2)}, u32[]{:S(2)}) collective-permute-start(bf16[256,2048]{1,0:T(8,128)(2,1)} %get-tuple-element.165), channel_id=1, source_target_pairs={{0,16},{2,18},{20,4},{22,6},{1,17},{3,19},{21,5},{23,7},{8,24},{10... | collective-permute-start | bytes 3145736 | tf_op jit(solution)/shard_map/ppermute | solution.py:708
  238.0 27.9 %collective-permute-start.38 = (bf16[128,2048]{1,0:T(8,128)(2,1)S(1)}, bf16[128,2048]{1,0:T(8,128)(2,1)S(1)}, u32[]{:S(2)}, u32[]{:S(2)}) collective-permute-start(bf16[128,2048]{1,0:T(8,128)(2,1)S(1)} %multiply_convert_fusion.12), channel_id=1, source_target_pairs={{0,4},{2,6},{4,0},{6,2},{1,5},{3,7},{5,1},{7,3},{8,12},{10,14},{12... | collective-permute-start | bytes 1572872 | tf_op jit(solution)/shard_map/ppermute | solution.py:365
  238.0 28.0 %collective-permute-start.31 = (bf16[128,2048]{1,0:T(8,128)(2,1)S(1)}, bf16[128,2048]{1,0:T(8,128)(2,1)S(1)}, u32[]{:S(2)}, u32[]{:S(2)}) collective-permute-start(bf16[128,2048]{1,0:T(8,128)(2,1)S(1)} %multiply_convert_fusion.12), channel_id=1, source_target_pairs={{0,2},{2,0},{4,6},{6,4},{1,3},{3,1},{5,7},{7,5},{8,10},{10,8},{12,... | collective-permute-start | bytes 1572872 | tf_op jit(solution)/shard_map/ppermute | solution.py:365
  240.1 26.6 %collective-permute-start.33 = (bf16[128,2048]{1,0:T(8,128)(2,1)}, bf16[128,2048]{1,0:T(8,128)(2,1)S(1)}, u32[]{:S(2)}, u32[]{:S(2)}) collective-permute-start(bf16[128,2048]{1,0:T(8,128)(2,1)} %collective-permute-done.14), channel_id=1, source_target_pairs={{0,8},{8,0},{1,9},{9,1},{2,10},{10,2},{3,11},{11,3},{4,12},{12,4},... | collective-permute-start | bytes 1572872 | tf_op jit(solution)/shard_map/ppermute | solution.py:361
  254.2 38.6 %collective-permute-start.30 = (bf16[128,2048]{1,0:T(8,128)(2,1)S(1)}, bf16[128,2048]{1,0:T(8,128)(2,1)S(1)}, u32[]{:S(2)}, u32[]{:S(2)}) collective-permute-start(bf16[128,2048]{1,0:T(8,128)(2,1)S(1)} %multiply_convert_fusion.12), channel_id=1, source_target_pairs={{0,6},{2,4},{4,2},{6,0},{1,7},{3,5},{5,3},{7,1},{8,14},{10,12},{12... | collective-permute-start | bytes 1572872 | tf_op jit(solution)/shard_map/ppermute | solution.py:365
  265.9 26.3 %collective-permute-start.29 = (bf16[256,2048]{1,0:T(8,128)(2,1)S(1)}, bf16[256,2048]{1,0:T(8,128)(2,1)S(1)}, u32[]{:S(2)}, u32[]{:S(2)}) collective-permute-start(bf16[256,2048]{1,0:T(8,128)(2,1)S(1)} %pad_maximum_fusion.12), channel_id=1, source_target_pairs={{0,1},{1,0},{2,3},{3,2},{4,5},{5,4},{6,7},{7,6},{8,9},{9,8},{10,11... | collective-permute-start | bytes 3145736 | tf_op jit(solution)/shard_map/ppermute | solution.py:361
  269.3 33.5 %collective-permute-start.34 = (bf16[256,2048]{1,0:T(8,128)(2,1)S(1)}, bf16[256,2048]{1,0:T(8,128)(2,1)S(1)}, u32[]{:S(2)}, u32[]{:S(2)}) collective-permute-start(bf16[256,2048]{1,0:T(8,128)(2,1)S(1)} %copy-done.35), channel_id=1, source_target_pairs={{0,16},{2,18},{20,4},{22,6},{1,17},{3,19},{21,5},{23,7},{8,24},{10... | collective-permute-start | bytes 3145736 | tf_op jit(solution)/shard_map/ppermute | solution.py:708
  292.9 35.1 %collective-permute-start.44 = (bf16[256,2048]{1,0:T(8,128)(2,1)S(1)}, bf16[256,2048]{1,0:T(8,128)(2,1)S(1)}, u32[]{:S(2)}, u32[]{:S(2)}) collective-permute-start(bf16[256,2048]{1,0:T(8,128)(2,1)S(1)} %pad_maximum_fusion.15), channel_id=1, source_target_pairs={{0,1},{1,0},{2,3},{3,2},{4,5},{5,4},{6,7},{7,6},{8,9},{9,8},{10,11... | collective-permute-start | bytes 3145736 | tf_op jit(solution)/shard_map/ppermute | solution.py:361
  310.9 26.7 %collective-permute-start.41 = (bf16[256,2048]{1,0:T(8,128)(2,1)S(1)}, bf16[256,2048]{1,0:T(8,128)(2,1)S(1)}, u32[]{:S(2)}, u32[]{:S(2)}) collective-permute-start(bf16[256,2048]{1,0:T(8,128)(2,1)S(1)} %copy-done.34), channel_id=1, source_target_pairs={{0,16},{2,18},{20,4},{22,6},{1,17},{3,19},{21,5},{23,7},{8,24},{10... | collective-permute-start | bytes 3145736 | tf_op jit(solution)/shard_map/ppermute | solution.py:708
  361.5 25.3 %collective-permute-start.51 = (bf16[256,2048]{1,0:T(8,128)(2,1)}, bf16[256,2048]{1,0:T(8,128)(2,1)}, u32[]{:S(2)}, u32[]{:S(2)}) collective-permute-start(bf16[256,2048]{1,0:T(8,128)(2,1)} %slice.475), channel_id=1, source_target_pairs={{0,1},{1,0},{2,3},{3,2},{4,5},{5,4},{6,7},{7,6},{8,9},{9,8},{10,11... | collective-permute-start | bytes 3145736 | tf_op jit(solution)/shard_map/ppermute | solution.py:361
  369.7 64.9 %collective-permute-start.61 = (bf16[128,2048]{1,0:T(8,128)(2,1)}, bf16[128,2048]{1,0:T(8,128)(2,1)}, u32[]{:S(2)}, u32[]{:S(2)}) collective-permute-start(bf16[128,2048]{1,0:T(8,128)(2,1)} %convert_add_fusion.15), channel_id=1, source_target_pairs={{0,6},{2,4},{4,2},{6,0},{1,7},{3,5},{5,3},{7,1},{8,14},{10,12},{12... | collective-permute-start | bytes 1572872 | tf_op jit(solution)/shard_map/ppermute | solution.py:365
  390.1 45.7 %collective-permute-start.62 = (bf16[128,2048]{1,0:T(8,128)(2,1)}, bf16[128,2048]{1,0:T(8,128)(2,1)}, u32[]{:S(2)}, u32[]{:S(2)}) collective-permute-start(bf16[128,2048]{1,0:T(8,128)(2,1)} %convert_add_fusion.14), channel_id=1, source_target_pairs={{0,4},{2,6},{4,0},{6,2},{1,5},{3,7},{5,1},{7,3},{8,12},{10,14},{12... | collective-permute-start | bytes 1572872 | tf_op jit(solution)/shard_map/ppermute | solution.py:365
  439.0 35.3 %collective-permute-start.69 = (bf16[128,2048]{1,0:T(8,128)(2,1)S(1)}, bf16[128,2048]{1,0:T(8,128)(2,1)}, u32[]{:S(2)}, u32[]{:S(2)}) collective-permute-start(bf16[128,2048]{1,0:T(8,128)(2,1)S(1)} %slice.482), channel_id=1, source_target_pairs={{0,8},{8,0},{1,9},{9,1},{2,10},{10,2},{3,11},{11,3},{4,12},{12,4},... | collective-permute-start | bytes 1572872 | tf_op jit(solution)/shard_map/ppermute | solution.py:361
  440.6 39.8 %collective-permute-start.68 = (bf16[128,2048]{1,0:T(8,128)(2,1)}, bf16[128,2048]{1,0:T(8,128)(2,1)}, u32[]{:S(2)}, u32[]{:S(2)}) collective-permute-start(bf16[128,2048]{1,0:T(8,128)(2,1)} %slice.483), channel_id=1, source_target_pairs={{0,8},{8,0},{1,9},{9,1},{2,10},{10,2},{3,11},{11,3},{4,12},{12,4},... | collective-permute-start | bytes 1572872 | tf_op jit(solution)/shard_map/ppermute | solution.py:361
  495.7 48.6 %collective-permute-start.76 = (bf16[2,256,2048]{2,1,0:T(8,128)(2,1)S(1)}, bf16[2,256,2048]{2,1,0:T(8,128)(2,1)S(1)}, u32[]{:S(2)}, u32[]{:S(2)}) collective-permute-start(bf16[2,256,2048]{2,1,0:T(8,128)(2,1)S(1)} %fusion.3), channel_id=1, source_target_pairs={{0,16},{16,0},{1,17},{17,1},{2,18},{18,2},{3,19},{19,3},{4,20},{20... | collective-permute-start | bytes 6291464 | tf_op jit(solution)/shard_map/ppermute | solution.py:361
  496.4 69.9 %collective-permute-start.77 = (bf16[2048,256]{1,0:T(8,128)(2,1)S(1)}, bf16[2048,256]{1,0:T(8,128)(2,1)S(1)}, u32[]{:S(2)}, u32[]{:S(2)}) collective-permute-start(bf16[2048,256]{1,0:T(8,128)(2,1)S(1)} %copy-done.63), channel_id=1, source_target_pairs={{0,16},{16,0},{1,17},{17,1},{2,18},{18,2},{3,19},{19,3},{4,20},{20... | collective-permute-start | bytes 3145736 | tf_op jit(solution)/shard_map/ppermute | solution.py:361
  497.8 68.4 %collective-permute-start.78 = (bf16[128,2048]{1,0:T(8,128)(2,1)S(1)}, bf16[128,2048]{1,0:T(8,128)(2,1)S(1)}, u32[]{:S(2)}, u32[]{:S(2)}) collective-permute-start(bf16[128,2048]{1,0:T(8,128)(2,1)S(1)} %copy-done.69), channel_id=1, source_target_pairs={{0,2},{2,0},{4,6},{6,4},{1,3},{3,1},{5,7},{7,5},{8,10},{10,8},{12,... | collective-permute-start | bytes 1572872 | tf_op jit(solution)/shard_map/ppermute | solution.py:365
  521.4 44.9 %collective-permute-start.79 = (bf16[128,2048]{1,0:T(8,128)(2,1)S(1)}, bf16[128,2048]{1,0:T(8,128)(2,1)S(1)}, u32[]{:S(2)}, u32[]{:S(2)}) collective-permute-start(bf16[128,2048]{1,0:T(8,128)(2,1)S(1)} %copy-done.71), channel_id=1, source_target_pairs={{0,6},{2,4},{4,2},{6,0},{1,7},{3,5},{5,3},{7,1},{8,14},{10,12},{12... | collective-permute-start | bytes 1572872 | tf_op jit(solution)/shard_map/ppermute | solution.py:365
  524.6 45.4 %collective-permute-start.80 = (bf16[128,2048]{1,0:T(8,128)(2,1)S(1)}, bf16[128,2048]{1,0:T(8,128)(2,1)S(1)}, u32[]{:S(2)}, u32[]{:S(2)}) collective-permute-start(bf16[128,2048]{1,0:T(8,128)(2,1)S(1)} %copy-done.70), channel_id=1, source_target_pairs={{0,4},{2,6},{4,0},{6,2},{1,5},{3,7},{5,1},{7,3},{8,12},{10,14},{12... | collective-permute-start | bytes 1572872 | tf_op jit(solution)/shard_map/ppermute | solution.py:365
  570.0 32.3 %collective-permute-start.92 = (bf16[128,2048]{1,0:T(8,128)(2,1)S(1)}, bf16[128,2048]{1,0:T(8,128)(2,1)S(1)}, u32[]{:S(2)}, u32[]{:S(2)}) collective-permute-start(bf16[128,2048]{1,0:T(8,128)(2,1)S(1)} %copy-done.24), channel_id=1, source_target_pairs={{0,2},{2,0},{4,6},{6,4},{1,3},{3,1},{5,7},{7,5},{8,10},{10,8},{12,... | collective-permute-start | bytes 1572872 | tf_op jit(solution)/shard_map/ppermute | solution.py:365
  570.0 38.2 %collective-permute-start.82 = (bf16[128,2048]{1,0:T(8,128)(2,1)S(1)}, bf16[128,2048]{1,0:T(8,128)(2,1)S(1)}, u32[]{:S(2)}, u32[]{:S(2)}) collective-permute-start(bf16[128,2048]{1,0:T(8,128)(2,1)S(1)} %copy-done.24), channel_id=1, source_target_pairs={{0,6},{2,4},{4,2},{6,0},{1,7},{3,5},{5,3},{7,1},{8,14},{10,12},{12... | collective-permute-start | bytes 1572872 | tf_op jit(solution)/shard_map/ppermute | solution.py:365
  573.0 25.4 %collective-permute-start.87 = (bf16[128,2048]{1,0:T(8,128)(2,1)S(1)}, bf16[128,2048]{1,0:T(8,128)(2,1)S(1)}, u32[]{:S(2)}, u32[]{:S(2)}) collective-permute-start(bf16[128,2048]{1,0:T(8,128)(2,1)S(1)} %slice.479), channel_id=1, source_target_pairs={{0,16},{16,0},{1,17},{17,1},{2,18},{18,2},{3,19},{19,3},{4,20},{20... | collective-permute-start | bytes 1572872 | tf_op jit(solution)/shard_map/ppermute | solution.py:361
  575.7 31.9 %collective-permute-start.81 = (bf16[128,2048]{1,0:T(8,128)(2,1)S(1)}, bf16[128,2048]{1,0:T(8,128)(2,1)S(1)}, u32[]{:S(2)}, u32[]{:S(2)}) collective-permute-start(bf16[128,2048]{1,0:T(8,128)(2,1)S(1)} %slice.481), channel_id=1, source_target_pairs={{0,16},{16,0},{1,17},{17,1},{2,18},{18,2},{3,19},{19,3},{4,20},{20... | collective-permute-start | bytes 1572872 | tf_op jit(solution)/shard_map/ppermute | solution.py:361
  598.4 46.5 %collective-permute-start.89 = (bf16[2048,256]{1,0:T(8,128)(2,1)S(1)}, bf16[2048,256]{1,0:T(8,128)(2,1)S(1)}, u32[]{:S(2)}, u32[]{:S(2)}) collective-permute-start(bf16[2048,256]{1,0:T(8,128)(2,1)S(1)} %add_convert_fusion.4), channel_id=1, source_target_pairs={{0,0},{1,1},{2,8},{3,9},{4,4},{5,5},{6,12},{7,13},{8,2},{9,3},{10,... | collective-permute-start | bytes 3145736 | tf_op jit(solution)/shard_map/ppermute | solution.py:847
  602.3 34.6 %collective-permute-start.88 = (bf16[128,2048]{1,0:T(8,128)(2,1)S(1)}, bf16[128,2048]{1,0:T(8,128)(2,1)S(1)}, u32[]{:S(2)}, u32[]{:S(2)}) collective-permute-start(bf16[128,2048]{1,0:T(8,128)(2,1)S(1)} %copy-done.24), channel_id=1, source_target_pairs={{0,4},{2,6},{4,0},{6,2},{1,5},{3,7},{5,1},{7,3},{8,12},{10,14},{12... | collective-permute-start | bytes 1572872 | tf_op jit(solution)/shard_map/ppermute | solution.py:365
  607.7 54.5 %collective-permute-start.101 = (bf16[128,2048]{1,0:T(8,128)(2,1)S(1)}, bf16[128,2048]{1,0:T(8,128)(2,1)S(1)}, u32[]{:S(2)}, u32[]{:S(2)}) collective-permute-start(bf16[128,2048]{1,0:T(8,128)(2,1)S(1)} %copy-done.24), channel_id=1, source_target_pairs={{0,16},{16,0},{1,17},{17,1},{2,18},{18,2},{3,19},{19,3},{4,20},{20... | collective-permute-start | bytes 1572872 | tf_op jit(solution)/shard_map/ppermute | solution.py:361
  608.3 103.1 %collective-permute-start.85 = (bf16[2,256,2048]{2,1,0:T(8,128)(2,1)S(1)}, bf16[2,256,2048]{2,1,0:T(8,128)(2,1)S(1)}, u32[]{:S(2)}, u32[]{:S(2)}) collective-permute-start(bf16[2,256,2048]{2,1,0:T(8,128)(2,1)S(1)} %add_convert_fusion), channel_id=1, source_target_pairs={{0,0},{1,1},{2,8},{3,9},{4,4},{5,5},{6,12},{7,13},{8,2},{9,3},{10,... | collective-permute-start | bytes 6291464 | tf_op jit(solution)/shard_map/ppermute | solution.py:846
  611.7 52.6 %collective-permute-start.103 = (bf16[128,2048]{1,0:T(8,128)(2,1)S(1)}, bf16[128,2048]{1,0:T(8,128)(2,1)S(1)}, u32[]{:S(2)}, u32[]{:S(2)}) collective-permute-start(bf16[128,2048]{1,0:T(8,128)(2,1)S(1)} %collective-permute-done.92), channel_id=1, source_target_pairs={{0,16},{16,0},{1,17},{17,1},{2,18},{18,2},{3,19},{19,3},{4,20},{20... | collective-permute-start | bytes 1572872 | tf_op jit(solution)/shard_map/ppermute | solution.py:361
  636.9 56.2 %collective-permute-start.84 = (bf16[128,2048]{1,0:T(8,128)(2,1)S(1)}, bf16[128,2048]{1,0:T(8,128)(2,1)S(1)}, u32[]{:S(2)}, u32[]{:S(2)}) collective-permute-start(bf16[128,2048]{1,0:T(8,128)(2,1)S(1)} %convert_add_fusion.7), channel_id=1, source_target_pairs={{0,4},{2,6},{4,0},{6,2},{1,5},{3,7},{5,1},{7,3},{8,12},{10,14},{12... | collective-permute-start | bytes 1572872 | tf_op jit(solution)/shard_map/ppermute | solution.py:365
  644.8 48.4 %collective-permute-start.105 = (bf16[128,2048]{1,0:T(8,128)(2,1)S(1)}, bf16[128,2048]{1,0:T(8,128)(2,1)S(1)}, u32[]{:S(2)}, u32[]{:S(2)}) collective-permute-start(bf16[128,2048]{1,0:T(8,128)(2,1)S(1)} %collective-permute-done.82), channel_id=1, source_target_pairs={{0,16},{16,0},{1,17},{17,1},{2,18},{18,2},{3,19},{19,3},{4,20},{20... | collective-permute-start | bytes 1572872 | tf_op jit(solution)/shard_map/ppermute | solution.py:361
  662.2 47.9 %collective-permute-start.100 = (bf16[3,64,2048]{2,1,0:T(8,128)(2,1)S(1)}, bf16[3,64,2048]{2,1,0:T(8,128)(2,1)S(1)}, u32[]{:S(2)}, u32[]{:S(2)}) collective-permute-start(bf16[3,64,2048]{2,1,0:T(8,128)(2,1)S(1)} %add_convert_fusion.5), channel_id=1, source_target_pairs={{0,0},{1,1},{2,2},{3,3},{4,16},{5,17},{6,18},{7,19},{8,8},{9,9},{1... | collective-permute-start | bytes 2359304 | tf_op jit(solution)/shard_map/ppermute | solution.py:853
  664.3 38.5 %collective-permute-start.107 = (bf16[128,2048]{1,0:T(8,128)(2,1)S(1)}, bf16[128,2048]{1,0:T(8,128)(2,1)S(1)}, u32[]{:S(2)}, u32[]{:S(2)}) collective-permute-start(bf16[128,2048]{1,0:T(8,128)(2,1)S(1)} %collective-permute-done.88), channel_id=1, source_target_pairs={{0,16},{16,0},{1,17},{17,1},{2,18},{18,2},{3,19},{19,3},{4,20},{20... | collective-permute-start | bytes 1572872 | tf_op jit(solution)/shard_map/ppermute | solution.py:361
  693.3 26.5 %collective-permute-start.93 = (bf16[128,2048]{1,0:T(8,128)(2,1)S(1)}, bf16[128,2048]{1,0:T(8,128)(2,1)S(1)}, u32[]{:S(2)}, u32[]{:S(2)}) collective-permute-start(bf16[128,2048]{1,0:T(8,128)(2,1)S(1)} %convert_add_fusion.5), channel_id=1, source_target_pairs={{0,6},{2,4},{4,2},{6,0},{1,7},{3,5},{5,3},{7,1},{8,14},{10,12},{12... | collective-permute-start | bytes 1572872 | tf_op jit(solution)/shard_map/ppermute | solution.py:365
  702.9 41.9 %collective-permute-start.102 = (bf16[256,2048]{1,0:T(8,128)(2,1)S(1)}, bf16[256,2048]{1,0:T(8,128)(2,1)S(1)}, u32[]{:S(2)}, u32[]{:S(2)}) collective-permute-start(bf16[256,2048]{1,0:T(8,128)(2,1)S(1)} %pad_maximum_fusion.19), channel_id=1, source_target_pairs={{0,1},{1,0},{2,3},{3,2},{4,5},{5,4},{6,7},{7,6},{8,9},{9,8},{10,11... | collective-permute-start | bytes 3145736 | tf_op jit(solution)/shard_map/ppermute | solution.py:361
  710.1 27.1 %collective-permute-start.104 = (bf16[256,2048]{1,0:T(8,128)(2,1)S(1)}, bf16[256,2048]{1,0:T(8,128)(2,1)S(1)}, u32[]{:S(2)}, u32[]{:S(2)}) collective-permute-start(bf16[256,2048]{1,0:T(8,128)(2,1)S(1)} %pad_maximum_fusion.20), channel_id=1, source_target_pairs={{0,1},{1,0},{2,3},{3,2},{4,5},{5,4},{6,7},{7,6},{8,9},{9,8},{10,11... | collective-permute-start | bytes 3145736 | tf_op jit(solution)/shard_map/ppermute | solution.py:361
  715.1 28.0 %collective-permute-start.106 = (bf16[256,2048]{1,0:T(8,128)(2,1)S(1)}, bf16[256,2048]{1,0:T(8,128)(2,1)S(1)}, u32[]{:S(2)}, u32[]{:S(2)}) collective-permute-start(bf16[256,2048]{1,0:T(8,128)(2,1)S(1)} %pad_maximum_fusion.21), channel_id=1, source_target_pairs={{0,1},{1,0},{2,3},{3,2},{4,5},{5,4},{6,7},{7,6},{8,9},{9,8},{10,11... | collective-permute-start | bytes 3145736 | tf_op jit(solution)/shard_map/ppermute | solution.py:361
  (154 other events, 1858.5 us)

commit v3 on v2

--- a/solution.py
+++ b/solution.py
@@ -565,29 +565,33 @@
     return pairs
 
 
-def join_kernel(place, half, other, out):
-    cols = half.shape[1]
-
-    @pl.when(place[3] == 0)
-    def _():
-        out[:, :cols] = half[...]
-        out[:, cols:] = other[...]
-
-    @pl.when(place[3] != 0)
-    def _():
-        out[:, :cols] = other[...]
-        out[:, cols:] = half[...]
-
-
-def join_out(place, half, other):
-    rows, cols = half.shape[0] // 4, half.shape[1]
-    block = pl.BlockSpec((rows, cols), lambda i, place: (i, 0))
+def join_kernel(place, pair, far, pair_c, far_c, out):
+    cols = pair.shape[1]
+    early = pl.program_id(0) < 2
+    for core in range(2):
+        here, there = slice(core * cols, (core + 1) * cols), slice((1 - core) * cols, (2 - core) * cols)
+
+        @pl.when((place[3] == core) & early)
+        def _():
+            out[:, here] = pair[...]
+            out[:, there] = pair_c[...]
+
+        @pl.when((place[3] == core) & jnp.logical_not(early))
+        def _():
+            out[:, here] = far[...]
+            out[:, there] = far_c[...]
+
+
+def join_out(place, pair, far, pair_c, far_c):
+    rows, cols = pair.shape[0] // 2, pair.shape[1]
+    early = pl.BlockSpec((rows, cols), lambda i, place: (jnp.minimum(i, 1), 0))
+    late = pl.BlockSpec((rows, cols), lambda i, place: (jnp.maximum(i - 2, 0), 0))
     return pl.pallas_call(
         join_kernel,
         grid_spec=pltpu.PrefetchScalarGridSpec(
             num_scalar_prefetch=1,
             grid=(4,),
-            in_specs=[block, block],
+            in_specs=[early, late, early, late],
             out_specs=pl.BlockSpec(
                 (rows, 2 * cols), lambda i, place: (place[2] ^ (((i & 1) << 1) | (i >> 1)), 0)
             ),
@@ -595,7 +599,7 @@
         out_shape=jax.ShapeDtypeStruct((4 * rows, 2 * cols), BF),
         cost_estimate=pl.CostEstimate(flops=0, bytes_accessed=1 << 20, transcendentals=0),
         name="join_out",
-    )(place, half, other)
+    )(place, pair, far, pair_c, far_c)
 
 
 def order_kernel(place, block, out):
@@ -666,6 +670,12 @@
     return lax.ppermute(value.astype(BF), AXES, perm_of(target)).astype(F32)
 
 
+def ff_step(value, name, leaving):
+    flip = 8 if name == "x" else 2
+    pairs = [(i, i ^ flip) for i in range(32) if (((i >> 3) ^ (i >> 1)) & 1) == leaving]
+    return lax.ppermute(value, AXES, pairs)
+
+
 def body(residual_in, attn_gain, mlp_gain, w_qkv, w_out, w_gate_up, w_down, cotangent):
     y, x, z, c = [lax.axis_index(name) for name in AXES]
     z1, z0 = z >> 1, z & 1
@@ -729,23 +739,24 @@
     out_x = swap(out_pair, "x")
     down_pair = jnp.concatenate([down_own, down_x], axis=0)
     down_y = swap(down_pair, "y")
+    pair_c = swap(out_pair, "c")
     pieces = send_plane(pieces, "y")
     pieces, cot_hops[2] = tick(pieces, cot_hops[2])
     pieces = send_hops(pieces)
-    pieces, out_x, down_y, gate_sent[0], cot = tick(pieces, out_x, down_y, gate_sent[0], cot)
+    pieces, out_x, down_y, gate_sent[0], cot, pair_c = tick(pieces, out_x, down_y, gate_sent[0], cot, pair_c)
     cot_hops[3] = hop(cot, 2)
     gate_moved = [to_y(gate_sent[0])]
-    out_half = jnp.concatenate([out_pair, out_x], axis=0)
-    out_c = swap(out_half, "c")
     attended = reorder(to_heads_kernel, place, pieces.reshape(16, BLK, 128), (BLK, width))
-    out_full = join_out(place, out_half, out_c)
+    out_full = join_out(place, out_pair, out_x, pair_c, swap(out_x, "c"))
     attended, out_full, cot_hops[1], cot_hops[2] = tick(attended, out_full, cot_hops[1], cot_hops[2])
     cot_others += [swap(item, "x") for item in cot_hops[1:3]]
     residual = inputs + dot(attended, out_full, 1, 1)
     scale_two = rms_scale(residual)
     normed_two = (residual * scale_two * gain_two).astype(BF)
 
-    normed_two, cot_hops[3], gate_moved[0], gate_sent[1] = tick(normed_two, cot_hops[3], gate_moved[0], gate_sent[1])
+    normed_two, cot_hops[3], gate_moved[0], gate_sent[1], down_pair, down_y, cot_hops[0], cot_others[0] = tick(
+        normed_two, cot_hops[3], gate_moved[0], gate_sent[1], down_pair, down_y, cot_hops[0], cot_others[0]
+    )
     gate_moved.append(to_y(gate_sent[1]))
     hops = [normed_two] + [hop(normed_two, j) for j in ORDER[1:]]
     others = [swap(normed_two, "x")]
@@ -774,9 +785,10 @@
             ff_chunks[i], back_parts[first] = tick(ff_chunks[i], back_parts[first])
             back_parts[first] = fold_plane(back_parts[first], "x")
         if i == last:
-            ff_chunks[i], back_parts[second], back_parts[first] = tick(
-                ff_chunks[i], back_parts[second], back_parts[first]
+            ff_chunks[i], back_parts[second], back_parts[first], mlp_parts[first] = tick(
+                ff_chunks[i], back_parts[second], back_parts[first], mlp_parts[first]
             )
+            mlp_parts[first] = fold_plane(mlp_parts[first], "x")
             back_parts[second] = fold_plane(back_parts[second], "x")
         gate, up = dot(ff_chunks[i], w_gate, 1, 1), dot(ff_chunks[i], w_up, 1, 1)
         sigmoid_gate = jax.nn.sigmoid(gate)
@@ -791,6 +803,7 @@
             back_parts[i], gate_grads[1:], up_grads[1:], hiddens[1:] = tied[0], tied[1:4], tied[4:7], tied[7:10]
             grad_gate, grad_up, hidden = tied[10:]
         back_parts[i] = fold_core(back_parts[i])
+        mlp_parts[i] = fold_core(dot(hidden, down, 1, 1))
         hiddens[i], gate_grads[i], up_grads[i] = hidden, grad_gate, grad_up
 
     def over_chunks(left, right):
@@ -799,31 +812,38 @@
     back_hops = [None] * 4
 
     def send_back(i):
-        back_hops[i] = hop(back_parts[i].astype(BF), ORDER[i]).astype(F32)
+        back_hops[i] = hop(back_parts[i].astype(BF), ORDER[i])
 
     send_back(first)
     gate_grad = over_chunks(gate_grads, ff_chunks)
-    gate_grad, *up_grads, back_parts[third], back_parts[second] = tick(
-        gate_grad, *up_grads, back_parts[third], back_parts[second]
-    )
+    gate_grad, *up_grads, back_parts[third], back_parts[second], mlp_parts[second], mlp_parts[first] = tick(
+        gate_grad, *up_grads, back_parts[third], back_parts[second], mlp_parts[second], mlp_parts[first]
+    )
+    mlp_parts[second] = fold_plane(mlp_parts[second], "x")
     back_parts[third] = fold_plane(back_parts[third], "x")
     send_back(second)
+    gate_own, gate_other = split(gate_grad, 0, y)
+    gate_other = swap(gate_other, "y")
     up_grad = over_chunks(up_grads, ff_chunks)
-    up_grad, *hiddens, back_parts[last], back_parts[third] = tick(up_grad, *hiddens, back_parts[last], back_parts[third])
+    up_grad, *hiddens, back_parts[last], back_parts[third], mlp_parts[third], gate_other = tick(
+        up_grad, *hiddens, back_parts[last], back_parts[third], mlp_parts[third], gate_other
+    )
+    mlp_parts[third] = fold_plane(mlp_parts[third], "x")
     back_parts[last] = fold_plane(back_parts[last], "x")
     send_back(third)
-    gu_own, gu_other = split(jnp.stack([gate_grad, up_grad]), 1, y)
-    gu_other = swap(gu_other, "y")
-    mlp_parts = [dot(item, down, 1, 1).astype(BF) for item in hiddens]
-    mlp_parts = [fold_core(item) for item in mlp_parts]
+    up_own, up_other = split(up_grad, 0, y)
+    up_other = swap(up_other, "y")
     down_grad = over_chunks(cot_chunks, hiddens)
     down_own, down_other = split(down_grad, 1, y)
-    back_parts[last], down_other, *mlp_parts = tick(back_parts[last], down_other, *mlp_parts)
+    back_parts[last], down_other, mlp_parts[last], mlp_parts[second] = tick(
+        back_parts[last], down_other, mlp_parts[last], mlp_parts[second]
+    )
+    mlp_parts[last] = fold_plane(mlp_parts[last], "x")
+    mlp_hops = [None] + [hop(mlp_parts[i].astype(BF), ORDER[i]) for i in (1, 2, 3)]
+    back_parts[last], *back_hops[1:], up_other, down_other = tick(
+        back_parts[last], *back_hops[1:], up_other, down_other
+    )
     down_other = swap(down_other, "y")
-    mlp_parts = [fold_plane(item, "x") for item in mlp_parts]
-    back_parts[last], *back_hops[1:], mlp_parts[0], mlp_parts[1] = tick(
-        back_parts[last], *back_hops[1:], mlp_parts[0], mlp_parts[1]
-    )
     grad_normed_two = back_parts[last] + back_hops[1] + back_hops[2] + back_hops[3]
 
     grad_norm_two, grad_gain_two = rms_back(grad_normed_two, residual, scale_two, gain_two)
@@ -832,31 +852,43 @@
     grad_attended = dot(grad_branch, out_full, 1, 0).astype(BF)
     grad_slots = reorder(to_slots_kernel, place, grad_attended, (16, BLK, 128))
     pieces = send_hops(grad_slots.reshape(4, 2, 2, BLK, 128))
-    pieces, *mlp_parts = tick(pieces, *mlp_parts)
-    mlp_hops = [mlp_parts[0]] + [hop(item.astype(BF), j) for j, item in zip(ORDER[1:], mlp_parts[1:])]
+    pieces, mlp_hops[first], grad_branch, down_other, gate_other, up_other = tick(
+        pieces, mlp_hops[first], grad_branch, down_other, gate_other, up_other
+    )
+    gate_sum = (gate_own.astype(F32) + gate_other.astype(F32)).astype(BF)
+    up_sum = (up_own.astype(F32) + up_other.astype(F32)).astype(BF)
+    gate_step, up_step = ff_step(gate_sum, "x", 1), ff_step(up_sum, "z", 1)
+    branch_hops = [grad_branch] + [hop(grad_branch, j) for j in ORDER[1:]]
     pieces = send_core(send_plane(pieces, "y"))
     grad_proj = attend_back(place, saved, pieces, cosine, sine).reshape(16 * BLK, 384)
     back_parts = [fold_core(dot(grad_proj[j * quarter : (j + 1) * quarter], heads_qkv, 1, 0)) for j in range(4)]
     qkv_grad = dot(grad_proj, normed_all, 0, 0)
     qkv_own, qkv_other = split(qkv_grad.reshape(3, 2 * HD, width), 1, x)
-    tied = tick(*back_parts, qkv_other.astype(BF), grad_branch, gu_other, down_other, *mlp_hops)
-    back_parts, (qkv_other, grad_branch, gu_other, down_other), mlp_hops = list(tied[:4]), tied[4:8], tied[8:]
+    *back_parts, qkv_other, mlp_hops[second] = tick(*back_parts, qkv_other.astype(BF), mlp_hops[second])
     qkv_other = swap(qkv_other, "x")
     back_parts = [fold_plane(item, "y") for item in back_parts]
-    gu_moved = lax.ppermute((gu_own.astype(F32) + gu_other.astype(F32)).astype(BF), AXES, perm_of(ff_place))
-    down_moved = lax.ppermute((down_own.astype(F32) + down_other.astype(F32)).astype(BF), AXES, perm_of(ff_place))
-    branch_hops = [grad_branch] + [hop(grad_branch, j) for j in ORDER[1:]]
-    back_parts[first], branch_hops[1] = tick(back_parts[first], branch_hops[1])
+    down_sum = (down_own.astype(F32) + down_other.astype(F32)).astype(BF)
+    half = down_sum.shape[0] // 2
+    down_steps = [ff_step(down_sum[:half], "x", 1), ff_step(down_sum[half:], "z", 1)]
+    back_parts[first], branch_hops[1], branch_hops[2] = tick(back_parts[first], branch_hops[1], branch_hops[2])
     send_back(first)
-    back_parts[second], branch_hops[2], qkv_other = tick(back_parts[second], branch_hops[2], qkv_other)
+    back_parts[second], branch_hops[3], qkv_other, mlp_hops[third], gate_step, up_step = tick(
+        back_parts[second], branch_hops[3], qkv_other, mlp_hops[third], gate_step, up_step
+    )
     send_back(second)
+    gate_step, up_step = ff_step(gate_step, "z", 0), ff_step(up_step, "x", 0)
     qkv_moved = lax.ppermute((qkv_own + qkv_other.astype(F32)).astype(BF), AXES, perm_of(attn_place))
-    back_parts[third], branch_hops[3], down_moved = tick(back_parts[third], branch_hops[3], down_moved)
+    back_parts[third], back_parts[last], back_hops[first], down_steps[0], down_steps[1], *branch_hops = tick(
+        back_parts[third], back_parts[last], back_hops[first], *down_steps, *branch_hops
+    )
+    down_steps = [ff_step(down_steps[0], "z", 0), ff_step(down_steps[1], "x", 0)]
     send_back(third)
     branch_others = [swap(item, "y") for item in branch_hops]
+    branch_others[0], back_hops[second], mlp_parts[last], qkv_grad, gate_step, up_step = tick(
+        branch_others[0], back_hops[second], mlp_parts[last], qkv_grad, gate_step, up_step
+    )
     branch_chunks = [with_partner(*item) for item in zip(branch_hops, branch_others)]
-    back_hops[3], gu_moved, qkv_grad, *mlp_hops = tick(back_hops[3], gu_moved, qkv_grad, *mlp_hops)
-    mlp_term = mlp_hops[0] + sum(item.astype(F32) for item in mlp_hops[1:])
+    mlp_term = mlp_parts[last] + sum(item.astype(F32) for item in mlp_hops[1:])
     layer_out = (residual + mlp_term).astype(BF)
     gain_part = jnp.sum(qkv_grad * heads_qkv.astype(F32), axis=0) / gain_one
     low_chunks = low_slots.reshape(4, quarter, 128)
@@ -865,8 +897,9 @@
     grad_out_proj = move(out_own + swap(out_other.astype(BF), "x").astype(F32), attn_place)
     grad_normed_one = back_parts[last] + back_hops[1] + back_hops[2] + back_hops[3]
     grad_qkv = jnp.transpose(qkv_moved.astype(F32), (1, 0, 2))
-    grad_gate_up = jnp.transpose(gu_moved.astype(F32), (1, 0, 2))
-    grad_down = down_moved.astype(F32)
+    stays = x == z0
+    grad_gate_up = jnp.stack([jnp.where(stays, gate_sum, gate_step), jnp.where(stays, up_sum, up_step)], axis=1).astype(F32)
+    grad_down = jnp.where(stays, down_sum, jnp.concatenate(down_steps, axis=0)).astype(F32)
 
     weighted = grad_normed_one * gain_one
     inner_mean = jnp.mean(weighted * inputs, axis=-1, keepdims=True)

time: 780 us -> 731 us (0.937)
  waiting for transfers between devices: 355 us -> 260 us
  other arithmetic: 61.6 us -> 83.3 us
  local copies, waits for them, and re-layouts: 74.4 us -> 91.8 us
  starting transfers between devices: 153 us -> 162 us
    ppermute x72 -> x74, waiting for transfers between devices: 223 us -> 178 us  [swap(): return lax.ppermute(value, axis, PAIR)]
    ppermute x30, waiting for transfers between devices: 95.8 us -> 61.6 us  [hop(): return lax.ppermute(value, 'z', [(i, i ^ dist) for i in range(4)])]
    unnamed x207 -> x229, local copies, waits for them, and re-layouts: 35.1 us -> 47.3 us
    add x12, other arithmetic: 6.61 us -> 18.5 us  [fold_core(): return part[:n].astype(F32) + swap(part[n:].astype(BF), 'c').astype(F32)]
    ppermute x4, waiting for transfers between devices: 15.7 us -> 4.97 us  [to_y(): return lax.ppermute(value, ('y', 'z'), y_pairs)]
    ppermute x72 -> x74, starting transfers between devices: 62.6 us -> 60.2 us  [swap(): return lax.ppermute(value, axis, PAIR)]
  transfers between devices with their start and end apart: 111 -> 119, of which waited for: 51 -> 41; matrix products, arithmetic and copies ran while one was open for 26% -> 34% of each run, Pallas kernels for 4% -> 4%
where the time goes in v3:
time: 731 us; the launch traced here: 719 us
  waiting for transfers between devices  260 us (36%)
  starting transfers between devices  162 us (22%)
  local copies, waits for them, and re-layouts  91.8 us (13%)
  matrix products  86.4 us (12%)
  other arithmetic  83.3 us (11%)
  Pallas kernels  31.7 us (4%)
    ppermute x74, waiting for transfers between devices, swap(): return lax.ppermute(value, axis, PAIR)  178 us
    dot_general x48, matrix products, dot(): lax.dot_general(left, right, (((left_dim,), (right_dim,)), ((), ())), pre...  86.4 us
    ppermute x30, starting transfers between devices, hop(): return lax.ppermute(value, 'z', [(i, i ^ dist) for i in range(4)])  74.9 us
    ppermute x30, waiting for transfers between devices, hop(): return lax.ppermute(value, 'z', [(i, i ^ dist) for i in range(4)])  61.6 us
    ppermute x74, starting transfers between devices, swap(): return lax.ppermute(value, axis, PAIR)  60.2 us
    unnamed x229, local copies, waits for them, and re-layouts  47.3 us
    add x12, other arithmetic, fold_core(): return part[:n].astype(F32) + swap(part[n:].astype(BF), 'c').astype(F32)  18.5 us
  transfers between devices with their start and end apart: 119, of which 41 were waited for; matrix products, arithmetic and copies ran while one was open for 34% of the time, Pallas kernels for 4%

profile of v3, /device:TPU:6, one launch (start us, length us, event | category | flops | bytes accessed | tf_op | source)
XLA Modules:
  0.0 718.5 jit_solution(5679298726361640428)
XLA Ops:
  14.2 10.6 %constant_dynamic-slice_fusion.18 = (bf16[256,1,2048]{2,1,0:T(2,128)(2,1)}, bf16[256,1,2048]{2,1,0:T(2,128)(2,1)}, bf16[256,1,2048]{2,1,0:T(2,128)(2,1)}, bf16[256,1,2048]{2,1,0:T(2,128)(2,1)}) fusion(bf16[2048,2,2048]{2,1,0:T(2,128)(2,1)} %param.13, s32[]{:T(128)S(6)} %select_n.135, s32[]{:T(128)S(6)} %add.494, s32[]{:T(128)S(6)} %select_n.134), kind=kLoop, calls=%fused_computation.248 | loop fusion | bytes 8388620 | tf_op jit(solution)/shard_map/slice | solution.py:714
  47.3 8.4 %collective-permute-done.6 = bf16[128,2048]{1,0:T(8,128)(2,1)} collective-permute-done((bf16[128,2048]{1,0:T(8,128)(2,1)S(1)}, bf16[128,2048]{1,0:T(8,128)(2,1)}, u32[]{:S(2)}, u32[]{:S(2)}) %collective-permute-start.6) | collective-permute-done | bytes 524320 | tf_op jit(solution)/shard_map/ppermute | solution.py:361
  66.6 10.7 %collective-permute-done.10 = bf16[128,2048]{1,0:T(8,128)(2,1)S(1)} collective-permute-done((bf16[128,2048]{1,0:T(8,128)(2,1)S(1)}, bf16[128,2048]{1,0:T(8,128)(2,1)S(1)}, u32[]{:S(2)}, u32[]{:S(2)}) %collective-permute-start.10) | collective-permute-done | bytes 524320 | tf_op jit(solution)/shard_map/ppermute | solution.py:361
  85.2 4.2 collective-permute-start.14
  93.4 6.9 fusion.75
  100.3 5.2 attend.1
  107.7 7.2 collective-permute-done.16
  121.8 7.0 collective-permute-done.17
  128.8 4.8 collective-permute-done.18
  133.7 9.9 %collective-permute-start.19 = (bf16[2,2,128,128]{3,2,0,1:T(8,128)(2,1)S(1)}, bf16[2,2,128,128]{3,2,0,1:T(8,128)(2,1)S(1)}, u32[]{:S(2)}, u32[]{:S(2)}) collective-permute-start(bf16[2,2,128,128]{3,2,0,1:T(8,128)(2,1)S(1)} %get-tuple-element.347), channel_id=1, source_target_pairs={{0,2},{2,0},{4,6},{6,4},{1,3},{3,1},{5,7},{7,5},{8,10},{10,8},{12,... | collective-permute-start | bytes 393224 | tf_op jit(solution)/shard_map/ppermute | solution.py:365
  147.2 4.0 collective-permute-start.21
  153.5 4.1 collective-permute-done.21
  158.4 4.0 collective-permute-done.22.far
  169.9 5.7 collective-permute-start.26
  175.6 8.2 %join_out.1 = bf16[2048,2048]{1,0:T(8,128)(2,1)} custom-call(s32[4]{0:T(128)} %copy-done.8, bf16[1024,1024]{1,0:T(8,128)(2,1)} %copy-done.39, bf16[1024,1024]{1,0:T(8,128)(2,1)} %collective-permute-done.22.far, bf16[1024,1024]{1,0:T(8,128)(2,1)} %copy-done.59, bf16[1024,1024]{1,0:T(8,128)(2,1)} %collective-permute-done.25.far_c), custom_call_target="tpu_custom_call" | custom-call | bytes 1048576 | tf_op jit(solution)/shard_map/join_out/pallas_call | solution.py:589
  183.8 6.6 multiply_reduce_fusion.3
  190.7 8.8 %collective-permute-done.26 = bf16[128,2048]{1,0:T(8,128)(2,1)} collective-permute-done((bf16[128,2048]{1,0:T(8,128)(2,1)}, bf16[128,2048]{1,0:T(8,128)(2,1)}, u32[]{:S(2)}, u32[]{:S(2)}) %collective-permute-start.26) | collective-permute-done | bytes 524320 | tf_op jit(solution)/shard_map/ppermute | solution.py:365
  217.6 8.9 %collective-permute-done.39 = bf16[128,2048]{1,0:T(8,128)(2,1)S(1)} collective-permute-done((bf16[128,2048]{1,0:T(8,128)(2,1)S(1)}, bf16[128,2048]{1,0:T(8,128)(2,1)S(1)}, u32[]{:S(2)}, u32[]{:S(2)}) %collective-permute-start.39) | collective-permute-done | bytes 524320 | tf_op jit(solution)/shard_map/ppermute | solution.py:365
  229.2 4.5 order_rows.1
  245.9 3.8 fusion.76
  254.3 10.5 %collective-permute-done.44 = bf16[128,2048]{1,0:T(8,128)(2,1)S(1)} collective-permute-done((bf16[128,2048]{1,0:T(8,128)(2,1)}, bf16[128,2048]{1,0:T(8,128)(2,1)S(1)}, u32[]{:S(2)}, u32[]{:S(2)}) %collective-permute-start.44) | collective-permute-done | bytes 524320 | tf_op jit(solution)/shard_map/ppermute | solution.py:361
  267.9 7.5 %collective-permute-done.36 = bf16[128,2048]{1,0:T(8,128)(2,1)S(1)} collective-permute-done((bf16[128,2048]{1,0:T(8,128)(2,1)S(1)}, bf16[128,2048]{1,0:T(8,128)(2,1)S(1)}, u32[]{:S(2)}, u32[]{:S(2)}) %collective-permute-start.36) | collective-permute-done | bytes 524320 | tf_op jit(solution)/shard_map/ppermute | solution.py:361
  285.9 4.3 collective-permute-done.47
  290.4 9.5 %collective-permute-done.37 = bf16[128,2048]{1,0:T(8,128)(2,1)S(1)} collective-permute-done((bf16[128,2048]{1,0:T(8,128)(2,1)}, bf16[128,2048]{1,0:T(8,128)(2,1)S(1)}, u32[]{:S(2)}, u32[]{:S(2)}) %collective-permute-start.37) | collective-permute-done | bytes 524320 | tf_op jit(solution)/shard_map/ppermute | solution.py:361
  303.9 5.0 collective-permute-done.42
  365.3 4.1 add_convert_fusion.2
  401.8 4.2 collective-permute-done.58
  409.0 10.1 %collective-permute-done.60 = bf16[256,2048]{1,0:T(8,128)(2,1)S(1)} collective-permute-done((bf16[256,2048]{1,0:T(8,128)(2,1)}, bf16[256,2048]{1,0:T(8,128)(2,1)S(1)}, u32[]{:S(2)}, u32[]{:S(2)}) %collective-permute-start.60) | collective-permute-done | bytes 1048608 | tf_op jit(solution)/shard_map/ppermute | solution.py:361
  432.4 4.6 collective-permute-done.61
  441.5 7.7 %collective-permute-done.67 = bf16[256,2048]{1,0:T(8,128)(2,1)S(1)} collective-permute-done((bf16[256,2048]{1,0:T(8,128)(2,1)S(1)}, bf16[256,2048]{1,0:T(8,128)(2,1)S(1)}, u32[]{:S(2)}, u32[]{:S(2)}) %collective-permute-start.67) | collective-permute-done | bytes 1048608 | tf_op jit(solution)/shard_map/ppermute | solution.py:361
  460.1 4.4 collective-permute-start.69
  470.4 4.3 collective-permute-start.79
  477.3 4.0 collective-permute-done.73
  483.6 9.9 %attend_back.1 = bf16[4,2,2,128,384]{4,3,2,1,0:T(8,128)(2,1)S(1)} custom-call(s32[4]{0:T(128)S(1)} %copy-done.9, bf16[2,1024,128]{2,1,0:T(8,128)(2,1)S(1)} %get-tuple-element.170.q_ref, bf16[2,1024,128]{2,1,0:T(8,128)(2,1)S(1)} %copy-done.5, bf16[2,1024,128]{2,1,0:T(8,128)(2,1)S(1)} %copy-done.7, f32[2,1024,128]{2,1,0:T(8,128)S(1)} %get-tuple-element.173.att_ref, ...), custom_call_target="tpu_custom_call" | custom-call | bytes 1048576 | tf_op jit(solution)/shard_map/attend_back/pallas_call | solution.py:540
  518.9 3.7 collective-permute-done.84
  522.6 9.9 %collective-permute-start.89 = (bf16[128,2048]{1,0:T(8,128)(2,1)S(1)}, bf16[128,2048]{1,0:T(8,128)(2,1)S(1)}, u32[]{:S(2)}, u32[]{:S(2)}) collective-permute-start(bf16[128,2048]{1,0:T(8,128)(2,1)S(1)} %get-tuple-element.261), channel_id=1, source_target_pairs={{0,4},{2,6},{4,0},{6,2},{1,5},{3,7},{5,1},{7,3},{8,12},{10,14},{12... | collective-permute-start | bytes 1572872 | tf_op jit(solution)/shard_map/ppermute | solution.py:365
  533.2 4.9 collective-permute-done.82
  539.6 15.7 %collective-permute-done.89 = bf16[128,2048]{1,0:T(8,128)(2,1)S(1)} collective-permute-done((bf16[128,2048]{1,0:T(8,128)(2,1)S(1)}, bf16[128,2048]{1,0:T(8,128)(2,1)S(1)}, u32[]{:S(2)}, u32[]{:S(2)}) %collective-permute-start.89) | collective-permute-done | bytes 524320 | tf_op jit(solution)/shard_map/ppermute | solution.py:365
  563.3 22.4 %collective-permute-done.90 = bf16[3,64,2048]{2,1,0:T(8,128)(2,1)S(1)} collective-permute-done((bf16[3,64,2048]{2,1,0:T(8,128)(2,1)S(1)}, bf16[3,64,2048]{2,1,0:T(8,128)(2,1)S(1)}, u32[]{:S(2)}, u32[]{:S(2)}) %collective-permute-start.90) | collective-permute-done | bytes 786464 | tf_op jit(solution)/shard_map/ppermute | solution.py:361
  587.4 5.4 collective-permute-start.107
  597.1 6.5 collective-permute-done.109
  606.3 22.5 %collective-permute-done.111 = bf16[128,2048]{1,0:T(8,128)(2,1)S(1)} collective-permute-done((bf16[128,2048]{1,0:T(8,128)(2,1)S(1)}, bf16[128,2048]{1,0:T(8,128)(2,1)S(1)}, u32[]{:S(2)}, u32[]{:S(2)}) %collective-permute-start.111) | collective-permute-done | bytes 524320 | tf_op jit(solution)/shard_map/ppermute | solution.py:361
  630.3 6.5 collective-permute-done.113
  644.3 9.7 %collective-permute-start.95 = (bf16[128,2048]{1,0:T(8,128)(2,1)S(1)}, bf16[128,2048]{1,0:T(8,128)(2,1)S(1)}, u32[]{:S(2)}, u32[]{:S(2)}) collective-permute-start(bf16[128,2048]{1,0:T(8,128)(2,1)S(1)} %get-tuple-element.261), channel_id=1, source_target_pairs={{0,16},{16,0},{1,17},{17,1},{2,18},{18,2},{3,19},{19,3},{4,20},{20... | collective-permute-start | bytes 1572872 | tf_op jit(solution)/shard_map/ppermute | solution.py:361
  655.5 5.6 collective-permute-done.96
  678.6 5.2 copy.45
  694.7 7.0 collective-permute-done.115
  704.3 13.0 %collective-permute-done.116 = bf16[2048,64]{0,1:T(8,128)(2,1)S(1)} collective-permute-done((bf16[2048,64]{0,1:T(8,128)(2,1)S(1)}, bf16[2048,64]{0,1:T(8,128)(2,1)S(1)}, u32[]{:S(2)}, u32[]{:S(2)}) %collective-permute-start.116) | collective-permute-done | bytes 262176 | tf_op jit(solution)/shard_map/ppermute | solution.py:670
  (633 shorter events, 353.2 us)
Async XLA Ops:
  7.6 26.8 %collective-permute-start.5 = (bf16[128,2048]{1,0:T(8,128)(2,1)}, bf16[128,2048]{1,0:T(8,128)(2,1)S(1)}, u32[]{:S(2)}, u32[]{:S(2)}) collective-permute-start(bf16[128,2048]{1,0:T(8,128)(2,1)} %get-tuple-element.306), channel_id=1, source_target_pairs={{0,6},{2,4},{4,2},{6,0},{1,7},{3,5},{5,3},{7,1},{8,14},{10,12},{12... | collective-permute-start | bytes 1572872 | tf_op jit(solution)/shard_map/ppermute | solution.py:365
  10.0 53.0 %collective-permute-start.8 = (bf16[128,2048]{1,0:T(8,128)(2,1)}, bf16[128,2048]{1,0:T(8,128)(2,1)S(1)}, u32[]{:S(2)}, u32[]{:S(2)}) collective-permute-start(bf16[128,2048]{1,0:T(8,128)(2,1)} %get-tuple-element.306), channel_id=1, source_target_pairs={{0,4},{2,6},{4,0},{6,2},{1,5},{3,7},{5,1},{7,3},{8,12},{10,14},{12... | collective-permute-start | bytes 1572872 | tf_op jit(solution)/shard_map/ppermute | solution.py:365
  12.9 50.1 %collective-permute-start.9 = (bf16[384,2048]{1,0:T(8,128)(2,1)}, bf16[384,2048]{1,0:T(8,128)(2,1)}, u32[]{:S(2)}, u32[]{:S(2)}) collective-permute-start(bf16[384,2048]{1,0:T(8,128)(2,1)} %bitcast.3), channel_id=1, source_target_pairs={{0,8},{10,2},{4,12},{14,6},{1,9},{11,3},{5,13},{15,7},{16,24},{26,... | collective-permute-start | bytes 4718600 | tf_op jit(solution)/shard_map/ppermute | solution.py:698
  29.8 27.1 %collective-permute-start.1 = (bf16[256,2048]{1,0:T(8,128)(2,1)}, bf16[256,2048]{1,0:T(8,128)(2,1)}, u32[]{:S(2)}, u32[]{:S(2)}) collective-permute-start(bf16[256,2048]{1,0:T(8,128)(2,1)} %pad_maximum_fusion.5), channel_id=1, source_target_pairs={{0,1},{1,0},{2,3},{3,2},{4,5},{5,4},{6,7},{7,6},{8,9},{9,8},{10,11... | collective-permute-start | bytes 3145736 | tf_op jit(solution)/shard_map/ppermute | solution.py:361
  47.2 30.3 %collective-permute-start.4 = (bf16[256,2048]{1,0:T(8,128)(2,1)S(1)}, bf16[256,2048]{1,0:T(8,128)(2,1)S(1)}, u32[]{:S(2)}, u32[]{:S(2)}) collective-permute-start(bf16[256,2048]{1,0:T(8,128)(2,1)S(1)} %pad_maximum_fusion.6), channel_id=1, source_target_pairs={{0,1},{1,0},{2,3},{3,2},{4,5},{5,4},{6,7},{7,6},{8,9},{9,8},{10,11... | collective-permute-start | bytes 3145736 | tf_op jit(solution)/shard_map/ppermute | solution.py:361
  56.8 24.5 %collective-permute-start.7 = (bf16[256,2048]{1,0:T(8,128)(2,1)S(1)}, bf16[256,2048]{1,0:T(8,128)(2,1)S(1)}, u32[]{:S(2)}, u32[]{:S(2)}) collective-permute-start(bf16[256,2048]{1,0:T(8,128)(2,1)S(1)} %pad_maximum_fusion.7), channel_id=1, source_target_pairs={{0,1},{1,0},{2,3},{3,2},{4,5},{5,4},{6,7},{7,6},{8,9},{9,8},{10,11... | collective-permute-start | bytes 3145736 | tf_op jit(solution)/shard_map/ppermute | solution.py:361
  89.8 25.5 %collective-permute-start.13 = (bf16[512,1024]{1,0:T(8,128)(2,1)}, bf16[512,1024]{1,0:T(8,128)(2,1)S(1)}, u32[]{:S(2)}, u32[]{:S(2)}) collective-permute-start(bf16[512,1024]{1,0:T(8,128)(2,1)} %constant_dynamic-slice_fusion.17), channel_id=1, source_target_pairs={{0,16},{16,0},{1,17},{17,1},{2,18},{18,2},{3,19},{19,3},{4,20},{20... | collective-permute-start | bytes 3145736 | tf_op jit(solution)/shard_map/ppermute | solution.py:361
  115.4 47.1 %collective-permute-start.22 = (bf16[1024,1024]{1,0:T(8,128)(2,1)S(1)}, bf16[1024,1024]{1,0:T(8,128)(2,1)}, u32[]{:S(2)}, u32[]{:S(2)}) collective-permute-start(bf16[1024,1024]{1,0:T(8,128)(2,1)S(1)} %constant_dynamic-update-slice_fusion.12.pair), channel_id=1, source_target_pairs={{0,8},{8,0},{1,9},{9,1},{2,10},{10,2},{3,11},{11,3},{4,12},{12,4},... | collective-permute-start | bytes 6291464 | tf_op jit(solution)/shard_map/ppermute | solution.py:361
  117.2 45.3 %collective-permute-start.24 = (bf16[1024,1024]{1,0:T(8,128)(2,1)S(1)}, bf16[1024,1024]{1,0:T(8,128)(2,1)S(1)}, u32[]{:S(2)}, u32[]{:S(2)}) collective-permute-start(bf16[1024,1024]{1,0:T(8,128)(2,1)S(1)} %constant_dynamic-update-slice_fusion.12.pair), channel_id=1, source_target_pairs={{0,1},{1,0},{2,3},{3,2},{4,5},{5,4},{6,7},{7,6},{8,9},{9,8},{10,11... | collective-permute-start | bytes 6291464 | tf_op jit(solution)/shard_map/ppermute | solution.py:361
  121.2 37.3 %collective-permute-start.23 = (bf16[1024,512]{1,0:T(8,128)(2,1)S(1)}, bf16[1024,512]{1,0:T(8,128)(2,1)S(1)}, u32[]{:S(2)}, u32[]{:S(2)}) collective-permute-start(bf16[1024,512]{1,0:T(8,128)(2,1)S(1)} %constant_dynamic-update-slice_fusion.14), channel_id=1, source_target_pairs={{0,16},{16,0},{1,17},{17,1},{2,18},{18,2},{3,19},{19,3},{4,20},{20... | collective-permute-start | bytes 3145736 | tf_op jit(solution)/shard_map/ppermute | solution.py:361
  168.5 31.0 %collective-permute-start.27 = (bf16[256,2048]{1,0:T(8,128)(2,1)}, bf16[256,2048]{1,0:T(8,128)(2,1)}, u32[]{:S(2)}, u32[]{:S(2)}) collective-permute-start(bf16[256,2048]{1,0:T(8,128)(2,1)} %bitcast.181), channel_id=1, source_target_pairs={{0,16},{2,18},{20,4},{22,6},{1,17},{3,19},{21,5},{23,7},{8,24},{10... | collective-permute-start | bytes 3145736 | tf_op jit(solution)/shard_map/ppermute | solution.py:718
  169.9 29.6 %collective-permute-start.26 = (bf16[128,2048]{1,0:T(8,128)(2,1)}, bf16[128,2048]{1,0:T(8,128)(2,1)}, u32[]{:S(2)}, u32[]{:S(2)}) collective-permute-start(bf16[128,2048]{1,0:T(8,128)(2,1)} %bitcast.15), channel_id=1, source_target_pairs={{0,4},{2,6},{4,0},{6,2},{1,5},{3,7},{5,1},{7,3},{8,12},{10,14},{12... | collective-permute-start | bytes 1572872 | tf_op jit(solution)/shard_map/ppermute | solution.py:365
  199.5 39.0 %collective-permute-start.32 = (bf16[128,2048]{1,0:T(8,128)(2,1)S(1)}, bf16[128,2048]{1,0:T(8,128)(2,1)}, u32[]{:S(2)}, u32[]{:S(2)}) collective-permute-start(bf16[128,2048]{1,0:T(8,128)(2,1)S(1)} %multiply_convert_fusion.12), channel_id=1, source_target_pairs={{0,2},{2,0},{4,6},{6,4},{1,3},{3,1},{5,7},{7,5},{8,10},{10,8},{12,... | collective-permute-start | bytes 1572872 | tf_op jit(solution)/shard_map/ppermute | solution.py:365
  200.1 26.4 %collective-permute-start.39 = (bf16[128,2048]{1,0:T(8,128)(2,1)S(1)}, bf16[128,2048]{1,0:T(8,128)(2,1)S(1)}, u32[]{:S(2)}, u32[]{:S(2)}) collective-permute-start(bf16[128,2048]{1,0:T(8,128)(2,1)S(1)} %multiply_convert_fusion.12), channel_id=1, source_target_pairs={{0,4},{2,6},{4,0},{6,2},{1,5},{3,7},{5,1},{7,3},{8,12},{10,14},{12... | collective-permute-start | bytes 1572872 | tf_op jit(solution)/shard_map/ppermute | solution.py:365
  203.5 31.4 %collective-permute-start.29 = (bf16[128,2048]{1,0:T(8,128)(2,1)S(1)}, bf16[128,2048]{1,0:T(8,128)(2,1)}, u32[]{:S(2)}, u32[]{:S(2)}) collective-permute-start(bf16[128,2048]{1,0:T(8,128)(2,1)S(1)} %multiply_convert_fusion.12), channel_id=1, source_target_pairs={{0,8},{8,0},{1,9},{9,1},{2,10},{10,2},{3,11},{11,3},{4,12},{12,4},... | collective-permute-start | bytes 1572872 | tf_op jit(solution)/shard_map/ppermute | solution.py:361
  204.1 35.3 %collective-permute-start.33 = (bf16[256,2048]{1,0:T(8,128)(2,1)}, bf16[256,2048]{1,0:T(8,128)(2,1)}, u32[]{:S(2)}, u32[]{:S(2)}) collective-permute-start(bf16[256,2048]{1,0:T(8,128)(2,1)} %bitcast.167), channel_id=1, source_target_pairs={{0,16},{2,18},{20,4},{22,6},{1,17},{3,19},{21,5},{23,7},{8,24},{10... | collective-permute-start | bytes 3145736 | tf_op jit(solution)/shard_map/ppermute | solution.py:718
  205.4 33.4 %collective-permute-start.34 = (bf16[128,2048]{1,0:T(8,128)(2,1)}, bf16[128,2048]{1,0:T(8,128)(2,1)}, u32[]{:S(2)}, u32[]{:S(2)}) collective-permute-start(bf16[128,2048]{1,0:T(8,128)(2,1)} %collective-permute-done.14), channel_id=1, source_target_pairs={{0,8},{8,0},{1,9},{9,1},{2,10},{10,2},{3,11},{11,3},{4,12},{12,4},... | collective-permute-start | bytes 1572872 | tf_op jit(solution)/shard_map/ppermute | solution.py:361
  234.9 32.9 %collective-permute-start.31 = (bf16[128,2048]{1,0:T(8,128)(2,1)S(1)}, bf16[128,2048]{1,0:T(8,128)(2,1)S(1)}, u32[]{:S(2)}, u32[]{:S(2)}) collective-permute-start(bf16[128,2048]{1,0:T(8,128)(2,1)S(1)} %multiply_convert_fusion.12), channel_id=1, source_target_pairs={{0,6},{2,4},{4,2},{6,0},{1,7},{3,5},{5,3},{7,1},{8,14},{10,12},{12... | collective-permute-start | bytes 1572872 | tf_op jit(solution)/shard_map/ppermute | solution.py:365
  238.5 27.5 %collective-permute-start.30 = (bf16[256,2048]{1,0:T(8,128)(2,1)S(1)}, bf16[256,2048]{1,0:T(8,128)(2,1)S(1)}, u32[]{:S(2)}, u32[]{:S(2)}) collective-permute-start(bf16[256,2048]{1,0:T(8,128)(2,1)S(1)} %pad_maximum_fusion.10), channel_id=1, source_target_pairs={{0,1},{1,0},{2,3},{3,2},{4,5},{5,4},{6,7},{7,6},{8,9},{9,8},{10,11... | collective-permute-start | bytes 3145736 | tf_op jit(solution)/shard_map/ppermute | solution.py:361
  239.4 36.0 %collective-permute-start.35 = (bf16[256,2048]{1,0:T(8,128)(2,1)S(1)}, bf16[256,2048]{1,0:T(8,128)(2,1)S(1)}, u32[]{:S(2)}, u32[]{:S(2)}) collective-permute-start(bf16[256,2048]{1,0:T(8,128)(2,1)S(1)} %bitcast.179), channel_id=1, source_target_pairs={{0,16},{2,18},{20,4},{22,6},{1,17},{3,19},{21,5},{23,7},{8,24},{10... | collective-permute-start | bytes 3145736 | tf_op jit(solution)/shard_map/ppermute | solution.py:718
  267.9 33.3 %collective-permute-start.45 = (bf16[256,2048]{1,0:T(8,128)(2,1)S(1)}, bf16[256,2048]{1,0:T(8,128)(2,1)S(1)}, u32[]{:S(2)}, u32[]{:S(2)}) collective-permute-start(bf16[256,2048]{1,0:T(8,128)(2,1)S(1)} %pad_maximum_fusion.13), channel_id=1, source_target_pairs={{0,1},{1,0},{2,3},{3,2},{4,5},{5,4},{6,7},{7,6},{8,9},{9,8},{10,11... | collective-permute-start | bytes 3145736 | tf_op jit(solution)/shard_map/ppermute | solution.py:361
  282.7 26.1 %collective-permute-start.42 = (bf16[256,2048]{1,0:T(8,128)(2,1)S(1)}, bf16[256,2048]{1,0:T(8,128)(2,1)S(1)}, u32[]{:S(2)}, u32[]{:S(2)}) collective-permute-start(bf16[256,2048]{1,0:T(8,128)(2,1)S(1)} %bitcast.177), channel_id=1, source_target_pairs={{0,16},{2,18},{20,4},{22,6},{1,17},{3,19},{21,5},{23,7},{8,24},{10... | collective-permute-start | bytes 3145736 | tf_op jit(solution)/shard_map/ppermute | solution.py:718
  335.9 41.0 %collective-permute-start.53 = (bf16[256,2048]{1,0:T(8,128)(2,1)}, bf16[256,2048]{1,0:T(8,128)(2,1)}, u32[]{:S(2)}, u32[]{:S(2)}) collective-permute-start(bf16[256,2048]{1,0:T(8,128)(2,1)} %slice.496), channel_id=1, source_target_pairs={{0,1},{1,0},{2,3},{3,2},{4,5},{5,4},{6,7},{7,6},{8,9},{9,8},{10,11... | collective-permute-start | bytes 3145736 | tf_op jit(solution)/shard_map/ppermute | solution.py:361
  338.3 49.7 %collective-permute-start.59 = (bf16[256,2048]{1,0:T(8,128)(2,1)}, bf16[256,2048]{1,0:T(8,128)(2,1)}, u32[]{:S(2)}, u32[]{:S(2)}) collective-permute-start(bf16[256,2048]{1,0:T(8,128)(2,1)} %slice.493), channel_id=1, source_target_pairs={{0,1},{1,0},{2,3},{3,2},{4,5},{5,4},{6,7},{7,6},{8,9},{9,8},{10,11... | collective-permute-start | bytes 3145736 | tf_op jit(solution)/shard_map/ppermute | solution.py:361
  365.3 29.6 %collective-permute-start.62 = (bf16[256,2048]{1,0:T(8,128)(2,1)}, bf16[256,2048]{1,0:T(8,128)(2,1)}, u32[]{:S(2)}, u32[]{:S(2)}) collective-permute-start(bf16[256,2048]{1,0:T(8,128)(2,1)} %slice.492), channel_id=1, source_target_pairs={{0,1},{1,0},{2,3},{3,2},{4,5},{5,4},{6,7},{7,6},{8,9},{9,8},{10,11... | collective-permute-start | bytes 3145736 | tf_op jit(solution)/shard_map/ppermute | solution.py:361
  370.6 36.7 %collective-permute-start.57 = (bf16[256,2048]{1,0:T(8,128)(2,1)}, bf16[256,2048]{1,0:T(8,128)(2,1)}, u32[]{:S(2)}, u32[]{:S(2)}) collective-permute-start(bf16[256,2048]{1,0:T(8,128)(2,1)} %slice.494), channel_id=1, source_target_pairs={{0,1},{1,0},{2,3},{3,2},{4,5},{5,4},{6,7},{7,6},{8,9},{9,8},{10,11... | collective-permute-start | bytes 3145736 | tf_op jit(solution)/shard_map/ppermute | solution.py:361
  374.6 65.7 %collective-permute-start.65 = (bf16[128,2048]{1,0:T(8,128)(2,1)}, bf16[128,2048]{1,0:T(8,128)(2,1)}, u32[]{:S(2)}, u32[]{:S(2)}) collective-permute-start(bf16[128,2048]{1,0:T(8,128)(2,1)} %convert_add_fusion.12), channel_id=1, source_target_pairs={{0,6},{2,4},{4,2},{6,0},{1,7},{3,5},{5,3},{7,1},{8,14},{10,12},{12... | collective-permute-start | bytes 1572872 | tf_op jit(solution)/shard_map/ppermute | solution.py:365
  394.9 24.2 %collective-permute-start.60 = (bf16[256,2048]{1,0:T(8,128)(2,1)}, bf16[256,2048]{1,0:T(8,128)(2,1)S(1)}, u32[]{:S(2)}, u32[]{:S(2)}) collective-permute-start(bf16[256,2048]{1,0:T(8,128)(2,1)} %constant_dynamic-slice_fusion.12), channel_id=1, source_target_pairs={{0,16},{16,0},{1,17},{17,1},{2,18},{18,2},{3,19},{19,3},{4,20},{20... | collective-permute-start | bytes 3145736 | tf_op jit(solution)/shard_map/ppermute | solution.py:361
  399.6 41.8 %collective-permute-start.66 = (bf16[128,2048]{1,0:T(8,128)(2,1)S(1)}, bf16[128,2048]{1,0:T(8,128)(2,1)}, u32[]{:S(2)}, u32[]{:S(2)}) collective-permute-start(bf16[128,2048]{1,0:T(8,128)(2,1)S(1)} %copy-done.83), channel_id=1, source_target_pairs={{0,4},{2,6},{4,0},{6,2},{1,5},{3,7},{5,1},{7,3},{8,12},{10,14},{12... | collective-permute-start | bytes 1572872 | tf_op jit(solution)/shard_map/ppermute | solution.py:365
  437.0 37.8 %collective-permute-start.71 = (bf16[128,2048]{1,0:T(8,128)(2,1)}, bf16[128,2048]{1,0:T(8,128)(2,1)}, u32[]{:S(2)}, u32[]{:S(2)}) collective-permute-start(bf16[128,2048]{1,0:T(8,128)(2,1)} %convert_add_fusion.10), channel_id=1, source_target_pairs={{0,6},{2,4},{4,2},{6,0},{1,7},{3,5},{5,3},{7,1},{8,14},{10,12},{12... | collective-permute-start | bytes 1572872 | tf_op jit(solution)/shard_map/ppermute | solution.py:365
  467.8 47.2 %collective-permute-start.92 = (bf16[128,2048]{1,0:T(8,128)(2,1)}, bf16[128,2048]{1,0:T(8,128)(2,1)}, u32[]{:S(2)}, u32[]{:S(2)}) collective-permute-start(bf16[128,2048]{1,0:T(8,128)(2,1)} %add_convert_fusion.8), channel_id=1, source_target_pairs={{0,2},{2,0},{4,6},{6,4},{1,3},{3,1},{5,7},{7,5},{8,10},{10,8},{12,... | collective-permute-start | bytes 1572872 | tf_op jit(solution)/shard_map/ppermute | solution.py:365
  470.4 41.5 %collective-permute-start.79 = (bf16[128,2048]{1,0:T(8,128)(2,1)}, bf16[128,2048]{1,0:T(8,128)(2,1)}, u32[]{:S(2)}, u32[]{:S(2)}) collective-permute-start(bf16[128,2048]{1,0:T(8,128)(2,1)} %convert_add_fusion.7), channel_id=1, source_target_pairs={{0,4},{2,6},{4,0},{6,2},{1,5},{3,7},{5,1},{7,3},{8,12},{10,14},{12... | collective-permute-start | bytes 1572872 | tf_op jit(solution)/shard_map/ppermute | solution.py:365
  475.5 42.6 %collective-permute-start.83 = (bf16[128,2048]{1,0:T(8,128)(2,1)S(1)}, bf16[128,2048]{1,0:T(8,128)(2,1)}, u32[]{:S(2)}, u32[]{:S(2)}) collective-permute-start(bf16[128,2048]{1,0:T(8,128)(2,1)S(1)} %get-tuple-element.261), channel_id=1, source_target_pairs={{0,2},{2,0},{4,6},{6,4},{1,3},{3,1},{5,7},{7,5},{8,10},{10,8},{12,... | collective-permute-start | bytes 1572872 | tf_op jit(solution)/shard_map/ppermute | solution.py:365
  510.1 46.5 %collective-permute-start.94 = (bf16[256,2048]{1,0:T(8,128)(2,1)S(1)}, bf16[256,2048]{1,0:T(8,128)(2,1)S(1)}, u32[]{:S(2)}, u32[]{:S(2)}) collective-permute-start(bf16[256,2048]{1,0:T(8,128)(2,1)S(1)} %add_convert_fusion.3), channel_id=1, source_target_pairs={{2,0},{3,1},{6,4},{7,5},{8,10},{9,11},{12,14},{13,15},{18,16},{19,... | collective-permute-start | bytes 3145736 | tf_op jit(solution)/shard_map/ppermute | solution.py:676
  515.1 42.8 %collective-permute-start.93 = (bf16[256,2048]{1,0:T(8,128)(2,1)S(1)}, bf16[256,2048]{1,0:T(8,128)(2,1)S(1)}, u32[]{:S(2)}, u32[]{:S(2)}) collective-permute-start(bf16[256,2048]{1,0:T(8,128)(2,1)S(1)} %add_convert_fusion.4), channel_id=1, source_target_pairs={{2,10},{3,11},{6,14},{7,15},{8,0},{9,1},{12,4},{13,5},{18,26},{19,... | collective-permute-start | bytes 3145736 | tf_op jit(solution)/shard_map/ppermute | solution.py:676
  522.6 32.7 %collective-permute-start.89 = (bf16[128,2048]{1,0:T(8,128)(2,1)S(1)}, bf16[128,2048]{1,0:T(8,128)(2,1)S(1)}, u32[]{:S(2)}, u32[]{:S(2)}) collective-permute-start(bf16[128,2048]{1,0:T(8,128)(2,1)S(1)} %get-tuple-element.261), channel_id=1, source_target_pairs={{0,4},{2,6},{4,0},{6,2},{1,5},{3,7},{5,1},{7,3},{8,12},{10,14},{12... | collective-permute-start | bytes 1572872 | tf_op jit(solution)/shard_map/ppermute | solution.py:365
  532.5 26.3 %collective-permute-start.88 = (bf16[128,2048]{1,0:T(8,128)(2,1)S(1)}, bf16[128,2048]{1,0:T(8,128)(2,1)S(1)}, u32[]{:S(2)}, u32[]{:S(2)}) collective-permute-start(bf16[128,2048]{1,0:T(8,128)(2,1)S(1)} %slice.502), channel_id=1, source_target_pairs={{0,16},{16,0},{1,17},{17,1},{2,18},{18,2},{3,19},{19,3},{4,20},{20... | collective-permute-start | bytes 1572872 | tf_op jit(solution)/shard_map/ppermute | solution.py:361
  555.2 30.4 %collective-permute-start.86 = (bf16[1024,256]{1,0:T(8,128)(2,1)S(1)}, bf16[1024,256]{1,0:T(8,128)(2,1)S(1)}, u32[]{:S(2)}, u32[]{:S(2)}) collective-permute-start(bf16[1024,256]{1,0:T(8,128)(2,1)S(1)} %get-tuple-element.332), channel_id=1, source_target_pairs={{2,10},{3,11},{6,14},{7,15},{8,0},{9,1},{12,4},{13,5},{18,26},{19,... | collective-permute-start | bytes 1572872 | tf_op jit(solution)/shard_map/ppermute | solution.py:676
  556.6 29.1 %collective-permute-start.87 = (bf16[1024,256]{1,0:T(8,128)(2,1)S(1)}, bf16[1024,256]{1,0:T(8,128)(2,1)S(1)}, u32[]{:S(2)}, u32[]{:S(2)}) collective-permute-start(bf16[1024,256]{1,0:T(8,128)(2,1)S(1)} %get-tuple-element.331), channel_id=1, source_target_pairs={{2,0},{3,1},{6,4},{7,5},{8,10},{9,11},{12,14},{13,15},{18,16},{19,... | collective-permute-start | bytes 1572872 | tf_op jit(solution)/shard_map/ppermute | solution.py:676
  557.9 27.8 %collective-permute-start.90 = (bf16[3,64,2048]{2,1,0:T(8,128)(2,1)S(1)}, bf16[3,64,2048]{2,1,0:T(8,128)(2,1)S(1)}, u32[]{:S(2)}, u32[]{:S(2)}) collective-permute-start(bf16[3,64,2048]{2,1,0:T(8,128)(2,1)S(1)} %dynamic-slice_convert_fusion), channel_id=1, source_target_pairs={{0,8},{8,0},{1,9},{9,1},{2,10},{10,2},{3,11},{11,3},{4,12},{12,4},... | collective-permute-start | bytes 2359304 | tf_op jit(solution)/shard_map/ppermute | solution.py:361
  558.7 27.0 %collective-permute-start.85 = (bf16[128,2048]{1,0:T(8,128)(2,1)S(1)}, bf16[128,2048]{1,0:T(8,128)(2,1)S(1)}, u32[]{:S(2)}, u32[]{:S(2)}) collective-permute-start(bf16[128,2048]{1,0:T(8,128)(2,1)S(1)} %convert_add_fusion.3), channel_id=1, source_target_pairs={{0,6},{2,4},{4,2},{6,0},{1,7},{3,5},{5,3},{7,1},{8,14},{10,12},{12... | collective-permute-start | bytes 1572872 | tf_op jit(solution)/shard_map/ppermute | solution.py:365
  561.1 34.6 %collective-permute-start.97 = (bf16[128,2048]{1,0:T(8,128)(2,1)S(1)}, bf16[128,2048]{1,0:T(8,128)(2,1)S(1)}, u32[]{:S(2)}, u32[]{:S(2)}) collective-permute-start(bf16[128,2048]{1,0:T(8,128)(2,1)S(1)} %slice.500), channel_id=1, source_target_pairs={{0,8},{8,0},{1,9},{9,1},{2,10},{10,2},{3,11},{11,3},{4,12},{12,4},... | collective-permute-start | bytes 1572872 | tf_op jit(solution)/shard_map/ppermute | solution.py:361
  587.4 50.8 %collective-permute-start.107 = (bf16[3,64,2048]{2,1,0:T(8,128)(2,1)S(1)}, bf16[3,64,2048]{2,1,0:T(8,128)(2,1)S(1)}, u32[]{:S(2)}, u32[]{:S(2)}) collective-permute-start(bf16[3,64,2048]{2,1,0:T(8,128)(2,1)S(1)} %add_convert_fusion.6), channel_id=1, source_target_pairs={{0,0},{1,1},{2,2},{3,3},{4,16},{5,17},{6,18},{7,19},{8,8},{9,9},{1... | collective-permute-start | bytes 2359304 | tf_op jit(solution)/shard_map/ppermute | solution.py:880
  592.7 36.1 %collective-permute-start.111 = (bf16[128,2048]{1,0:T(8,128)(2,1)S(1)}, bf16[128,2048]{1,0:T(8,128)(2,1)S(1)}, u32[]{:S(2)}, u32[]{:S(2)}) collective-permute-start(bf16[128,2048]{1,0:T(8,128)(2,1)S(1)} %collective-permute-done.84), channel_id=1, source_target_pairs={{0,16},{16,0},{1,17},{17,1},{2,18},{18,2},{3,19},{19,3},{4,20},{20... | collective-permute-start | bytes 1572872 | tf_op jit(solution)/shard_map/ppermute | solution.py:361
  592.8 44.0 %collective-permute-start.113 = (bf16[128,2048]{1,0:T(8,128)(2,1)S(1)}, bf16[128,2048]{1,0:T(8,128)(2,1)S(1)}, u32[]{:S(2)}, u32[]{:S(2)}) collective-permute-start(bf16[128,2048]{1,0:T(8,128)(2,1)S(1)} %collective-permute-done.89), channel_id=1, source_target_pairs={{0,16},{16,0},{1,17},{17,1},{2,18},{18,2},{3,19},{19,3},{4,20},{20... | collective-permute-start | bytes 1572872 | tf_op jit(solution)/shard_map/ppermute | solution.py:361
  595.8 68.5 %collective-permute-start.98 = (bf16[256,2048]{1,0:T(8,128)(2,1)S(1)}, bf16[256,2048]{1,0:T(8,128)(2,1)S(1)}, u32[]{:S(2)}, u32[]{:S(2)}) collective-permute-start(bf16[256,2048]{1,0:T(8,128)(2,1)S(1)} %collective-permute-done.93), channel_id=1, source_target_pairs={{0,2},{1,3},{4,6},{5,7},{10,8},{11,9},{14,12},{15,13},{16,18},{17,... | collective-permute-start | bytes 3145736 | tf_op jit(solution)/shard_map/ppermute | solution.py:676
  603.7 61.2 %collective-permute-start.99 = (bf16[256,2048]{1,0:T(8,128)(2,1)S(1)}, bf16[256,2048]{1,0:T(8,128)(2,1)S(1)}, u32[]{:S(2)}, u32[]{:S(2)}) collective-permute-start(bf16[256,2048]{1,0:T(8,128)(2,1)S(1)} %collective-permute-done.94), channel_id=1, source_target_pairs={{0,8},{1,9},{4,12},{5,13},{10,2},{11,3},{14,6},{15,7},{16,24},{17,... | collective-permute-start | bytes 3145736 | tf_op jit(solution)/shard_map/ppermute | solution.py:676
  664.3 27.8 %collective-permute-start.114 = (bf16[256,2048]{1,0:T(8,128)(2,1)S(1)}, bf16[256,2048]{1,0:T(8,128)(2,1)S(1)}, u32[]{:S(2)}, u32[]{:S(2)}) collective-permute-start(bf16[256,2048]{1,0:T(8,128)(2,1)S(1)} %pad_maximum_fusion.20), channel_id=1, source_target_pairs={{0,1},{1,0},{2,3},{3,2},{4,5},{5,4},{6,7},{7,6},{8,9},{9,8},{10,11... | collective-permute-start | bytes 3145736 | tf_op jit(solution)/shard_map/ppermute | solution.py:361
  (171 other events, 1957.1 us)

commit v4 on v3

--- a/solution.py
+++ b/solution.py
@@ -872,20 +872,21 @@
     down_steps = [ff_step(down_sum[:half], "x", 1), ff_step(down_sum[half:], "z", 1)]
     back_parts[first], branch_hops[1], branch_hops[2] = tick(back_parts[first], branch_hops[1], branch_hops[2])
     send_back(first)
-    back_parts[second], branch_hops[3], qkv_other, mlp_hops[third], gate_step, up_step = tick(
-        back_parts[second], branch_hops[3], qkv_other, mlp_hops[third], gate_step, up_step
+    back_parts[second], branch_hops[3], mlp_hops[third], gate_step, up_step = tick(
+        back_parts[second], branch_hops[3], mlp_hops[third], gate_step, up_step
     )
     send_back(second)
     gate_step, up_step = ff_step(gate_step, "z", 0), ff_step(up_step, "x", 0)
-    qkv_moved = lax.ppermute((qkv_own + qkv_other.astype(F32)).astype(BF), AXES, perm_of(attn_place))
-    back_parts[third], back_parts[last], back_hops[first], down_steps[0], down_steps[1], *branch_hops = tick(
-        back_parts[third], back_parts[last], back_hops[first], *down_steps, *branch_hops
-    )
-    down_steps = [ff_step(down_steps[0], "z", 0), ff_step(down_steps[1], "x", 0)]
+    back_parts[third], back_parts[last], *branch_hops = tick(back_parts[third], back_parts[last], *branch_hops)
     send_back(third)
     branch_others = [swap(item, "y") for item in branch_hops]
-    branch_others[0], back_hops[second], mlp_parts[last], qkv_grad, gate_step, up_step = tick(
-        branch_others[0], back_hops[second], mlp_parts[last], qkv_grad, gate_step, up_step
+    branch_others[0], back_hops[first], qkv_other, *down_steps = tick(
+        branch_others[0], back_hops[first], qkv_other, *down_steps
+    )
+    down_steps = [ff_step(down_steps[0], "z", 0), ff_step(down_steps[1], "x", 0)]
+    qkv_moved = lax.ppermute((qkv_own + qkv_other.astype(F32)).astype(BF), AXES, perm_of(attn_place))
+    branch_others[2], back_hops[second], mlp_parts[last], qkv_grad, gate_step, up_step, qkv_moved = tick(
+        branch_others[2], back_hops[second], mlp_parts[last], qkv_grad, gate_step, up_step, qkv_moved
     )
     branch_chunks = [with_partner(*item) for item in zip(branch_hops, branch_others)]
     mlp_term = mlp_parts[last] + sum(item.astype(F32) for item in mlp_hops[1:])

time: 731 us -> 731 us (level)
    ppermute x8, waiting for transfers between devices: 2.45 us -> 26.6 us  [ff_step(): return lax.ppermute(value, AXES, pairs)]
    ppermute x74, waiting for transfers between devices: 178 us -> 155 us  [swap(): return lax.ppermute(value, axis, PAIR)]
    ppermute x30, starting transfers between devices: 74.9 us -> 63.2 us  [hop(): return lax.ppermute(value, 'z', [(i, i ^ dist) for i in range(4)])]
    ppermute x8, starting transfers between devices: 12.4 us -> 23 us  [ff_step(): return lax.ppermute(value, AXES, pairs)]
    unnamed x229 -> x231, local copies, waits for them, and re-layouts: 47.3 us -> 47.1 us
  transfers between devices with their start and end apart: 119 -> 119, of which waited for: 41 -> 42; matrix products, arithmetic and copies ran while one was open for 34% -> 34% of each run, Pallas kernels for 4% -> 4%
where the time goes in v4:
time: 731 us; the launch traced here: 718 us
  waiting for transfers between devices  255 us (35%)
  starting transfers between devices  168 us (23%)
  local copies, waits for them, and re-layouts  90.9 us (12%)
  matrix products  86.1 us (12%)
  other arithmetic  83.1 us (11%)
  Pallas kernels  31.7 us (4%)
    ppermute x74, waiting for transfers between devices, swap(): return lax.ppermute(value, axis, PAIR)  155 us
    dot_general x48, matrix products, dot(): lax.dot_general(left, right, (((left_dim,), (right_dim,)), ((), ())), pre...  86.1 us
    ppermute x74, starting transfers between devices, swap(): return lax.ppermute(value, axis, PAIR)  63.4 us
    ppermute x30, starting transfers between devices, hop(): return lax.ppermute(value, 'z', [(i, i ^ dist) for i in range(4)])  63.2 us
    ppermute x30, waiting for transfers between devices, hop(): return lax.ppermute(value, 'z', [(i, i ^ dist) for i in range(4)])  56.8 us
    unnamed x231, local copies, waits for them, and re-layouts  47.1 us
    ppermute x8, waiting for transfers between devices, ff_step(): return lax.ppermute(value, AXES, pairs)  26.6 us
    ppermute x8, starting transfers between devices, ff_step(): return lax.ppermute(value, AXES, pairs)  23 us
  transfers between devices with their start and end apart: 119, of which 42 were waited for; matrix products, arithmetic and copies ran while one was open for 34% of the time, Pallas kernels for 4%

profile of v4, /device:TPU:6, one launch (start us, length us, event | category | flops | bytes accessed | tf_op | source)
XLA Modules:
  0.0 718.3 jit_solution(76351182919647389)
XLA Ops:
  14.3 10.7 %constant_dynamic-slice_fusion.18 = (bf16[256,1,2048]{2,1,0:T(2,128)(2,1)}, bf16[256,1,2048]{2,1,0:T(2,128)(2,1)}, bf16[256,1,2048]{2,1,0:T(2,128)(2,1)}, bf16[256,1,2048]{2,1,0:T(2,128)(2,1)}) fusion(bf16[2048,2,2048]{2,1,0:T(2,128)(2,1)} %param.13, s32[]{:T(128)S(6)} %select_n.135, s32[]{:T(128)S(6)} %add.494, s32[]{:T(128)S(6)} %select_n.134), kind=kLoop, calls=%fused_computation.248 | loop fusion | bytes 8388620 | tf_op jit(solution)/shard_map/slice | solution.py:714
  47.3 8.4 %collective-permute-done.6 = bf16[128,2048]{1,0:T(8,128)(2,1)} collective-permute-done((bf16[128,2048]{1,0:T(8,128)(2,1)S(1)}, bf16[128,2048]{1,0:T(8,128)(2,1)}, u32[]{:S(2)}, u32[]{:S(2)}) %collective-permute-start.6) | collective-permute-done | bytes 524320 | tf_op jit(solution)/shard_map/ppermute | solution.py:361
  66.7 10.7 %collective-permute-done.10 = bf16[128,2048]{1,0:T(8,128)(2,1)S(1)} collective-permute-done((bf16[128,2048]{1,0:T(8,128)(2,1)S(1)}, bf16[128,2048]{1,0:T(8,128)(2,1)S(1)}, u32[]{:S(2)}, u32[]{:S(2)}) %collective-permute-start.10) | collective-permute-done | bytes 524320 | tf_op jit(solution)/shard_map/ppermute | solution.py:361
  85.3 4.2 collective-permute-start.14
  93.5 6.9 fusion.75
  100.4 5.2 attend.1
  107.8 7.1 collective-permute-done.16
  121.9 7.0 collective-permute-done.17
  128.9 4.8 collective-permute-done.18
  133.8 9.9 %collective-permute-start.19 = (bf16[2,2,128,128]{3,2,0,1:T(8,128)(2,1)S(1)}, bf16[2,2,128,128]{3,2,0,1:T(8,128)(2,1)S(1)}, u32[]{:S(2)}, u32[]{:S(2)}) collective-permute-start(bf16[2,2,128,128]{3,2,0,1:T(8,128)(2,1)S(1)} %get-tuple-element.351), channel_id=1, source_target_pairs={{0,2},{2,0},{4,6},{6,4},{1,3},{3,1},{5,7},{7,5},{8,10},{10,8},{12,... | collective-permute-start | bytes 393224 | tf_op jit(solution)/shard_map/ppermute | solution.py:365
  153.6 4.1 collective-permute-done.21
  158.5 4.0 collective-permute-done.22.far
  169.1 5.7 collective-permute-start.26
  174.8 8.2 %join_out.1 = bf16[2048,2048]{1,0:T(8,128)(2,1)} custom-call(s32[4]{0:T(128)} %copy-done.10, bf16[1024,1024]{1,0:T(8,128)(2,1)} %copy-done.42, bf16[1024,1024]{1,0:T(8,128)(2,1)} %collective-permute-done.22.far, bf16[1024,1024]{1,0:T(8,128)(2,1)} %copy-done.64, bf16[1024,1024]{1,0:T(8,128)(2,1)} %collective-permute-done.25.far_c), custom_call_target="tpu_custom_call" | custom-call | bytes 1048576 | tf_op jit(solution)/shard_map/join_out/pallas_call | solution.py:589
  183.0 6.7 multiply_reduce_fusion.3
  190.6 8.0 %collective-permute-done.26 = bf16[128,2048]{1,0:T(8,128)(2,1)} collective-permute-done((bf16[128,2048]{1,0:T(8,128)(2,1)}, bf16[128,2048]{1,0:T(8,128)(2,1)}, u32[]{:S(2)}, u32[]{:S(2)}) %collective-permute-start.26) | collective-permute-done | bytes 524320 | tf_op jit(solution)/shard_map/ppermute | solution.py:365
  216.8 9.2 %collective-permute-done.39 = bf16[128,2048]{1,0:T(8,128)(2,1)} collective-permute-done((bf16[128,2048]{1,0:T(8,128)(2,1)}, bf16[128,2048]{1,0:T(8,128)(2,1)}, u32[]{:S(2)}, u32[]{:S(2)}) %collective-permute-start.39) | collective-permute-done | bytes 524320 | tf_op jit(solution)/shard_map/ppermute | solution.py:365
  227.9 4.5 order_rows.1
  254.4 9.4 %collective-permute-done.44 = bf16[128,2048]{1,0:T(8,128)(2,1)S(1)} collective-permute-done((bf16[128,2048]{1,0:T(8,128)(2,1)}, bf16[128,2048]{1,0:T(8,128)(2,1)S(1)}, u32[]{:S(2)}, u32[]{:S(2)}) %collective-permute-start.44) | collective-permute-done | bytes 524320 | tf_op jit(solution)/shard_map/ppermute | solution.py:361
  267.2 7.3 %collective-permute-done.36 = bf16[128,2048]{1,0:T(8,128)(2,1)S(1)} collective-permute-done((bf16[128,2048]{1,0:T(8,128)(2,1)S(1)}, bf16[128,2048]{1,0:T(8,128)(2,1)S(1)}, u32[]{:S(2)}, u32[]{:S(2)}) %collective-permute-start.36) | collective-permute-done | bytes 524320 | tf_op jit(solution)/shard_map/ppermute | solution.py:361
  284.9 4.3 collective-permute-done.47
  289.4 9.5 %collective-permute-done.37 = bf16[128,2048]{1,0:T(8,128)(2,1)S(1)} collective-permute-done((bf16[128,2048]{1,0:T(8,128)(2,1)}, bf16[128,2048]{1,0:T(8,128)(2,1)S(1)}, u32[]{:S(2)}, u32[]{:S(2)}) %collective-permute-start.37) | collective-permute-done | bytes 524320 | tf_op jit(solution)/shard_map/ppermute | solution.py:361
  303.0 5.0 collective-permute-done.42
  364.5 4.1 add_convert_fusion.2
  401.0 4.2 collective-permute-done.58
  409.0 9.5 %collective-permute-done.60 = bf16[256,2048]{1,0:T(8,128)(2,1)S(1)} collective-permute-done((bf16[256,2048]{1,0:T(8,128)(2,1)}, bf16[256,2048]{1,0:T(8,128)(2,1)S(1)}, u32[]{:S(2)}, u32[]{:S(2)}) %collective-permute-start.60) | collective-permute-done | bytes 1048608 | tf_op jit(solution)/shard_map/ppermute | solution.py:361
  431.7 4.6 collective-permute-done.61
  440.9 7.7 %collective-permute-done.67 = bf16[256,2048]{1,0:T(8,128)(2,1)S(1)} collective-permute-done((bf16[256,2048]{1,0:T(8,128)(2,1)S(1)}, bf16[256,2048]{1,0:T(8,128)(2,1)S(1)}, u32[]{:S(2)}, u32[]{:S(2)}) %collective-permute-start.67) | collective-permute-done | bytes 1048608 | tf_op jit(solution)/shard_map/ppermute | solution.py:361
  460.3 4.6 collective-permute-start.69
  467.9 4.0 collective-permute-done.69
  483.8 9.9 %attend_back.1 = bf16[4,2,2,128,384]{4,3,2,1,0:T(8,128)(2,1)S(1)} custom-call(s32[4]{0:T(128)S(1)} %copy-done.11, bf16[2,1024,128]{2,1,0:T(8,128)(2,1)S(1)} %copy-done.5, bf16[2,1024,128]{2,1,0:T(8,128)(2,1)S(1)} %copy-done.7, bf16[2,1024,128]{2,1,0:T(8,128)(2,1)S(1)} %copy-done.9, f32[2,1024,128]{2,1,0:T(8,128)S(1)} %get-tuple-element.175.att_ref, ...), custom_call_target="tpu_custom_call" | custom-call | bytes 1048576 | tf_op jit(solution)/shard_map/attend_back/pallas_call | solution.py:540
  514.5 8.8 %collective-permute-done.81 = bf16[128,2048]{1,0:T(8,128)(2,1)S(1)} collective-permute-done((bf16[128,2048]{1,0:T(8,128)(2,1)S(1)}, bf16[128,2048]{1,0:T(8,128)(2,1)S(1)}, u32[]{:S(2)}, u32[]{:S(2)}) %collective-permute-start.81) | collective-permute-done | bytes 524320 | tf_op jit(solution)/shard_map/ppermute | solution.py:361
  523.7 10.9 %collective-permute-done.85 = bf16[128,2048]{1,0:T(8,128)(2,1)S(1)} collective-permute-done((bf16[128,2048]{1,0:T(8,128)(2,1)S(1)}, bf16[128,2048]{1,0:T(8,128)(2,1)S(1)}, u32[]{:S(2)}, u32[]{:S(2)}) %collective-permute-start.85) | collective-permute-done | bytes 524320 | tf_op jit(solution)/shard_map/ppermute | solution.py:361
  539.6 6.2 collective-permute-done.82
  550.4 6.0 collective-permute-done.80
  557.6 10.9 %collective-permute-start.99 = (bf16[1024,256]{1,0:T(8,128)(2,1)S(1)}, bf16[1024,256]{1,0:T(8,128)(2,1)S(1)}, u32[]{:S(2)}, u32[]{:S(2)}) collective-permute-start(bf16[1024,256]{1,0:T(8,128)(2,1)S(1)} %get-tuple-element.336), channel_id=1, source_target_pairs={{2,10},{3,11},{6,14},{7,15},{8,0},{9,1},{12,4},{13,5},{18,26},{19,... | collective-permute-start | bytes 1572872 | tf_op jit(solution)/shard_map/ppermute | solution.py:676
  569.5 4.9 collective-permute-done.100
  575.1 10.1 %collective-permute-done.99 = bf16[1024,256]{1,0:T(8,128)(2,1)S(1)} collective-permute-done((bf16[1024,256]{1,0:T(8,128)(2,1)S(1)}, bf16[1024,256]{1,0:T(8,128)(2,1)S(1)}, u32[]{:S(2)}, u32[]{:S(2)}) %collective-permute-start.99) | collective-permute-done | bytes 524320 | tf_op jit(solution)/shard_map/ppermute | solution.py:676
  591.4 8.9 %collective-permute-done.113 = bf16[128,2048]{1,0:T(8,128)(2,1)S(1)} collective-permute-done((bf16[128,2048]{1,0:T(8,128)(2,1)S(1)}, bf16[128,2048]{1,0:T(8,128)(2,1)S(1)}, u32[]{:S(2)}, u32[]{:S(2)}) %collective-permute-start.113) | collective-permute-done | bytes 524320 | tf_op jit(solution)/shard_map/ppermute | solution.py:361
  600.3 9.8 %collective-permute-start.101 = (bf16[3,64,2048]{2,1,0:T(8,128)(2,1)S(1)}, bf16[3,64,2048]{2,1,0:T(8,128)(2,1)S(1)}, u32[]{:S(2)}, u32[]{:S(2)}) collective-permute-start(bf16[3,64,2048]{2,1,0:T(8,128)(2,1)S(1)} %add_convert_fusion.6), channel_id=1, source_target_pairs={{0,0},{1,1},{2,2},{3,3},{4,16},{5,17},{6,18},{7,19},{8,8},{9,9},{1... | collective-permute-start | bytes 2359304 | tf_op jit(solution)/shard_map/ppermute | solution.py:887
  610.3 11.6 %collective-permute-done.117 = bf16[1024,256]{1,0:T(8,128)(2,1)S(1)} collective-permute-done((bf16[1024,256]{1,0:T(8,128)(2,1)S(1)}, bf16[1024,256]{1,0:T(8,128)(2,1)S(1)}, u32[]{:S(2)}, u32[]{:S(2)}) %collective-permute-start.117) | collective-permute-done | bytes 524320 | tf_op jit(solution)/shard_map/ppermute | solution.py:676
  622.0 17.5 %collective-permute-start.91 = (bf16[128,2048]{1,0:T(8,128)(2,1)S(1)}, bf16[128,2048]{1,0:T(8,128)(2,1)S(1)}, u32[]{:S(2)}, u32[]{:S(2)}) collective-permute-start(bf16[128,2048]{1,0:T(8,128)(2,1)S(1)} %collective-permute-done.84), channel_id=1, source_target_pairs={{0,16},{16,0},{1,17},{17,1},{2,18},{18,2},{3,19},{19,3},{4,20},{20... | collective-permute-start | bytes 1572872 | tf_op jit(solution)/shard_map/ppermute | solution.py:361
  641.0 8.4 %collective-permute-done.91 = bf16[128,2048]{1,0:T(8,128)(2,1)S(1)} collective-permute-done((bf16[128,2048]{1,0:T(8,128)(2,1)S(1)}, bf16[128,2048]{1,0:T(8,128)(2,1)S(1)}, u32[]{:S(2)}, u32[]{:S(2)}) %collective-permute-start.91) | collective-permute-done | bytes 524320 | tf_op jit(solution)/shard_map/ppermute | solution.py:361
  652.6 9.6 %collective-permute-done.92 = bf16[128,2048]{1,0:T(8,128)(2,1)S(1)} collective-permute-done((bf16[128,2048]{1,0:T(8,128)(2,1)S(1)}, bf16[128,2048]{1,0:T(8,128)(2,1)S(1)}, u32[]{:S(2)}, u32[]{:S(2)}) %collective-permute-start.92) | collective-permute-done | bytes 524320 | tf_op jit(solution)/shard_map/ppermute | solution.py:365
  664.0 8.8 %collective-permute-done.102 = bf16[128,2048]{1,0:T(8,128)(2,1)S(1)} collective-permute-done((bf16[128,2048]{1,0:T(8,128)(2,1)S(1)}, bf16[128,2048]{1,0:T(8,128)(2,1)S(1)}, u32[]{:S(2)}, u32[]{:S(2)}) %collective-permute-start.102) | collective-permute-done | bytes 524320 | tf_op jit(solution)/shard_map/ppermute | solution.py:365
  681.7 5.2 copy.45
  698.8 4.3 collective-permute-done.115
  705.6 11.5 %collective-permute-done.116 = bf16[2048,64]{0,1:T(8,128)(2,1)S(1)} collective-permute-done((bf16[2048,64]{0,1:T(8,128)(2,1)S(1)}, bf16[2048,64]{0,1:T(8,128)(2,1)S(1)}, u32[]{:S(2)}, u32[]{:S(2)}) %collective-permute-start.116) | collective-permute-done | bytes 262176 | tf_op jit(solution)/shard_map/ppermute | solution.py:670
  (635 shorter events, 351.7 us)
Async XLA Ops:
  7.6 26.8 %collective-permute-start.5 = (bf16[128,2048]{1,0:T(8,128)(2,1)}, bf16[128,2048]{1,0:T(8,128)(2,1)S(1)}, u32[]{:S(2)}, u32[]{:S(2)}) collective-permute-start(bf16[128,2048]{1,0:T(8,128)(2,1)} %get-tuple-element.310), channel_id=1, source_target_pairs={{0,6},{2,4},{4,2},{6,0},{1,7},{3,5},{5,3},{7,1},{8,14},{10,12},{12... | collective-permute-start | bytes 1572872 | tf_op jit(solution)/shard_map/ppermute | solution.py:365
  10.1 53.0 %collective-permute-start.8 = (bf16[128,2048]{1,0:T(8,128)(2,1)}, bf16[128,2048]{1,0:T(8,128)(2,1)S(1)}, u32[]{:S(2)}, u32[]{:S(2)}) collective-permute-start(bf16[128,2048]{1,0:T(8,128)(2,1)} %get-tuple-element.310), channel_id=1, source_target_pairs={{0,4},{2,6},{4,0},{6,2},{1,5},{3,7},{5,1},{7,3},{8,12},{10,14},{12... | collective-permute-start | bytes 1572872 | tf_op jit(solution)/shard_map/ppermute | solution.py:365
  12.9 50.1 %collective-permute-start.9 = (bf16[384,2048]{1,0:T(8,128)(2,1)}, bf16[384,2048]{1,0:T(8,128)(2,1)}, u32[]{:S(2)}, u32[]{:S(2)}) collective-permute-start(bf16[384,2048]{1,0:T(8,128)(2,1)} %bitcast.3), channel_id=1, source_target_pairs={{0,8},{10,2},{4,12},{14,6},{1,9},{11,3},{5,13},{15,7},{16,24},{26,... | collective-permute-start | bytes 4718600 | tf_op jit(solution)/shard_map/ppermute | solution.py:698
  29.9 27.1 %collective-permute-start.1 = (bf16[256,2048]{1,0:T(8,128)(2,1)}, bf16[256,2048]{1,0:T(8,128)(2,1)}, u32[]{:S(2)}, u32[]{:S(2)}) collective-permute-start(bf16[256,2048]{1,0:T(8,128)(2,1)} %pad_maximum_fusion.5), channel_id=1, source_target_pairs={{0,1},{1,0},{2,3},{3,2},{4,5},{5,4},{6,7},{7,6},{8,9},{9,8},{10,11... | collective-permute-start | bytes 3145736 | tf_op jit(solution)/shard_map/ppermute | solution.py:361
  47.3 30.3 %collective-permute-start.4 = (bf16[256,2048]{1,0:T(8,128)(2,1)S(1)}, bf16[256,2048]{1,0:T(8,128)(2,1)S(1)}, u32[]{:S(2)}, u32[]{:S(2)}) collective-permute-start(bf16[256,2048]{1,0:T(8,128)(2,1)S(1)} %pad_maximum_fusion.6), channel_id=1, source_target_pairs={{0,1},{1,0},{2,3},{3,2},{4,5},{5,4},{6,7},{7,6},{8,9},{9,8},{10,11... | collective-permute-start | bytes 3145736 | tf_op jit(solution)/shard_map/ppermute | solution.py:361
  89.9 25.5 %collective-permute-start.13 = (bf16[512,1024]{1,0:T(8,128)(2,1)}, bf16[512,1024]{1,0:T(8,128)(2,1)S(1)}, u32[]{:S(2)}, u32[]{:S(2)}) collective-permute-start(bf16[512,1024]{1,0:T(8,128)(2,1)} %constant_dynamic-slice_fusion.17), channel_id=1, source_target_pairs={{0,16},{16,0},{1,17},{17,1},{2,18},{18,2},{3,19},{19,3},{4,20},{20... | collective-permute-start | bytes 3145736 | tf_op jit(solution)/shard_map/ppermute | solution.py:361
  115.5 47.1 %collective-permute-start.22 = (bf16[1024,1024]{1,0:T(8,128)(2,1)S(1)}, bf16[1024,1024]{1,0:T(8,128)(2,1)}, u32[]{:S(2)}, u32[]{:S(2)}) collective-permute-start(bf16[1024,1024]{1,0:T(8,128)(2,1)S(1)} %constant_dynamic-update-slice_fusion.12.pair), channel_id=1, source_target_pairs={{0,8},{8,0},{1,9},{9,1},{2,10},{10,2},{3,11},{11,3},{4,12},{12,4},... | collective-permute-start | bytes 6291464 | tf_op jit(solution)/shard_map/ppermute | solution.py:361
  117.3 45.3 %collective-permute-start.24 = (bf16[1024,1024]{1,0:T(8,128)(2,1)S(1)}, bf16[1024,1024]{1,0:T(8,128)(2,1)S(1)}, u32[]{:S(2)}, u32[]{:S(2)}) collective-permute-start(bf16[1024,1024]{1,0:T(8,128)(2,1)S(1)} %constant_dynamic-update-slice_fusion.12.pair), channel_id=1, source_target_pairs={{0,1},{1,0},{2,3},{3,2},{4,5},{5,4},{6,7},{7,6},{8,9},{9,8},{10,11... | collective-permute-start | bytes 6291464 | tf_op jit(solution)/shard_map/ppermute | solution.py:361
  121.3 37.3 %collective-permute-start.23 = (bf16[1024,512]{1,0:T(8,128)(2,1)S(1)}, bf16[1024,512]{1,0:T(8,128)(2,1)S(1)}, u32[]{:S(2)}, u32[]{:S(2)}) collective-permute-start(bf16[1024,512]{1,0:T(8,128)(2,1)S(1)} %constant_dynamic-update-slice_fusion.14), channel_id=1, source_target_pairs={{0,16},{16,0},{1,17},{17,1},{2,18},{18,2},{3,19},{19,3},{4,20},{20... | collective-permute-start | bytes 3145736 | tf_op jit(solution)/shard_map/ppermute | solution.py:361
  167.8 30.8 %collective-permute-start.27 = (bf16[256,2048]{1,0:T(8,128)(2,1)}, bf16[256,2048]{1,0:T(8,128)(2,1)}, u32[]{:S(2)}, u32[]{:S(2)}) collective-permute-start(bf16[256,2048]{1,0:T(8,128)(2,1)} %bitcast.181), channel_id=1, source_target_pairs={{0,16},{2,18},{20,4},{22,6},{1,17},{3,19},{21,5},{23,7},{8,24},{10... | collective-permute-start | bytes 3145736 | tf_op jit(solution)/shard_map/ppermute | solution.py:718
  169.1 29.6 %collective-permute-start.26 = (bf16[128,2048]{1,0:T(8,128)(2,1)}, bf16[128,2048]{1,0:T(8,128)(2,1)}, u32[]{:S(2)}, u32[]{:S(2)}) collective-permute-start(bf16[128,2048]{1,0:T(8,128)(2,1)} %bitcast.15), channel_id=1, source_target_pairs={{0,4},{2,6},{4,0},{6,2},{1,5},{3,7},{5,1},{7,3},{8,12},{10,14},{12... | collective-permute-start | bytes 1572872 | tf_op jit(solution)/shard_map/ppermute | solution.py:365
  198.7 38.7 %collective-permute-start.32 = (bf16[128,2048]{1,0:T(8,128)(2,1)}, bf16[128,2048]{1,0:T(8,128)(2,1)}, u32[]{:S(2)}, u32[]{:S(2)}) collective-permute-start(bf16[128,2048]{1,0:T(8,128)(2,1)} %multiply_convert_fusion.12), channel_id=1, source_target_pairs={{0,2},{2,0},{4,6},{6,4},{1,3},{3,1},{5,7},{7,5},{8,10},{10,8},{12,... | collective-permute-start | bytes 1572872 | tf_op jit(solution)/shard_map/ppermute | solution.py:365
  199.3 26.8 %collective-permute-start.39 = (bf16[128,2048]{1,0:T(8,128)(2,1)}, bf16[128,2048]{1,0:T(8,128)(2,1)}, u32[]{:S(2)}, u32[]{:S(2)}) collective-permute-start(bf16[128,2048]{1,0:T(8,128)(2,1)} %multiply_convert_fusion.12), channel_id=1, source_target_pairs={{0,4},{2,6},{4,0},{6,2},{1,5},{3,7},{5,1},{7,3},{8,12},{10,14},{12... | collective-permute-start | bytes 1572872 | tf_op jit(solution)/shard_map/ppermute | solution.py:365
  202.7 30.9 %collective-permute-start.29 = (bf16[128,2048]{1,0:T(8,128)(2,1)}, bf16[128,2048]{1,0:T(8,128)(2,1)}, u32[]{:S(2)}, u32[]{:S(2)}) collective-permute-start(bf16[128,2048]{1,0:T(8,128)(2,1)} %multiply_convert_fusion.12), channel_id=1, source_target_pairs={{0,8},{8,0},{1,9},{9,1},{2,10},{10,2},{3,11},{11,3},{4,12},{12,4},... | collective-permute-start | bytes 1572872 | tf_op jit(solution)/shard_map/ppermute | solution.py:361
  203.2 35.0 %collective-permute-start.33 = (bf16[256,2048]{1,0:T(8,128)(2,1)}, bf16[256,2048]{1,0:T(8,128)(2,1)}, u32[]{:S(2)}, u32[]{:S(2)}) collective-permute-start(bf16[256,2048]{1,0:T(8,128)(2,1)} %bitcast.167), channel_id=1, source_target_pairs={{0,16},{2,18},{20,4},{22,6},{1,17},{3,19},{21,5},{23,7},{8,24},{10... | collective-permute-start | bytes 3145736 | tf_op jit(solution)/shard_map/ppermute | solution.py:718
  204.5 33.1 %collective-permute-start.34 = (bf16[128,2048]{1,0:T(8,128)(2,1)}, bf16[128,2048]{1,0:T(8,128)(2,1)}, u32[]{:S(2)}, u32[]{:S(2)}) collective-permute-start(bf16[128,2048]{1,0:T(8,128)(2,1)} %collective-permute-done.14), channel_id=1, source_target_pairs={{0,8},{8,0},{1,9},{9,1},{2,10},{10,2},{3,11},{11,3},{4,12},{12,4},... | collective-permute-start | bytes 1572872 | tf_op jit(solution)/shard_map/ppermute | solution.py:361
  233.6 33.4 %collective-permute-start.31 = (bf16[128,2048]{1,0:T(8,128)(2,1)}, bf16[128,2048]{1,0:T(8,128)(2,1)S(1)}, u32[]{:S(2)}, u32[]{:S(2)}) collective-permute-start(bf16[128,2048]{1,0:T(8,128)(2,1)} %multiply_convert_fusion.12), channel_id=1, source_target_pairs={{0,6},{2,4},{4,2},{6,0},{1,7},{3,5},{5,3},{7,1},{8,14},{10,12},{12... | collective-permute-start | bytes 1572872 | tf_op jit(solution)/shard_map/ppermute | solution.py:365
  237.3 27.7 %collective-permute-start.30 = (bf16[256,2048]{1,0:T(8,128)(2,1)S(1)}, bf16[256,2048]{1,0:T(8,128)(2,1)S(1)}, u32[]{:S(2)}, u32[]{:S(2)}) collective-permute-start(bf16[256,2048]{1,0:T(8,128)(2,1)S(1)} %pad_maximum_fusion.10), channel_id=1, source_target_pairs={{0,1},{1,0},{2,3},{3,2},{4,5},{5,4},{6,7},{7,6},{8,9},{9,8},{10,11... | collective-permute-start | bytes 3145736 | tf_op jit(solution)/shard_map/ppermute | solution.py:361
  238.2 36.2 %collective-permute-start.35 = (bf16[256,2048]{1,0:T(8,128)(2,1)S(1)}, bf16[256,2048]{1,0:T(8,128)(2,1)S(1)}, u32[]{:S(2)}, u32[]{:S(2)}) collective-permute-start(bf16[256,2048]{1,0:T(8,128)(2,1)S(1)} %bitcast.179), channel_id=1, source_target_pairs={{0,16},{2,18},{20,4},{22,6},{1,17},{3,19},{21,5},{23,7},{8,24},{10... | collective-permute-start | bytes 3145736 | tf_op jit(solution)/shard_map/ppermute | solution.py:718
  267.1 33.2 %collective-permute-start.45 = (bf16[256,2048]{1,0:T(8,128)(2,1)S(1)}, bf16[256,2048]{1,0:T(8,128)(2,1)S(1)}, u32[]{:S(2)}, u32[]{:S(2)}) collective-permute-start(bf16[256,2048]{1,0:T(8,128)(2,1)S(1)} %pad_maximum_fusion.13), channel_id=1, source_target_pairs={{0,1},{1,0},{2,3},{3,2},{4,5},{5,4},{6,7},{7,6},{8,9},{9,8},{10,11... | collective-permute-start | bytes 3145736 | tf_op jit(solution)/shard_map/ppermute | solution.py:361
  281.8 26.2 %collective-permute-start.42 = (bf16[256,2048]{1,0:T(8,128)(2,1)S(1)}, bf16[256,2048]{1,0:T(8,128)(2,1)S(1)}, u32[]{:S(2)}, u32[]{:S(2)}) collective-permute-start(bf16[256,2048]{1,0:T(8,128)(2,1)S(1)} %bitcast.177), channel_id=1, source_target_pairs={{0,16},{2,18},{20,4},{22,6},{1,17},{3,19},{21,5},{23,7},{8,24},{10... | collective-permute-start | bytes 3145736 | tf_op jit(solution)/shard_map/ppermute | solution.py:718
  335.0 41.0 %collective-permute-start.53 = (bf16[256,2048]{1,0:T(8,128)(2,1)}, bf16[256,2048]{1,0:T(8,128)(2,1)}, u32[]{:S(2)}, u32[]{:S(2)}) collective-permute-start(bf16[256,2048]{1,0:T(8,128)(2,1)} %slice.496), channel_id=1, source_target_pairs={{0,1},{1,0},{2,3},{3,2},{4,5},{5,4},{6,7},{7,6},{8,9},{9,8},{10,11... | collective-permute-start | bytes 3145736 | tf_op jit(solution)/shard_map/ppermute | solution.py:361
  337.4 49.7 %collective-permute-start.59 = (bf16[256,2048]{1,0:T(8,128)(2,1)}, bf16[256,2048]{1,0:T(8,128)(2,1)}, u32[]{:S(2)}, u32[]{:S(2)}) collective-permute-start(bf16[256,2048]{1,0:T(8,128)(2,1)} %slice.493), channel_id=1, source_target_pairs={{0,1},{1,0},{2,3},{3,2},{4,5},{5,4},{6,7},{7,6},{8,9},{9,8},{10,11... | collective-permute-start | bytes 3145736 | tf_op jit(solution)/shard_map/ppermute | solution.py:361
  364.5 29.6 %collective-permute-start.62 = (bf16[256,2048]{1,0:T(8,128)(2,1)}, bf16[256,2048]{1,0:T(8,128)(2,1)}, u32[]{:S(2)}, u32[]{:S(2)}) collective-permute-start(bf16[256,2048]{1,0:T(8,128)(2,1)} %slice.492), channel_id=1, source_target_pairs={{0,1},{1,0},{2,3},{3,2},{4,5},{5,4},{6,7},{7,6},{8,9},{9,8},{10,11... | collective-permute-start | bytes 3145736 | tf_op jit(solution)/shard_map/ppermute | solution.py:361
  369.7 37.5 %collective-permute-start.57 = (bf16[256,2048]{1,0:T(8,128)(2,1)}, bf16[256,2048]{1,0:T(8,128)(2,1)}, u32[]{:S(2)}, u32[]{:S(2)}) collective-permute-start(bf16[256,2048]{1,0:T(8,128)(2,1)} %slice.494), channel_id=1, source_target_pairs={{0,1},{1,0},{2,3},{3,2},{4,5},{5,4},{6,7},{7,6},{8,9},{9,8},{10,11... | collective-permute-start | bytes 3145736 | tf_op jit(solution)/shard_map/ppermute | solution.py:361
  373.7 66.1 %collective-permute-start.65 = (bf16[128,2048]{1,0:T(8,128)(2,1)}, bf16[128,2048]{1,0:T(8,128)(2,1)}, u32[]{:S(2)}, u32[]{:S(2)}) collective-permute-start(bf16[128,2048]{1,0:T(8,128)(2,1)} %convert_add_fusion.12), channel_id=1, source_target_pairs={{0,6},{2,4},{4,2},{6,0},{1,7},{3,5},{5,3},{7,1},{8,14},{10,12},{12... | collective-permute-start | bytes 1572872 | tf_op jit(solution)/shard_map/ppermute | solution.py:365
  398.8 42.1 %collective-permute-start.66 = (bf16[128,2048]{1,0:T(8,128)(2,1)S(1)}, bf16[128,2048]{1,0:T(8,128)(2,1)}, u32[]{:S(2)}, u32[]{:S(2)}) collective-permute-start(bf16[128,2048]{1,0:T(8,128)(2,1)S(1)} %copy-done.88), channel_id=1, source_target_pairs={{0,4},{2,6},{4,0},{6,2},{1,5},{3,7},{5,1},{7,3},{8,12},{10,14},{12... | collective-permute-start | bytes 1572872 | tf_op jit(solution)/shard_map/ppermute | solution.py:365
  436.4 38.9 %collective-permute-start.71 = (bf16[128,2048]{1,0:T(8,128)(2,1)}, bf16[128,2048]{1,0:T(8,128)(2,1)}, u32[]{:S(2)}, u32[]{:S(2)}) collective-permute-start(bf16[128,2048]{1,0:T(8,128)(2,1)} %convert_add_fusion.10), channel_id=1, source_target_pairs={{0,6},{2,4},{4,2},{6,0},{1,7},{3,5},{5,3},{7,1},{8,14},{10,12},{12... | collective-permute-start | bytes 1572872 | tf_op jit(solution)/shard_map/ppermute | solution.py:365
  439.8 25.1 %collective-permute-start.87 = (bf16[128,2048]{1,0:T(8,128)(2,1)}, bf16[128,2048]{1,0:T(8,128)(2,1)}, u32[]{:S(2)}, u32[]{:S(2)}) collective-permute-start(bf16[128,2048]{1,0:T(8,128)(2,1)} %slice.501), channel_id=1, source_target_pairs={{0,8},{8,0},{1,9},{9,1},{2,10},{10,2},{3,11},{11,3},{4,12},{12,4},... | collective-permute-start | bytes 1572872 | tf_op jit(solution)/shard_map/ppermute | solution.py:361
  467.5 47.0 %collective-permute-start.88 = (bf16[128,2048]{1,0:T(8,128)(2,1)S(1)}, bf16[128,2048]{1,0:T(8,128)(2,1)S(1)}, u32[]{:S(2)}, u32[]{:S(2)}) collective-permute-start(bf16[128,2048]{1,0:T(8,128)(2,1)S(1)} %add_convert_fusion.8), channel_id=1, source_target_pairs={{0,2},{2,0},{4,6},{6,4},{1,3},{3,1},{5,7},{7,5},{8,10},{10,8},{12,... | collective-permute-start | bytes 1572872 | tf_op jit(solution)/shard_map/ppermute | solution.py:365
  471.9 36.5 %collective-permute-start.79 = (bf16[128,2048]{1,0:T(8,128)(2,1)S(1)}, bf16[128,2048]{1,0:T(8,128)(2,1)S(1)}, u32[]{:S(2)}, u32[]{:S(2)}) collective-permute-start(bf16[128,2048]{1,0:T(8,128)(2,1)S(1)} %copy-done.87), channel_id=1, source_target_pairs={{0,4},{2,6},{4,0},{6,2},{1,5},{3,7},{5,1},{7,3},{8,12},{10,14},{12... | collective-permute-start | bytes 1572872 | tf_op jit(solution)/shard_map/ppermute | solution.py:365
  477.4 62.1 %collective-permute-start.90 = (bf16[256,2048]{1,0:T(8,128)(2,1)S(1)}, bf16[256,2048]{1,0:T(8,128)(2,1)S(1)}, u32[]{:S(2)}, u32[]{:S(2)}) collective-permute-start(bf16[256,2048]{1,0:T(8,128)(2,1)S(1)} %add_convert_fusion.4), channel_id=1, source_target_pairs={{2,0},{3,1},{6,4},{7,5},{8,10},{9,11},{12,14},{13,15},{18,16},{19,... | collective-permute-start | bytes 3145736 | tf_op jit(solution)/shard_map/ppermute | solution.py:676
  509.3 25.3 %collective-permute-start.85 = (bf16[128,2048]{1,0:T(8,128)(2,1)S(1)}, bf16[128,2048]{1,0:T(8,128)(2,1)S(1)}, u32[]{:S(2)}, u32[]{:S(2)}) collective-permute-start(bf16[128,2048]{1,0:T(8,128)(2,1)S(1)} %slice.502), channel_id=1, source_target_pairs={{0,16},{16,0},{1,17},{17,1},{2,18},{18,2},{3,19},{19,3},{4,20},{20... | collective-permute-start | bytes 1572872 | tf_op jit(solution)/shard_map/ppermute | solution.py:361
  511.2 37.8 %collective-permute-start.89 = (bf16[256,2048]{1,0:T(8,128)(2,1)S(1)}, bf16[256,2048]{1,0:T(8,128)(2,1)S(1)}, u32[]{:S(2)}, u32[]{:S(2)}) collective-permute-start(bf16[256,2048]{1,0:T(8,128)(2,1)S(1)} %add_convert_fusion.5), channel_id=1, source_target_pairs={{2,10},{3,11},{6,14},{7,15},{8,0},{9,1},{12,4},{13,5},{18,26},{19,... | collective-permute-start | bytes 3145736 | tf_op jit(solution)/shard_map/ppermute | solution.py:676
  538.9 30.0 %collective-permute-start.93 = (bf16[128,2048]{1,0:T(8,128)(2,1)S(1)}, bf16[128,2048]{1,0:T(8,128)(2,1)S(1)}, u32[]{:S(2)}, u32[]{:S(2)}) collective-permute-start(bf16[128,2048]{1,0:T(8,128)(2,1)S(1)} %slice.500), channel_id=1, source_target_pairs={{0,8},{8,0},{1,9},{9,1},{2,10},{10,2},{3,11},{11,3},{4,12},{12,4},... | collective-permute-start | bytes 1572872 | tf_op jit(solution)/shard_map/ppermute | solution.py:361
  549.0 25.4 %collective-permute-start.100 = (bf16[1024,256]{1,0:T(8,128)(2,1)S(1)}, bf16[1024,256]{1,0:T(8,128)(2,1)S(1)}, u32[]{:S(2)}, u32[]{:S(2)}) collective-permute-start(bf16[1024,256]{1,0:T(8,128)(2,1)S(1)} %get-tuple-element.335), channel_id=1, source_target_pairs={{2,0},{3,1},{6,4},{7,5},{8,10},{9,11},{12,14},{13,15},{18,16},{19,... | collective-permute-start | bytes 1572872 | tf_op jit(solution)/shard_map/ppermute | solution.py:676
  556.4 30.1 %collective-permute-start.98 = (bf16[3,64,2048]{2,1,0:T(8,128)(2,1)S(1)}, bf16[3,64,2048]{2,1,0:T(8,128)(2,1)S(1)}, u32[]{:S(2)}, u32[]{:S(2)}) collective-permute-start(bf16[3,64,2048]{2,1,0:T(8,128)(2,1)S(1)} %dynamic-slice_convert_fusion), channel_id=1, source_target_pairs={{0,8},{8,0},{1,9},{9,1},{2,10},{10,2},{3,11},{11,3},{4,12},{12,4},... | collective-permute-start | bytes 2359304 | tf_op jit(solution)/shard_map/ppermute | solution.py:361
  557.6 27.5 %collective-permute-start.99 = (bf16[1024,256]{1,0:T(8,128)(2,1)S(1)}, bf16[1024,256]{1,0:T(8,128)(2,1)S(1)}, u32[]{:S(2)}, u32[]{:S(2)}) collective-permute-start(bf16[1024,256]{1,0:T(8,128)(2,1)S(1)} %get-tuple-element.336), channel_id=1, source_target_pairs={{2,10},{3,11},{6,14},{7,15},{8,0},{9,1},{12,4},{13,5},{18,26},{19,... | collective-permute-start | bytes 1572872 | tf_op jit(solution)/shard_map/ppermute | solution.py:676
  585.2 77.0 %collective-permute-start.94 = (bf16[256,2048]{1,0:T(8,128)(2,1)S(1)}, bf16[256,2048]{1,0:T(8,128)(2,1)S(1)}, u32[]{:S(2)}, u32[]{:S(2)}) collective-permute-start(bf16[256,2048]{1,0:T(8,128)(2,1)S(1)} %collective-permute-done.89), channel_id=1, source_target_pairs={{0,2},{1,3},{4,6},{5,7},{10,8},{11,9},{14,12},{15,13},{16,18},{17,... | collective-permute-start | bytes 3145736 | tf_op jit(solution)/shard_map/ppermute | solution.py:676
  586.5 76.2 %collective-permute-start.95 = (bf16[256,2048]{1,0:T(8,128)(2,1)S(1)}, bf16[256,2048]{1,0:T(8,128)(2,1)S(1)}, u32[]{:S(2)}, u32[]{:S(2)}) collective-permute-start(bf16[256,2048]{1,0:T(8,128)(2,1)S(1)} %collective-permute-done.90), channel_id=1, source_target_pairs={{0,8},{1,9},{4,12},{5,13},{10,2},{11,3},{14,6},{15,7},{16,24},{17,... | collective-permute-start | bytes 3145736 | tf_op jit(solution)/shard_map/ppermute | solution.py:676
  588.3 33.7 %collective-permute-start.117 = (bf16[1024,256]{1,0:T(8,128)(2,1)S(1)}, bf16[1024,256]{1,0:T(8,128)(2,1)S(1)}, u32[]{:S(2)}, u32[]{:S(2)}) collective-permute-start(bf16[1024,256]{1,0:T(8,128)(2,1)S(1)} %collective-permute-done.99), channel_id=1, source_target_pairs={{0,2},{1,3},{4,6},{5,7},{10,8},{11,9},{14,12},{15,13},{16,18},{17,... | collective-permute-start | bytes 1572872 | tf_op jit(solution)/shard_map/ppermute | solution.py:676
  590.0 49.4 %collective-permute-start.118 = (bf16[1024,256]{1,0:T(8,128)(2,1)S(1)}, bf16[1024,256]{1,0:T(8,128)(2,1)S(1)}, u32[]{:S(2)}, u32[]{:S(2)}) collective-permute-start(bf16[1024,256]{1,0:T(8,128)(2,1)S(1)} %collective-permute-done.100), channel_id=1, source_target_pairs={{0,8},{1,9},{4,12},{5,13},{10,2},{11,3},{14,6},{15,7},{16,24},{17,... | collective-permute-start | bytes 1572872 | tf_op jit(solution)/shard_map/ppermute | solution.py:676
  600.3 62.4 %collective-permute-start.101 = (bf16[3,64,2048]{2,1,0:T(8,128)(2,1)S(1)}, bf16[3,64,2048]{2,1,0:T(8,128)(2,1)S(1)}, u32[]{:S(2)}, u32[]{:S(2)}) collective-permute-start(bf16[3,64,2048]{2,1,0:T(8,128)(2,1)S(1)} %add_convert_fusion.6), channel_id=1, source_target_pairs={{0,0},{1,1},{2,2},{3,3},{4,16},{5,17},{6,18},{7,19},{8,8},{9,9},{1... | collective-permute-start | bytes 2359304 | tf_op jit(solution)/shard_map/ppermute | solution.py:887
  622.0 27.5 %collective-permute-start.91 = (bf16[128,2048]{1,0:T(8,128)(2,1)S(1)}, bf16[128,2048]{1,0:T(8,128)(2,1)S(1)}, u32[]{:S(2)}, u32[]{:S(2)}) collective-permute-start(bf16[128,2048]{1,0:T(8,128)(2,1)S(1)} %collective-permute-done.84), channel_id=1, source_target_pairs={{0,16},{16,0},{1,17},{17,1},{2,18},{18,2},{3,19},{19,3},{4,20},{20... | collective-permute-start | bytes 1572872 | tf_op jit(solution)/shard_map/ppermute | solution.py:361
  662.1 33.6 %collective-permute-start.109 = (bf16[256,2048]{1,0:T(8,128)(2,1)S(1)}, bf16[256,2048]{1,0:T(8,128)(2,1)S(1)}, u32[]{:S(2)}, u32[]{:S(2)}) collective-permute-start(bf16[256,2048]{1,0:T(8,128)(2,1)S(1)} %pad_maximum_fusion.17), channel_id=1, source_target_pairs={{0,1},{1,0},{2,3},{3,2},{4,5},{5,4},{6,7},{7,6},{8,9},{9,8},{10,11... | collective-permute-start | bytes 3145736 | tf_op jit(solution)/shard_map/ppermute | solution.py:361
  662.1 25.0 %collective-permute-start.111 = (bf16[256,2048]{1,0:T(8,128)(2,1)S(1)}, bf16[256,2048]{1,0:T(8,128)(2,1)}, u32[]{:S(2)}, u32[]{:S(2)}) collective-permute-start(bf16[256,2048]{1,0:T(8,128)(2,1)S(1)} %pad_maximum_fusion.18), channel_id=1, source_target_pairs={{0,1},{1,0},{2,3},{3,2},{4,5},{5,4},{6,7},{7,6},{8,9},{9,8},{10,11... | collective-permute-start | bytes 3145736 | tf_op jit(solution)/shard_map/ppermute | solution.py:361
  662.7 29.0 %collective-permute-start.114 = (bf16[256,2048]{1,0:T(8,128)(2,1)S(1)}, bf16[256,2048]{1,0:T(8,128)(2,1)S(1)}, u32[]{:S(2)}, u32[]{:S(2)}) collective-permute-start(bf16[256,2048]{1,0:T(8,128)(2,1)S(1)} %pad_maximum_fusion.20), channel_id=1, source_target_pairs={{0,1},{1,0},{2,3},{3,2},{4,5},{5,4},{6,7},{7,6},{8,9},{9,8},{10,11... | collective-permute-start | bytes 3145736 | tf_op jit(solution)/shard_map/ppermute | solution.py:361
  662.9 31.1 %collective-permute-start.112 = (bf16[256,2048]{1,0:T(8,128)(2,1)S(1)}, bf16[256,2048]{1,0:T(8,128)(2,1)}, u32[]{:S(2)}, u32[]{:S(2)}) collective-permute-start(bf16[256,2048]{1,0:T(8,128)(2,1)S(1)} %pad_maximum_fusion.19), channel_id=1, source_target_pairs={{0,1},{1,0},{2,3},{3,2},{4,5},{5,4},{6,7},{7,6},{8,9},{9,8},{10,11... | collective-permute-start | bytes 3145736 | tf_op jit(solution)/shard_map/ppermute | solution.py:361
  (172 other events, 1968.5 us)
